TPU v7x, 32 devices: a whole 2x2x4 slice. The times are simulated.
32 devices in a mesh: shard: 2 (over y), blk: 4 (over z), ckpt: 2 (over x), qry: 2 (over core).
Axes of the slice: x: 2, y: 2, z: 4, core: 2. Of those that a mesh axis runs over, the one named last changes fastest.
Arguments:
- query_feats: bfloat16 [2, 8192, 2048], P('ckpt', ('shard', 'blk', 'qry')), parts along dimension 1, may hold values from -6 to 6
- train_feats: bfloat16 [2, 1024, 2048], P('ckpt', ('shard', 'blk')), parts along dimension 1, may hold values from -0.125 to 0.125
- loss_weights: bfloat16 [2, 1024], P('ckpt', ('shard', 'blk')), parts along dimension 1, may hold values from 0.099609375 to 1
- pair_list: int32 [32, 2], P(('shard', 'blk', 'qry')), parts along dimension 0, may hold values from 0 to 3, all different within a row
- tile_owner: int32 [8], P('shard'), parts along dimension 0, may hold values from 0 to 3, each once
Outputs:
- scores: float32 [8192, 512], P(('shard', 'blk', 'qry'), 'ckpt'), parts along dimension 0
There are 2 independent parts, one for each index of `shard`. A program takes and returns all parts, laid end to end along the dimension named above; each array names one. Nothing has to cross between parts.
Inputs may be any that keep to these rules, and one draw needn't show every extreme that they name: `pair_list`: each row names 2 different training blocks; every training block is named by some row. `tile_owner`: a permutation of the training blocks.
All inputs are finite; a program needn't handle non-finite values.
Results may differ from a plain program's by a relative error of at most 0.0003.
Values may be sent and summed in bfloat16 or wider, within the bound.
No kernel may reach another device: no remote copies, remote signals or barrier semaphores. Data moves between devices by JAX's collectives and lax.ppermute only.
A program may use at most 128 MiB of HBM per device.

v0:
```python
import jax
import jax.numpy as jnp
from jax import lax
from jax.sharding import PartitionSpec as P

QBLK = 256
TBLK = 128


def per_device(query_feats, train_feats, loss_weights, pair_list, tile_owner):
    queries = query_feats[0]
    block_count = lax.axis_size("blk")
    total_rows = TBLK * block_count
    block_ids = jnp.arange(block_count, dtype=jnp.int32)
    wanted = jnp.any(pair_list[:, :, None] == block_ids[None, None, :], axis=1).astype(jnp.float32)
    own_rows = train_feats[0]
    own_weights = loss_weights[0]
    gathered_rows, gathered_weights = (
        lax.all_gather(own_rows, "blk", axis=0, tiled=True),
        lax.all_gather(own_weights, "blk", axis=0, tiled=True),
    )
    row_blocks = gathered_rows.reshape(block_count, TBLK, gathered_rows.shape[1])
    weight_blocks = gathered_weights.reshape(block_count, TBLK)
    query_mask = jnp.transpose(jnp.repeat(wanted, QBLK, axis=0))
    owner_rows = total_rows // lax.axis_size("ckpt")
    picked = row_blocks[tile_owner].reshape(lax.axis_size("ckpt") * owner_rows, row_blocks.shape[2])
    picked_weights = (
        weight_blocks[tile_owner].reshape(lax.axis_size("ckpt") * owner_rows).astype(jnp.float32)
    )
    products = lax.dot_general(
        picked, queries, (((1,), (1,)), ((), ())), preferred_element_type=jnp.float32
    )
    mask_rows = jnp.repeat(query_mask[tile_owner], TBLK, axis=0)
    summed_rows = lax.psum_scatter(
        products * picked_weights[:, None] * mask_rows, "ckpt", scatter_dimension=0, tiled=True
    )
    return jnp.transpose(summed_rows)


def solution(mesh):
    return jax.shard_map(
        per_device,
        mesh=mesh,
        in_specs=(
            P("ckpt", ("shard", "blk", "qry"), None),
            P("ckpt", ("shard", "blk"), None),
            P("ckpt", ("shard", "blk")),
            P(("shard", "blk", "qry"), None),
            P("shard"),
        ),
        out_specs=P(("shard", "blk", "qry"), "ckpt"),
        check_vma=False,
    )
```

profile of v0, /device:TPU:0, one launch (start us, length us, event | category | flops | bytes accessed | tf_op | source)
XLA Modules:
  0.0 93.2 jit_solution(14550216381288683997)
XLA Ops:
  6.5 0.0 copy-start
  6.5 0.0 all-gather.4.cloned.1.call-start
  6.5 0.7 all-gather.4.cloned.1.call-update
  7.3 0.0 reduce-scatter.2.cloned.1.call-start
  7.3 0.8 compare_reduce_fusion
  8.1 0.1 copy.7
  8.2 0.1 broadcast_bitcast_fusion
  8.3 0.7 compare_select_fusion
  8.9 0.6 gather_fusion.2
  9.5 12.8 %all-gather.1 = bf16[1,512]{1,0:T(2,128)(2,1)S(1)} all-gather(bf16[1,128]{1,0:T(2,128)(2,1)} %param.7), channel_id=3, replica_groups=mesh['shard'=2,'blk'=4,'ckpt'=2,'qry'=2] {'blk'}, dimensions={1}, use_global_device_ids=true | all-gather | bytes 1280 | tf_op jit(solution)/shard_map/all_gather | solution.py:20
  22.3 0.6 gather_fusion.1
  22.9 34.4 %all-gather.4.cloned.1.call-done = bf16[1,512,2048]{2,1,0:T(8,128)(2,1)} async-done(((bf16[1,128,2048]{2,1,0:T(8,128)(2,1)}), bf16[1,512,2048]{2,1,0:T(8,128)(2,1)}) %all-gather.4.cloned.1.call-update) | async-done | bytes 2097168 | tf_op jit(solution)/shard_map/all_gather | solution.py:19
  57.3 3.6 %gather_fusion = bf16[4,128,2048]{2,1,0:T(8,128)(2,1)} fusion(bf16[4,128,2048]{2,1,0:T(8,128)(2,1)} %bitcast.23, s32[1024]{0:T(1024)S(1)} %pad_clamp_fusion), kind=kCustom, calls=%fused_computation | custom fusion | bytes 4194320 | tf_op jit(solution)/shard_map/gather | solution.py:26
  60.9 0.1 broadcast_in_dim.16
  61.1 0.0 copy-done
  61.1 3.9 %fusion.5 = f32[512,512]{1,0:T(8,128)} fusion(f32[512,512]{1,0:T(8,128)S(1)} %bitcast.25, bf16[512,2048]{1,0:T(8,128)(2,1)} %bitcast.24, bf16[1,512,2048]{2,1,0:T(8,128)(2,1)S(1)} %copy-done, f32[512]{0:T(512)S(1)} %bitcast_convert_fusion), kind=kOutput, calls=%fused_computation.6 | convolution fusion | flops 1074266112 | bytes 6293504 | tf_op jit(solution)/shard_map/dot_general | solution.py:30
  64.9 0.0 reduce-scatter.2.cloned.1.call-update
  65.0 19.3 %reduce-scatter.2.cloned.1.call-done = f32[256,512]{1,0:T(8,128)} async-done(((f32[512,512]{1,0:T(8,128)}), f32[256,512]{1,0:T(8,128)}) %reduce-scatter.2.cloned.1.call-update) | async-done | bytes 524304 | tf_op jit(solution)/shard_map/reduce_scatter | solution.py:34
  84.3 2.0 %copy.8 = f32[512,256]{1,0:T(8,128)} copy(f32[512,256]{0,1:T(8,128)} %bitcast.27) | data formatting | bytes 1048576 | tf_op jit(solution)/shard_map/transpose | solution.py:37
  (5 shorter events, 0.0 us)
Async XLA Ops:
  6.5 54.5 %copy-start = (bf16[1,512,2048]{2,1,0:T(8,128)(2,1)S(1)}, bf16[1,512,2048]{2,1,0:T(8,128)(2,1)}, u32[]{:S(2)}) copy-start(bf16[1,512,2048]{2,1,0:T(8,128)(2,1)} %param.5) | copy-start | bytes 6291460
  6.5 50.8 %all-gather.4.cloned.1.call-start = ((), (), s32[]{:S(2)}) async-start(), calls=%async_computation.2 | async-start | bytes 2621440 | tf_op jit(solution)/shard_map/all_gather | solution.py:19
  7.3 77.0 %reduce-scatter.2.cloned.1.call-start = ((), (), s32[]{:S(2)}) async-start(), calls=%async_computation.1 | async-start | bytes 1572864 | tf_op jit(solution)/shard_map/reduce_scatter | solution.py:34
Sparse Core Ops, SparseCore 0:
  8.9 48.3 all-gather.3
  65.1 19.1 reduce-scatter.1
where the time goes:
time: 93.4 us; the launch traced here: 93.2 us
  waiting for transfers between devices  54.5 us (58%)
  between operations  13.4 us (14%)
  blocking collectives  12.8 us (14%)
  local copies, waits for them, and re-layouts  7.07 us (8%)
  matrix products  3.86 us (4%)
  other arithmetic  1.47 us (2%)
    all_gather x1, waiting for transfers between devices, per_device(): lax.all_gather(own_rows, 'blk', axis=0, tiled=True)  34.4 us
    reduce_scatter x1, waiting for transfers between devices, per_device(): lax.psum_scatter(products * picked_weights[:, None] * mask_rows, 'ckpt',...  19.3 us
    all_gather x1, blocking collectives, per_device(): lax.all_gather(own_weights, 'blk', axis=0, tiled=True)  12.8 us
    dot_general x1, matrix products, per_device(): lax.dot_general(picked, queries, (((1,), (1,)), ((), ())), preferred_elem...  3.86 us
    gather x1, local copies, waits for them, and re-layouts, per_device(): row_blocks[tile_owner]  3.62 us
    transpose x1, local copies, waits for them, and re-layouts, per_device(): return jnp.transpose(summed_rows)  2.04 us
  transfers between devices with their start and end apart: 2, of which 2 were waited for; matrix products, arithmetic and copies ran while one was open for 3% of the time, Pallas kernels for 0%

commit v1 on v0

v1 whole, which is shorter than its diff:
```python
import functools

import jax
import jax.numpy as jnp
from jax import lax
from jax.experimental import pallas as pl
from jax.experimental.pallas import tpu as pltpu
from jax.sharding import PartitionSpec as P

CHUNKS = 2


def fold_ring(n):
    order = [2 * z for z in range(n)] + [2 * z + 1 for z in reversed(range(n))]
    return [(order[i], order[(i + 1) % len(order)]) for i in range(len(order))]


def shift(n, by):
    return [(i, (i + by) % n) for i in range(n)]


def xor(n, bit):
    return [(i, i ^ bit) for i in range(n)]


def whole(shape, dtype):
    return jax.ShapeDtypeStruct(shape, dtype)


VMEM = pl.BlockSpec(memory_space=pltpu.VMEM)
SMEM = pl.BlockSpec(memory_space=pltpu.SMEM)


def place_of(block, z, owner_ref, n, per):
    position = jnp.int32(0)
    for j in range(n):
        position = jnp.where(owner_ref[j] == block, j, position)
    owner = position // per
    slot = position % per
    mine = jnp.abs(block - z)
    rank = jnp.int32(0)
    for k in range(per):
        other = owner_ref[owner * per + k]
        far = jnp.abs(other - z)
        nearer = (far < mine) | ((far == mine) & (other < block))
        rank = rank + nearer.astype(jnp.int32)
    return owner, slot, rank


def score_into(put, sizes, block, rows, q_ref, w_ref, pair_ref, owner_ref):
    n, ckpts, per, nb, cand = sizes
    z = lax.axis_index("blk")
    c = lax.axis_index("ckpt")
    qblk = q_ref.shape[0] // nb

    @pl.when((block >= 0) & (block < n))
    def _():
        owner, slot, rank = place_of(block, z, owner_ref, n, per)
        away = lax.rem(owner - c + ckpts, ckpts)
        index = away * per + jnp.where(away == 0, slot, rank)
        weight = w_ref[pl.ds(block ^ z, 1), :]
        for b in range(nb):
            wanted = pair_ref[b, 0] == block
            for k in range(1, cand):
                wanted = wanted | (pair_ref[b, k] == block)

            @pl.when(wanted)
            def _():
                span = pl.ds(b * qblk, qblk)
                tile = lax.dot_general(
                    q_ref[span, :], rows(), (((1,), (1,)), ((), ())), preferred_element_type=jnp.float32
                )
                put(index, span, tile * weight)


def stacked(refs):
    if len(refs) == 1:
        return refs[0][...]
    return jnp.concatenate([ref[...] for ref in refs], axis=0)


def sources(dists, chunks, refs):
    z = lax.axis_index("blk")
    core = lax.axis_index("qry")
    at = 0
    for d in dists:
        if d == 0:
            yield z, refs[at : at + 1]
            at += 1
        else:
            yield z + jnp.where(core == 0, -d, d), refs[at : at + chunks]
            yield z + jnp.where(core == 0, d, -d), refs[at + chunks : at + 2 * chunks]
            at += 2 * chunks


def first_kernel(sizes, dists, chunks, pair_ref, owner_ref, w_ref, q_ref, *refs):
    n, ckpts, per, nb, cand = sizes
    count = 1 + 2 * chunks * (len(dists) - 1)
    ins, outs, terms = refs[:count], refs[count:-1], refs[-1]
    terms[...] = jnp.zeros_like(terms)

    def put(index, span, tile):
        terms[index, span, :] = tile

    for block, rows in sources(dists, chunks, ins):
        score_into(put, sizes, block, functools.partial(stacked, rows), q_ref, w_ref, pair_ref, owner_ref)
    width = terms.shape[2]
    for j in range(per):
        outs[0][:, j * width : (j + 1) * width] = terms[j]
    for i in range(per, ckpts * per):
        outs[1 + i - per][...] = terms[i]


def later_kernel(sizes, dist, chunks, pair_ref, owner_ref, w_ref, q_ref, *refs):
    n, ckpts, per, nb, cand = sizes
    rows_in = 2 * chunks
    outs = refs[rows_in + (len(refs) - rows_in) // 2 :]
    width = outs[1].shape[1]

    def put(index, span, tile):
        for i in range(ckpts * per):

            @pl.when(index == i)
            def _():
                if i < per:
                    outs[0][span, i * width : (i + 1) * width] = tile
                else:
                    outs[1 + i - per][span, :] = tile

    for i in range((len(refs) - rows_in) // 2):
        outs[i][...] = refs[rows_in + i][...]
    for block, rows in sources((dist,), chunks, refs[:rows_in]):
        score_into(put, sizes, block, functools.partial(stacked, rows), q_ref, w_ref, pair_ref, owner_ref)


def final_kernel(sizes, owner_ref, acc_ref, *refs):
    n, ckpts, per, nb, cand = sizes
    ins, out = refs[:-1], refs[-1]
    z = lax.axis_index("blk")
    c = lax.axis_index("ckpt")
    width = ins[0].shape[1]
    for j in range(per):
        owner, slot, rank = place_of(owner_ref[c * per + j], z, owner_ref, n, per)
        cols = slice(j * width, (j + 1) * width)
        for s in range(per):

            @pl.when(rank == s)
            def _():
                total = acc_ref[:, cols]
                for r in range(ckpts - 1):
                    total = total + ins[r * per + s][...]
                out[:, cols] = total


def per_device(query_feats, train_feats, loss_weights, pair_list, tile_owner):
    queries, own_rows, own_weights = query_feats[0], train_feats[0], loss_weights
    n, ckpts = lax.axis_size("blk"), lax.axis_size("ckpt")
    nb, cand = pair_list.shape
    per = n // ckpts
    rows = own_rows.shape[0]
    sizes = (n, ckpts, per, nb, cand)
    lines = ("blk", "qry")
    ring = fold_ring(n)
    swap = shift(2, 1)
    chunks = CHUNKS
    piece = rows // chunks

    held = [own_rows[i * piece : (i + 1) * piece] for i in range(chunks)]
    direct, crossed = [], []
    weights = own_weights.astype(jnp.float32)
    bit = 1
    for step in range(1, n):
        held = [lax.ppermute(part, lines, ring) for part in held]
        direct.append(held)
        crossed.append([lax.ppermute(part, "qry", swap) for part in held])
    while bit < n:
        weights = jnp.concatenate([weights, lax.ppermute(weights, "blk", xor(n, bit))], axis=0)
        bit *= 2

    queries_count = queries.shape[0]
    term = whole((queries_count, rows), jnp.float32)
    acc = whole((queries_count, per * rows), jnp.float32)
    ready = n - per
    near = [own_rows]
    for d in range(1, ready + 1):
        near += direct[d - 1] + crossed[d - 1]
    results = pl.pallas_call(
        functools.partial(first_kernel, sizes, tuple(range(ready + 1)), chunks),
        out_shape=[acc] + [term] * ((ckpts - 1) * per),
        in_specs=[SMEM, SMEM, VMEM, VMEM] + [VMEM] * len(near),
        out_specs=[VMEM] * (1 + (ckpts - 1) * per),
        scratch_shapes=[pltpu.VMEM((ckpts * per, queries_count, rows), jnp.float32)],
        name="near_scores",
    )(pair_list, tile_owner, weights, queries, *near)
    arrived = [None] * ((ckpts - 1) * per)
    for s in range(per):
        if s > 0:
            dist = ready + s
            news = direct[dist - 1] + crossed[dist - 1]
            results = pl.pallas_call(
                functools.partial(later_kernel, sizes, dist, chunks),
                out_shape=[acc] + [term] * ((ckpts - 1) * per),
                in_specs=[SMEM, SMEM, VMEM, VMEM] + [VMEM] * (len(news) + len(results)),
                out_specs=[VMEM] * len(results),
                name="far_scores",
            )(pair_list, tile_owner, weights, queries, *news, *results)
        for r in range(1, ckpts):
            at = (r - 1) * per + s
            arrived[at] = lax.ppermute(results[1 + at], "ckpt", shift(ckpts, r))
    return pl.pallas_call(
        functools.partial(final_kernel, sizes),
        out_shape=acc,
        in_specs=[SMEM, VMEM] + [VMEM] * len(arrived),
        out_specs=VMEM,
        name="sum_scores",
    )(tile_owner, results[0], *arrived)


def solution(mesh):
    return jax.shard_map(
        per_device,
        mesh=mesh,
        in_specs=(
            P("ckpt", ("shard", "blk", "qry"), None),
            P("ckpt", ("shard", "blk"), None),
            P("ckpt", ("shard", "blk")),
            P(("shard", "blk", "qry"), None),
            P("shard"),
        ),
        out_specs=P(("shard", "blk", "qry"), "ckpt"),
        check_vma=False,
    )
```

time: 93.4 us -> 53.2 us (0.57)
  waiting for transfers between devices: 54.5 us -> 15.9 us
  starting transfers between devices: 0.04 us -> 21.9 us
  between operations: 13.4 us -> 0.08 us
  blocking collectives: 12.8 us -> 0 us
  Pallas kernels: 0 us -> 10.6 us
  matrix products: 3.86 us -> 0 us
  local copies, waits for them, and re-layouts: 7.07 us -> 3.3 us
    all_gather x1 -> x0, waiting for transfers between devices: 34.4 us -> none  [per_device(): lax.all_gather(own_rows, 'blk', axis=0, tiled=True)]
    ppermute x0 -> x16, starting transfers between devices: none -> 21.9 us  [the longest x6 14.6 us: per_device(): held = [lax.ppermute(part, lines, ring) for part in held]]
    reduce_scatter x1 -> x0, waiting for transfers between devices: 19.3 us -> none  [per_device(): lax.psum_scatter(products * picked_weights[:, None] * mask_rows, 'ckpt',...]
    ppermute x0 -> x16, waiting for transfers between devices: none -> 15.9 us  [the longest x2 7.72 us: per_device(): arrived[at] = lax.ppermute(results[1 + at], 'ckpt', shift(ckpts, r))]
    all_gather x1 -> x0, blocking collectives: 12.8 us -> none  [per_device(): lax.all_gather(own_weights, 'blk', axis=0, tiled=True)]
    pallas_call x0 -> x3, Pallas kernels: none -> 10.6 us  [the longest x1 4.37 us: per_device(): pl.pallas_call(functools.partial(first_kernel, sizes, tuple(range(ready +...]
    gather x3 -> x0, local copies, waits for them, and re-layouts: 4.74 us -> none  [the longest x1 3.62 us: per_device(): row_blocks[tile_owner]]
    dot_general x1 -> x0, matrix products: 3.86 us -> none  [per_device(): lax.dot_general(picked, queries, (((1,), (1,)), ((), ())), preferred_elem...]
  transfers between devices with their start and end apart: 2 -> 16, of which waited for: 2 -> 9; matrix products, arithmetic and copies ran while one was open for 3% -> 2% of each run, Pallas kernels for 0% -> 16%
where the time goes in v1:
time: 53.2 us; the launch traced here: 53 us
  starting transfers between devices  21.9 us (41%)
  waiting for transfers between devices  15.9 us (30%)
  Pallas kernels  10.6 us (20%)
  local copies, waits for them, and re-layouts  3.3 us (6%)
  other arithmetic  1.26 us (2%)
    ppermute x6, starting transfers between devices, per_device(): held = [lax.ppermute(part, lines, ring) for part in held]  14.6 us
    ppermute x2, waiting for transfers between devices, per_device(): arrived[at] = lax.ppermute(results[1 + at], 'ckpt', shift(ckpts, r))  7.72 us
    pallas_call x1, Pallas kernels, per_device(): pl.pallas_call(functools.partial(first_kernel, sizes, tuple(range(ready +...  4.37 us
    ppermute x2, starting transfers between devices, per_device(): lax.ppermute(weights, 'blk', xor(n, bit))  4.17 us
    pallas_call x1, Pallas kernels, per_device(): pl.pallas_call(functools.partial(later_kernel, sizes, dist, chunks), out_...  4.13 us
    ppermute x6, waiting for transfers between devices, per_device(): held = [lax.ppermute(part, lines, ring) for part in held]  4.05 us
    ppermute x2, waiting for transfers between devices, per_device(): lax.ppermute(weights, 'blk', xor(n, bit))  3.87 us
    unnamed x28, local copies, waits for them, and re-layouts  2.23 us
  transfers between devices with their start and end apart: 16, of which 9 were waited for; matrix products, arithmetic and copies ran while one was open for 2% of the time, Pallas kernels for 16%

profile of v1, /device:TPU:0, one launch (start us, length us, event | category | flops | bytes accessed | tf_op | source)
XLA Modules:
  0.0 53.0 jit_solution(16474290846049979301)
XLA Ops:
  0.0 1.1 %slice_bitcast_fusion = (bf16[64,2048]{1,0:T(8,128)(2,1)S(1)}, bf16[64,2048]{1,0:T(8,128)(2,1)S(1)}) fusion(bf16[1,128,2048]{2,1,0:T(8,128)(2,1)} %param.6), kind=kLoop, calls=%fused_computation | loop fusion | bytes 1048576 | tf_op jit(solution)/shard_map/slice | solution.py:168
  1.1 3.1 %collective-permute-start.2 = (bf16[64,2048]{1,0:T(8,128)(2,1)S(1)}, bf16[64,2048]{1,0:T(8,128)(2,1)S(1)}, u32[]{:S(2)}, u32[]{:S(2)}) collective-permute-start(bf16[64,2048]{1,0:T(8,128)(2,1)S(1)} %get-tuple-element.16), channel_id=1, source_target_pairs={{0,4},{4,8},{8,12},{12,13},{13,9},{9,5},{5,1},{1,0},{2,6},{6,10},{... | collective-permute-start | bytes 786440 | tf_op jit(solution)/shard_map/ppermute | solution.py:173
  4.1 1.6 %collective-permute-start.5 = (bf16[64,2048]{1,0:T(8,128)(2,1)S(1)}, bf16[64,2048]{1,0:T(8,128)(2,1)S(1)}, u32[]{:S(2)}, u32[]{:S(2)}) collective-permute-start(bf16[64,2048]{1,0:T(8,128)(2,1)S(1)} %get-tuple-element.15), channel_id=1, source_target_pairs={{0,4},{4,8},{8,12},{12,13},{13,9},{9,5},{5,1},{1,0},{2,6},{6,10},{... | collective-permute-start | bytes 786440 | tf_op jit(solution)/shard_map/ppermute | solution.py:173
  5.7 2.3 %collective-permute-done.2.refs_1_ = bf16[64,2048]{1,0:T(8,128)(2,1)S(1)} collective-permute-done((bf16[64,2048]{1,0:T(8,128)(2,1)S(1)}, bf16[64,2048]{1,0:T(8,128)(2,1)S(1)}, u32[]{:S(2)}, u32[]{:S(2)}) %collective-permute-start.2) | collective-permute-done | bytes 262176 | tf_op jit(solution)/shard_map/ppermute | solution.py:173
  8.0 2.5 %collective-permute-start.3 = (bf16[64,2048]{1,0:T(8,128)(2,1)S(1)}, bf16[64,2048]{1,0:T(8,128)(2,1)S(1)}, u32[]{:S(2)}, u32[]{:S(2)}) collective-permute-start(bf16[64,2048]{1,0:T(8,128)(2,1)S(1)} %collective-permute-done.2.refs_1_), channel_id=1, source_target_pairs={{0,4},{4,8},{8,12},{12,13},{13,9},{9,5},{5,1},{1,0},{2,6},{6,10},{... | collective-permute-start | bytes 786440 | tf_op jit(solution)/shard_map/ppermute | solution.py:173
  10.8 2.5 %collective-permute-start.6 = (bf16[64,2048]{1,0:T(8,128)(2,1)S(1)}, bf16[64,2048]{1,0:T(8,128)(2,1)S(1)}, u32[]{:S(2)}, u32[]{:S(2)}) collective-permute-start(bf16[64,2048]{1,0:T(8,128)(2,1)S(1)} %collective-permute-done.5.refs_2_), channel_id=1, source_target_pairs={{0,4},{4,8},{8,12},{12,13},{13,9},{9,5},{5,1},{1,0},{2,6},{6,10},{... | collective-permute-start | bytes 786440 | tf_op jit(solution)/shard_map/ppermute | solution.py:173
  13.3 1.1 %collective-permute-done.3.refs_5_ = bf16[64,2048]{1,0:T(8,128)(2,1)S(1)} collective-permute-done((bf16[64,2048]{1,0:T(8,128)(2,1)S(1)}, bf16[64,2048]{1,0:T(8,128)(2,1)S(1)}, u32[]{:S(2)}, u32[]{:S(2)}) %collective-permute-start.3) | collective-permute-done | bytes 262176 | tf_op jit(solution)/shard_map/ppermute | solution.py:173
  14.4 2.5 %collective-permute-start.4 = (bf16[64,2048]{1,0:T(8,128)(2,1)S(1)}, bf16[64,2048]{1,0:T(8,128)(2,1)S(1)}, u32[]{:S(2)}, u32[]{:S(2)}) collective-permute-start(bf16[64,2048]{1,0:T(8,128)(2,1)S(1)} %collective-permute-done.3.refs_5_), channel_id=1, source_target_pairs={{0,4},{4,8},{8,12},{12,13},{13,9},{9,5},{5,1},{1,0},{2,6},{6,10},{... | collective-permute-start | bytes 786440 | tf_op jit(solution)/shard_map/ppermute | solution.py:173
  17.2 2.5 %collective-permute-start.7 = (bf16[64,2048]{1,0:T(8,128)(2,1)S(1)}, bf16[64,2048]{1,0:T(8,128)(2,1)S(1)}, u32[]{:S(2)}, u32[]{:S(2)}) collective-permute-start(bf16[64,2048]{1,0:T(8,128)(2,1)S(1)} %collective-permute-done.6.refs_6_), channel_id=1, source_target_pairs={{0,4},{4,8},{8,12},{12,13},{13,9},{9,5},{5,1},{1,0},{2,6},{6,10},{... | collective-permute-start | bytes 786440 | tf_op jit(solution)/shard_map/ppermute | solution.py:173
  19.7 0.7 %convert_element_type.3 = f32[1,128]{1,0:T(1,128)S(1)} convert(bf16[1,128]{1,0:T(2,128)(2,1)} %param.7) | non-fusion elementwise | flops 128 | bytes 768 | tf_op jit(solution)/shard_map/convert_element_type | solution.py:170
  20.4 1.6 %collective-permute-start = (f32[1,128]{1,0:T(1,128)S(1)}, f32[1,128]{1,0:T(1,128)S(1)}, u32[]{:S(2)}, u32[]{:S(2)}) collective-permute-start(f32[1,128]{1,0:T(1,128)S(1)} %convert_element_type.3), channel_id=1, source_target_pairs={{0,4},{4,0},{8,12},{12,8},{1,5},{5,1},{9,13},{13,9},{2,6},{6,2},{1... | collective-permute-start | bytes 1544 | tf_op jit(solution)/shard_map/ppermute | solution.py:177
  21.9 2.0 %collective-permute-done = f32[1,128]{1,0:T(1,128)S(1)} collective-permute-done((f32[1,128]{1,0:T(1,128)S(1)}, f32[1,128]{1,0:T(1,128)S(1)}, u32[]{:S(2)}, u32[]{:S(2)}) %collective-permute-start) | collective-permute-done | bytes 544 | tf_op jit(solution)/shard_map/ppermute | solution.py:177
  23.9 2.6 %collective-permute-start.1 = (f32[2,128]{1,0:T(2,128)S(1)}, f32[2,128]{1,0:T(2,128)S(1)}, u32[]{:S(2)}, u32[]{:S(2)}) collective-permute-start(f32[2,128]{1,0:T(2,128)S(1)} %pad_maximum_fusion.1), channel_id=1, source_target_pairs={{0,8},{4,12},{8,0},{12,4},{1,9},{5,13},{9,1},{13,5},{2,10},{6,14},... | collective-permute-start | bytes 3080 | tf_op jit(solution)/shard_map/ppermute | solution.py:177
  26.5 1.9 %collective-permute-done.1 = f32[2,128]{1,0:T(2,128)S(1)} collective-permute-done((f32[2,128]{1,0:T(2,128)S(1)}, f32[2,128]{1,0:T(2,128)S(1)}, u32[]{:S(2)}, u32[]{:S(2)}) %collective-permute-start.1) | collective-permute-done | bytes 1056 | tf_op jit(solution)/shard_map/ppermute | solution.py:177
  29.4 0.6 %pad_maximum_fusion.w_ref = f32[4,128]{1,0:T(4,128)} fusion(f32[2,128]{1,0:T(2,128)S(1)} %collective-permute-done.1, f32[1,128]{1,0:T(1,128)S(1)} %collective-permute-done, f32[1,128]{1,0:T(1,128)S(1)} %convert_element_type.3), kind=kLoop, calls=%fused_computation.2 | loop fusion | flops 1024 | bytes 4096 | tf_op jit(solution)/shard_map/concatenate | solution.py:177
  31.0 4.4 %near_scores.1 = (f32[512,256]{1,0:T(8,128)}, f32[512,128]{1,0:T(8,128)}, f32[512,128]{1,0:T(8,128)}) custom-call(s32[2,2]{1,0:T(2,128)} %pair_ref.3, s32[4]{0:T(128)} %owner_ref.5, f32[4,128]{1,0:T(4,128)} %pad_maximum_fusion.w_ref, bf16[512,2048]{1,0:T(8,128)(2,1)} %bitcast.6, bf16[128,2048]{1,0:T(8,128)(2,1)} %bitcast.8, bf16[64,2048]{1,0:T(8,128)(2,1)} %copy-done, ...), custom_call_target="tpu_custom_call" | custom-call | tf_op jit(solution)/shard_map/near_scores/pallas_call | solution.py:187
  35.4 1.6 %collective-permute-start.14 = (f32[512,128]{1,0:T(8,128)}, f32[512,128]{1,0:T(8,128)S(1)}, u32[]{:S(2)}, u32[]{:S(2)}) collective-permute-start(f32[512,128]{1,0:T(8,128)} %get-tuple-element.11.refs_5_), channel_id=1, source_target_pairs={{0,2},{2,0},{1,3},{3,1},{4,6},{6,4},{5,7},{7,5},{8,10},{10,8},{9,1... | collective-permute-start | bytes 786440 | tf_op jit(solution)/shard_map/ppermute | solution.py:209
  37.0 0.7 %copy-done.8 = bf16[64,2048]{1,0:T(8,128)(2,1)} copy-done((bf16[64,2048]{1,0:T(8,128)(2,1)}, bf16[64,2048]{1,0:T(8,128)(2,1)S(1)}, u32[]{:S(2)}) %copy-start.8) | copy-done | bytes 262168
  37.8 4.1 %far_scores.1 = (f32[512,256]{1,0:T(8,128)}, f32[512,128]{1,0:T(8,128)}, f32[512,128]{1,0:T(8,128)}) custom-call(s32[2,2]{1,0:T(2,128)} %pair_ref.3, s32[4]{0:T(128)} %owner_ref.5, f32[4,128]{1,0:T(4,128)} %pad_maximum_fusion.w_ref, bf16[512,2048]{1,0:T(8,128)(2,1)} %bitcast.7, bf16[64,2048]{1,0:T(8,128)(2,1)} %copy-done.2, bf16[64,2048]{1,0:T(8,128)(2,1)} %copy-done.4, ...), custom_call_target="tpu_custom_call" | custom-call | tf_op jit(solution)/shard_map/far_scores/pallas_call | solution.py:200
  41.9 0.5 %collective-permute-start.15 = (f32[512,128]{1,0:T(8,128)}, f32[512,128]{1,0:T(8,128)S(1)}, u32[]{:S(2)}, u32[]{:S(2)}) collective-permute-start(f32[512,128]{1,0:T(8,128)} %get-tuple-element.14), channel_id=1, source_target_pairs={{0,2},{2,0},{1,3},{3,1},{4,6},{6,4},{5,7},{7,5},{8,10},{10,8},{9,1... | collective-permute-start | bytes 786440 | tf_op jit(solution)/shard_map/ppermute | solution.py:209
  42.5 2.0 %collective-permute-done.14.refs_0_ = f32[512,128]{1,0:T(8,128)S(1)} collective-permute-done((f32[512,128]{1,0:T(8,128)}, f32[512,128]{1,0:T(8,128)S(1)}, u32[]{:S(2)}, u32[]{:S(2)}) %collective-permute-start.14) | collective-permute-done | bytes 262176 | tf_op jit(solution)/shard_map/ppermute | solution.py:209
  44.4 5.7 %collective-permute-done.15.refs_1_ = f32[512,128]{1,0:T(8,128)S(1)} collective-permute-done((f32[512,128]{1,0:T(8,128)}, f32[512,128]{1,0:T(8,128)S(1)}, u32[]{:S(2)}, u32[]{:S(2)}) %collective-permute-start.15) | collective-permute-done | bytes 262176 | tf_op jit(solution)/shard_map/ppermute | solution.py:209
  50.2 0.7 %copy-done.13 = f32[512,128]{1,0:T(8,128)} copy-done((f32[512,128]{1,0:T(8,128)}, f32[512,128]{1,0:T(8,128)S(1)}, u32[]{:S(2)}) %copy-start.13) | copy-done | bytes 262168
  50.9 2.1 %sum_scores.1 = f32[512,256]{1,0:T(8,128)} custom-call(s32[4]{0:T(128)} %owner_ref.5, f32[512,256]{1,0:T(8,128)} %get-tuple-element.13.acc_ref, f32[512,128]{1,0:T(8,128)} %copy-done.12, f32[512,128]{1,0:T(8,128)} %copy-done.13), custom_call_target="tpu_custom_call" | custom-call | tf_op jit(solution)/shard_map/sum_scores/pallas_call | solution.py:210
  (43 shorter events, 2.8 us)
Async XLA Ops:
  1.1 7.0 %collective-permute-start.2 = (bf16[64,2048]{1,0:T(8,128)(2,1)S(1)}, bf16[64,2048]{1,0:T(8,128)(2,1)S(1)}, u32[]{:S(2)}, u32[]{:S(2)}) collective-permute-start(bf16[64,2048]{1,0:T(8,128)(2,1)S(1)} %get-tuple-element.16), channel_id=1, source_target_pairs={{0,4},{4,8},{8,12},{12,13},{13,9},{9,5},{5,1},{1,0},{2,6},{6,10},{... | collective-permute-start | bytes 786440 | tf_op jit(solution)/shard_map/ppermute | solution.py:173
  4.1 6.7 %collective-permute-start.5 = (bf16[64,2048]{1,0:T(8,128)(2,1)S(1)}, bf16[64,2048]{1,0:T(8,128)(2,1)S(1)}, u32[]{:S(2)}, u32[]{:S(2)}) collective-permute-start(bf16[64,2048]{1,0:T(8,128)(2,1)S(1)} %get-tuple-element.15), channel_id=1, source_target_pairs={{0,4},{4,8},{8,12},{12,13},{13,9},{9,5},{5,1},{1,0},{2,6},{6,10},{... | collective-permute-start | bytes 786440 | tf_op jit(solution)/shard_map/ppermute | solution.py:173
  8.0 22.3 %copy-start = (bf16[64,2048]{1,0:T(8,128)(2,1)}, bf16[64,2048]{1,0:T(8,128)(2,1)S(1)}, u32[]{:S(2)}) copy-start(bf16[64,2048]{1,0:T(8,128)(2,1)S(1)} %collective-permute-done.2.refs_1_) | copy-start | bytes 786436
  8.0 6.4 %collective-permute-start.3 = (bf16[64,2048]{1,0:T(8,128)(2,1)S(1)}, bf16[64,2048]{1,0:T(8,128)(2,1)S(1)}, u32[]{:S(2)}, u32[]{:S(2)}) collective-permute-start(bf16[64,2048]{1,0:T(8,128)(2,1)S(1)} %collective-permute-done.2.refs_1_), channel_id=1, source_target_pairs={{0,4},{4,8},{8,12},{12,13},{13,9},{9,5},{5,1},{1,0},{2,6},{6,10},{... | collective-permute-start | bytes 786440 | tf_op jit(solution)/shard_map/ppermute | solution.py:173
  10.8 19.5 %copy-start.1 = (bf16[64,2048]{1,0:T(8,128)(2,1)}, bf16[64,2048]{1,0:T(8,128)(2,1)S(1)}, u32[]{:S(2)}) copy-start(bf16[64,2048]{1,0:T(8,128)(2,1)S(1)} %collective-permute-done.5.refs_2_) | copy-start | bytes 786436
  10.8 6.4 %collective-permute-start.6 = (bf16[64,2048]{1,0:T(8,128)(2,1)S(1)}, bf16[64,2048]{1,0:T(8,128)(2,1)S(1)}, u32[]{:S(2)}, u32[]{:S(2)}) collective-permute-start(bf16[64,2048]{1,0:T(8,128)(2,1)S(1)} %collective-permute-done.5.refs_2_), channel_id=1, source_target_pairs={{0,4},{4,8},{8,12},{12,13},{13,9},{9,5},{5,1},{1,0},{2,6},{6,10},{... | collective-permute-start | bytes 786440 | tf_op jit(solution)/shard_map/ppermute | solution.py:173
  13.3 15.1 %collective-permute-start.10 = (bf16[64,2048]{1,0:T(8,128)(2,1)S(1)}, bf16[64,2048]{1,0:T(8,128)(2,1)S(1)}, u32[]{:S(2)}, u32[]{:S(2)}) collective-permute-start(bf16[64,2048]{1,0:T(8,128)(2,1)S(1)} %collective-permute-done.2.refs_1_), channel_id=1, source_target_pairs={{0,1},{1,0},{2,3},{3,2},{4,5},{5,4},{6,7},{7,6},{8,9},{9,8},{10,11... | collective-permute-start | bytes 786440 | tf_op jit(solution)/shard_map/ppermute | solution.py:175
  14.4 15.9 %copy-start.3 = (bf16[64,2048]{1,0:T(8,128)(2,1)}, bf16[64,2048]{1,0:T(8,128)(2,1)S(1)}, u32[]{:S(2)}) copy-start(bf16[64,2048]{1,0:T(8,128)(2,1)S(1)} %collective-permute-done.3.refs_5_) | copy-start | bytes 786436
  14.4 14.5 %collective-permute-start.4 = (bf16[64,2048]{1,0:T(8,128)(2,1)S(1)}, bf16[64,2048]{1,0:T(8,128)(2,1)S(1)}, u32[]{:S(2)}, u32[]{:S(2)}) collective-permute-start(bf16[64,2048]{1,0:T(8,128)(2,1)S(1)} %collective-permute-done.3.refs_5_), channel_id=1, source_target_pairs={{0,4},{4,8},{8,12},{12,13},{13,9},{9,5},{5,1},{1,0},{2,6},{6,10},{... | collective-permute-start | bytes 786440 | tf_op jit(solution)/shard_map/ppermute | solution.py:173
  17.2 13.1 %copy-start.5 = (bf16[64,2048]{1,0:T(8,128)(2,1)}, bf16[64,2048]{1,0:T(8,128)(2,1)S(1)}, u32[]{:S(2)}) copy-start(bf16[64,2048]{1,0:T(8,128)(2,1)S(1)} %collective-permute-done.6.refs_6_) | copy-start | bytes 786436
  17.2 11.8 %collective-permute-start.7 = (bf16[64,2048]{1,0:T(8,128)(2,1)S(1)}, bf16[64,2048]{1,0:T(8,128)(2,1)S(1)}, u32[]{:S(2)}, u32[]{:S(2)}) collective-permute-start(bf16[64,2048]{1,0:T(8,128)(2,1)S(1)} %collective-permute-done.6.refs_6_), channel_id=1, source_target_pairs={{0,4},{4,8},{8,12},{12,13},{13,9},{9,5},{5,1},{1,0},{2,6},{6,10},{... | collective-permute-start | bytes 786440 | tf_op jit(solution)/shard_map/ppermute | solution.py:173
  20.4 3.6 %collective-permute-start = (f32[1,128]{1,0:T(1,128)S(1)}, f32[1,128]{1,0:T(1,128)S(1)}, u32[]{:S(2)}, u32[]{:S(2)}) collective-permute-start(f32[1,128]{1,0:T(1,128)S(1)} %convert_element_type.3), channel_id=1, source_target_pairs={{0,4},{4,0},{8,12},{12,8},{1,5},{5,1},{9,13},{13,9},{2,6},{6,2},{1... | collective-permute-start | bytes 1544 | tf_op jit(solution)/shard_map/ppermute | solution.py:177
  23.9 4.5 %collective-permute-start.1 = (f32[2,128]{1,0:T(2,128)S(1)}, f32[2,128]{1,0:T(2,128)S(1)}, u32[]{:S(2)}, u32[]{:S(2)}) collective-permute-start(f32[2,128]{1,0:T(2,128)S(1)} %pad_maximum_fusion.1), channel_id=1, source_target_pairs={{0,8},{4,12},{8,0},{12,4},{1,9},{5,13},{9,1},{13,5},{2,10},{6,14},... | collective-permute-start | bytes 3080 | tf_op jit(solution)/shard_map/ppermute | solution.py:177
  26.5 3.5 %collective-permute-start.11 = (bf16[64,2048]{1,0:T(8,128)(2,1)S(1)}, bf16[64,2048]{1,0:T(8,128)(2,1)S(1)}, u32[]{:S(2)}, u32[]{:S(2)}) collective-permute-start(bf16[64,2048]{1,0:T(8,128)(2,1)S(1)} %collective-permute-done.5.refs_2_), channel_id=1, source_target_pairs={{0,1},{1,0},{2,3},{3,2},{4,5},{5,4},{6,7},{7,6},{8,9},{9,8},{10,11... | collective-permute-start | bytes 786440 | tf_op jit(solution)/shard_map/ppermute | solution.py:175
  28.4 1.6 %collective-permute-start.12 = (bf16[64,2048]{1,0:T(8,128)(2,1)S(1)}, bf16[64,2048]{1,0:T(8,128)(2,1)S(1)}, u32[]{:S(2)}, u32[]{:S(2)}) collective-permute-start(bf16[64,2048]{1,0:T(8,128)(2,1)S(1)} %collective-permute-done.3.refs_5_), channel_id=1, source_target_pairs={{0,1},{1,0},{2,3},{3,2},{4,5},{5,4},{6,7},{7,6},{8,9},{9,8},{10,11... | collective-permute-start | bytes 786440 | tf_op jit(solution)/shard_map/ppermute | solution.py:175
  28.4 1.9 %copy-start.6 = (bf16[64,2048]{1,0:T(8,128)(2,1)}, bf16[64,2048]{1,0:T(8,128)(2,1)S(1)}, u32[]{:S(2)}) copy-start(bf16[64,2048]{1,0:T(8,128)(2,1)S(1)} %collective-permute-done.10.refs_3_) | copy-start | bytes 786436
  28.4 1.9 %collective-permute-start.13 = (bf16[64,2048]{1,0:T(8,128)(2,1)S(1)}, bf16[64,2048]{1,0:T(8,128)(2,1)S(1)}, u32[]{:S(2)}, u32[]{:S(2)}) collective-permute-start(bf16[64,2048]{1,0:T(8,128)(2,1)S(1)} %collective-permute-done.6.refs_6_), channel_id=1, source_target_pairs={{0,1},{1,0},{2,3},{3,2},{4,5},{5,4},{6,7},{7,6},{8,9},{9,8},{10,11... | collective-permute-start | bytes 786440 | tf_op jit(solution)/shard_map/ppermute | solution.py:175
  28.9 6.5 %copy-start.2 = (bf16[64,2048]{1,0:T(8,128)(2,1)}, bf16[64,2048]{1,0:T(8,128)(2,1)S(1)}, u32[]{:S(2)}) copy-start(bf16[64,2048]{1,0:T(8,128)(2,1)S(1)} %collective-permute-done.4.refs_0_) | copy-start | bytes 786436
  28.9 8.0 %collective-permute-start.8 = (bf16[64,2048]{1,0:T(8,128)(2,1)S(1)}, bf16[64,2048]{1,0:T(8,128)(2,1)S(1)}, u32[]{:S(2)}, u32[]{:S(2)}) collective-permute-start(bf16[64,2048]{1,0:T(8,128)(2,1)S(1)} %collective-permute-done.4.refs_0_), channel_id=1, source_target_pairs={{0,1},{1,0},{2,3},{3,2},{4,5},{5,4},{6,7},{7,6},{8,9},{9,8},{10,11... | collective-permute-start | bytes 786440 | tf_op jit(solution)/shard_map/ppermute | solution.py:175
  29.0 6.4 %copy-start.4 = (bf16[64,2048]{1,0:T(8,128)(2,1)}, bf16[64,2048]{1,0:T(8,128)(2,1)S(1)}, u32[]{:S(2)}) copy-start(bf16[64,2048]{1,0:T(8,128)(2,1)S(1)} %collective-permute-done.7.refs_1_) | copy-start | bytes 786436
  29.0 7.9 %collective-permute-start.9 = (bf16[64,2048]{1,0:T(8,128)(2,1)S(1)}, bf16[64,2048]{1,0:T(8,128)(2,1)S(1)}, u32[]{:S(2)}, u32[]{:S(2)}) collective-permute-start(bf16[64,2048]{1,0:T(8,128)(2,1)S(1)} %collective-permute-done.7.refs_1_), channel_id=1, source_target_pairs={{0,1},{1,0},{2,3},{3,2},{4,5},{5,4},{6,7},{7,6},{8,9},{9,8},{10,11... | collective-permute-start | bytes 786440 | tf_op jit(solution)/shard_map/ppermute | solution.py:175
  35.4 9.1 %collective-permute-start.14 = (f32[512,128]{1,0:T(8,128)}, f32[512,128]{1,0:T(8,128)S(1)}, u32[]{:S(2)}, u32[]{:S(2)}) collective-permute-start(f32[512,128]{1,0:T(8,128)} %get-tuple-element.11.refs_5_), channel_id=1, source_target_pairs={{0,2},{2,0},{1,3},{3,1},{4,6},{6,4},{5,7},{7,5},{8,10},{10,8},{9,1... | collective-permute-start | bytes 786440 | tf_op jit(solution)/shard_map/ppermute | solution.py:209
  41.9 8.3 %collective-permute-start.15 = (f32[512,128]{1,0:T(8,128)}, f32[512,128]{1,0:T(8,128)S(1)}, u32[]{:S(2)}, u32[]{:S(2)}) collective-permute-start(f32[512,128]{1,0:T(8,128)} %get-tuple-element.14), channel_id=1, source_target_pairs={{0,2},{2,0},{1,3},{3,1},{4,6},{6,4},{5,7},{7,5},{8,10},{10,8},{9,1... | collective-permute-start | bytes 786440 | tf_op jit(solution)/shard_map/ppermute | solution.py:209
  44.4 5.7 %copy-start.12 = (f32[512,128]{1,0:T(8,128)}, f32[512,128]{1,0:T(8,128)S(1)}, u32[]{:S(2)}) copy-start(f32[512,128]{1,0:T(8,128)S(1)} %collective-permute-done.14.refs_0_) | copy-start | bytes 786436
  (6 other events, 4.5 us)

commit v2 on v0

v2 whole, which is shorter than its diff:
```python
import functools

import jax
import jax.numpy as jnp
from jax import lax
from jax.experimental import pallas as pl
from jax.experimental.pallas import tpu as pltpu
from jax.sharding import PartitionSpec as P


CHUNKS = 2
ANY = pl.BlockSpec(memory_space=pl.ANY)
VMEM = pl.BlockSpec(memory_space=pltpu.VMEM)
SMEM = pl.BlockSpec(memory_space=pltpu.SMEM)
LIMIT = 20 * 2**20


def fold_ring(n):
    order = [2 * z for z in range(n)] + [2 * z + 1 for z in reversed(range(n))]
    return [(order[i], order[(i + 1) % len(order)]) for i in range(len(order))]


def shift(n, by):
    return [(i, (i + by) % n) for i in range(n)]


def xor(n, bit):
    return [(i, i ^ bit) for i in range(n)]


def rank_of(block, z, owned):
    mine = jnp.abs(block - z)
    rank = jnp.int32(0)
    for other in owned:
        far = jnp.abs(other - z)
        nearer = (far < mine) | ((far == mine) & (other < block))
        rank = rank + nearer.astype(jnp.int32)
    return rank


def listed(pair_ref, b, block):
    wanted = pair_ref[b, 0] == block
    for k in range(1, pair_ref.shape[1]):
        wanted = wanted | (pair_ref[b, k] == block)
    return wanted


def sources(dists, chunks, refs):
    z = lax.axis_index("blk")
    core = lax.axis_index("qry")
    at = 0
    found = []
    for d in dists:
        if d == 0:
            found.append((z, refs[at : at + 1]))
            at += 1
        else:
            found.append((z + jnp.where(core == 0, -d, d), refs[at : at + chunks]))
            found.append((z + jnp.where(core == 0, d, -d), refs[at + chunks : at + 2 * chunks]))
            at += 2 * chunks
    return found


def fetch(block, pool, into, sem):
    for held, refs in pool:

        @pl.when(held == block)
        def _():
            piece = into.shape[0] // len(refs)
            for i, ref in enumerate(refs):
                pltpu.make_async_copy(ref, into.at[pl.ds(i * piece, piece)], sem).start()


def dot_rows(a, b):
    return lax.dot_general(a, b, (((1,), (1,)), ((), ())), preferred_element_type=jnp.float32)


def slot_kernel(n, ckpts, s, dists, chunks, pair_ref, owner_ref, w_ref, q_ref, *refs):
    per, nb = n // ckpts, pair_ref.shape[0]
    ins = refs[: -(ckpts - 1) - 2]
    outs = refs[-(ckpts - 1) - 2 : -2]
    rows, sem = refs[-2:]
    z, c = lax.axis_index("blk"), lax.axis_index("ckpt")
    qblk = q_ref.shape[0] // nb
    pool = sources(dists, chunks, ins)
    for r in range(1, ckpts):
        owner = lax.rem(c + r, ckpts)
        owned = [owner_ref[owner * per + k] for k in range(per)]
        block = jnp.int32(0)
        for one in owned:
            block = jnp.where(rank_of(one, z, owned) == s, one, block)
        fetch(block, pool, rows, sem)
        pltpu.make_async_copy(ins[0], rows, sem).wait()
        weight = w_ref[pl.ds(block ^ z, 1), :]
        for b in range(nb):
            span = pl.ds(b * qblk, qblk)
            wanted = listed(pair_ref, b, block)

            @pl.when(wanted)
            def _():
                outs[r - 1][span, :] = dot_rows(q_ref[span, :], rows[...]) * weight

            @pl.when(jnp.logical_not(wanted))
            def _():
                outs[r - 1][span, :] = jnp.zeros((qblk, rows.shape[0]), jnp.float32)


def own_kernel(n, ckpts, dists, chunks, pair_ref, owner_ref, w_ref, q_ref, *refs):
    per, nb = n // ckpts, pair_ref.shape[0]
    early = (per - 1) * (ckpts - 1)
    ins, came, out = refs[: len(refs) - early - 3], refs[len(refs) - early - 3 : -3], refs[-3]
    rows, sem = refs[-2:]
    z, c = lax.axis_index("blk"), lax.axis_index("ckpt")
    qblk = q_ref.shape[0] // nb
    width = rows.shape[1]
    pool = sources(dists, chunks, ins)
    owned = [owner_ref[c * per + k] for k in range(per)]
    for j, block in enumerate(owned):
        fetch(block, pool, rows.at[j], sem.at[j])
    for j, block in enumerate(owned):
        pltpu.make_async_copy(ins[0], rows.at[j], sem.at[j]).wait()
        cols = slice(j * width, (j + 1) * width)
        weight = w_ref[pl.ds(block ^ z, 1), :]
        for b in range(nb):
            span = pl.ds(b * qblk, qblk)
            wanted = listed(pair_ref, b, block)

            @pl.when(wanted)
            def _():
                out[span, cols] = dot_rows(q_ref[span, :], rows[j]) * weight

            @pl.when(jnp.logical_not(wanted))
            def _():
                out[span, cols] = jnp.zeros((qblk, width), jnp.float32)

        rank = rank_of(block, z, owned)
        for s in range(per - 1):

            @pl.when(rank == s)
            def _():
                for r in range(ckpts - 1):
                    out[:, cols] += came[s * (ckpts - 1) + r][...]


def sum_kernel(n, ckpts, owner_ref, acc_ref, *refs):
    per = n // ckpts
    came, out, tile, sem = refs[:-3], refs[-3], refs[-2], refs[-1]
    z, c = lax.axis_index("blk"), lax.axis_index("ckpt")
    width = tile.shape[1]
    owned = [owner_ref[c * per + k] for k in range(per)]
    last = jnp.int32(0)
    for j, block in enumerate(owned):
        last = jnp.where(rank_of(block, z, owned) == per - 1, j, last)
    cols = pl.ds(pl.multiple_of(last * width, width), width)
    load = pltpu.make_async_copy(acc_ref.at[:, cols], tile, sem)
    load.start()
    load.wait()
    total = tile[...]
    for part in came:
        total = total + part[...]
    tile[...] = total
    store = pltpu.make_async_copy(tile, out.at[:, cols], sem)
    store.start()
    store.wait()


def per_device(query_feats, train_feats, loss_weights, pair_list, tile_owner):
    queries, own_rows = query_feats[0], train_feats[0]
    n, ckpts = lax.axis_size("blk"), lax.axis_size("ckpt")
    per = n // ckpts
    rows, feats = own_rows.shape
    count = queries.shape[0]
    lines = ("blk", "qry")
    ring, swap = fold_ring(n), shift(2, 1)
    chunks, piece = CHUNKS, rows // CHUNKS

    held = [own_rows[i * piece : (i + 1) * piece] for i in range(chunks)]
    near = {0: [own_rows]}
    for step in range(1, n):
        held = [lax.ppermute(part, lines, ring) for part in held]
        near[step] = held + [lax.ppermute(part, "qry", swap) for part in held]
    weights = loss_weights.astype(jnp.float32)
    bit = 1
    while bit < n:
        weights = jnp.concatenate([weights, lax.ppermute(weights, "blk", xor(n, bit))], axis=0)
        bit *= 2

    tile = jax.ShapeDtypeStruct((count, rows), jnp.float32)
    acc = jax.ShapeDtypeStruct((count, per * rows), jnp.float32)
    params = pltpu.CompilerParams(vmem_limit_bytes=LIMIT)
    flops = 2 * count * rows * feats
    came = []
    for s in range(per):
        dists = tuple(range(n - per + s + 1))
        pool = [ref for d in dists for ref in near[d]]
        terms = pl.pallas_call(
            functools.partial(slot_kernel, n, ckpts, s, dists, chunks),
            out_shape=[tile] * (ckpts - 1),
            in_specs=[SMEM, SMEM, VMEM, VMEM] + [ANY] * len(pool),
            out_specs=[VMEM] * (ckpts - 1),
            scratch_shapes=[pltpu.VMEM((rows, feats), jnp.bfloat16), pltpu.SemaphoreType.DMA],
            compiler_params=params,
            cost_estimate=pl.CostEstimate(flops=flops * (ckpts - 1), bytes_accessed=count * feats * 2, transcendentals=0),
        )(pair_list, tile_owner, weights, queries, *pool)
        came.append([lax.ppermute(terms[r - 1], "ckpt", shift(ckpts, r)) for r in range(1, ckpts)])
    early = [part for parts in came[:-1] for part in parts]
    total = pl.pallas_call(
        functools.partial(own_kernel, n, ckpts, dists, chunks),
        out_shape=acc,
        in_specs=[SMEM, SMEM, VMEM, VMEM] + [ANY] * len(pool) + [VMEM] * len(early),
        out_specs=VMEM,
        scratch_shapes=[pltpu.VMEM((per, rows, feats), jnp.bfloat16), pltpu.SemaphoreType.DMA((per,))],
        compiler_params=params,
        cost_estimate=pl.CostEstimate(flops=flops * per, bytes_accessed=count * feats * 2, transcendentals=0),
    )(pair_list, tile_owner, weights, queries, *pool, *early)
    return pl.pallas_call(
        functools.partial(sum_kernel, n, ckpts),
        out_shape=acc,
        in_specs=[SMEM, ANY] + [VMEM] * (ckpts - 1),
        out_specs=ANY,
        input_output_aliases={1: 0},
        scratch_shapes=[pltpu.VMEM((count, rows), jnp.float32), pltpu.SemaphoreType.DMA],
        compiler_params=params,
    )(tile_owner, total, *came[-1])


def solution(mesh):
    return jax.shard_map(
        per_device,
        mesh=mesh,
        in_specs=(
            P("ckpt", ("shard", "blk", "qry"), None),
            P("ckpt", ("shard", "blk"), None),
            P("ckpt", ("shard", "blk")),
            P(("shard", "blk", "qry"), None),
            P("shard"),
        ),
        out_specs=P(("shard", "blk", "qry"), "ckpt"),
        check_vma=False,
    )
```

time: 93.4 us -> 51.8 us (0.55)
  waiting for transfers between devices: 54.5 us -> 16.4 us
  starting transfers between devices: 0.04 us -> 22.2 us
  between operations: 13.4 us -> 0.06 us
  blocking collectives: 12.8 us -> 0 us
  Pallas kernels: 0 us -> 6.99 us
  matrix products: 3.86 us -> 0 us
  local copies, waits for them, and re-layouts: 7.07 us -> 5.03 us
    all_gather x1 -> x0, waiting for transfers between devices: 34.4 us -> none  [per_device(): lax.all_gather(own_rows, 'blk', axis=0, tiled=True)]
    ppermute x0 -> x16, starting transfers between devices: none -> 22.2 us  [the longest x6 14.6 us: per_device(): held = [lax.ppermute(part, lines, ring) for part in held]]
    reduce_scatter x1 -> x0, waiting for transfers between devices: 19.3 us -> none  [per_device(): lax.psum_scatter(products * picked_weights[:, None] * mask_rows, 'ckpt',...]
    ppermute x0 -> x16, waiting for transfers between devices: none -> 16.4 us  [the longest x2 7.64 us: per_device(): lax.ppermute(terms[r - 1], 'ckpt', shift(ckpts, r))]
    all_gather x1 -> x0, blocking collectives: 12.8 us -> none  [per_device(): lax.all_gather(own_weights, 'blk', axis=0, tiled=True)]
    pallas_call x0 -> x4, Pallas kernels: none -> 6.99 us  [the longest x1 2.5 us: per_device(): pl.pallas_call(functools.partial(own_kernel, n, ckpts, dists, chunks), ou...]
    gather x3 -> x0, local copies, waits for them, and re-layouts: 4.74 us -> none  [the longest x1 3.62 us: per_device(): row_blocks[tile_owner]]
    unnamed x4 -> x8, local copies, waits for them, and re-layouts: 0.08 us -> 3.97 us
  transfers between devices with their start and end apart: 2 -> 16, of which waited for: 2 -> 10; matrix products, arithmetic and copies ran while one was open for 3% -> 1% of each run, Pallas kernels for 0% -> 9%
where the time goes in v2:
time: 51.8 us; the launch traced here: 51.4 us
  starting transfers between devices  22.2 us (43%)
  waiting for transfers between devices  16.4 us (32%)
  Pallas kernels  6.99 us (13%)
  local copies, waits for them, and re-layouts  5.03 us (10%)
  other arithmetic  0.67 us (1%)
    ppermute x6, starting transfers between devices, per_device(): held = [lax.ppermute(part, lines, ring) for part in held]  14.6 us
    ppermute x2, waiting for transfers between devices, per_device(): lax.ppermute(terms[r - 1], 'ckpt', shift(ckpts, r))  7.64 us
    ppermute x2, starting transfers between devices, per_device(): lax.ppermute(weights, 'blk', xor(n, bit))  4.17 us
    ppermute x6, waiting for transfers between devices, per_device(): held = [lax.ppermute(part, lines, ring) for part in held]  4.05 us
    unnamed x8, local copies, waits for them, and re-layouts  3.97 us
    ppermute x2, waiting for transfers between devices, per_device(): lax.ppermute(weights, 'blk', xor(n, bit))  3.87 us
    pallas_call x1, Pallas kernels, per_device(): pl.pallas_call(functools.partial(own_kernel, n, ckpts, dists, chunks), ou...  2.5 us
    ppermute x2, starting transfers between devices, per_device(): lax.ppermute(terms[r - 1], 'ckpt', shift(ckpts, r))  2.48 us
  transfers between devices with their start and end apart: 16, of which 10 were waited for; matrix products, arithmetic and copies ran while one was open for 1% of the time, Pallas kernels for 9%

profile of v2, /device:TPU:0, one launch (start us, length us, event | category | flops | bytes accessed | tf_op | source)
XLA Modules:
  0.0 51.4 jit_solution(11879221518682215849)
XLA Ops:
  0.0 1.1 %slice_bitcast_fusion = (bf16[64,2048]{1,0:T(8,128)(2,1)S(1)}, bf16[64,2048]{1,0:T(8,128)(2,1)S(1)}) fusion(bf16[1,128,2048]{2,1,0:T(8,128)(2,1)} %param.6), kind=kLoop, calls=%fused_computation | loop fusion | bytes 1048576 | tf_op jit(solution)/shard_map/slice | solution.py:177
  1.1 3.1 %collective-permute-start.2 = (bf16[64,2048]{1,0:T(8,128)(2,1)S(1)}, bf16[64,2048]{1,0:T(8,128)(2,1)S(1)}, u32[]{:S(2)}, u32[]{:S(2)}) collective-permute-start(bf16[64,2048]{1,0:T(8,128)(2,1)S(1)} %get-tuple-element.6), channel_id=1, source_target_pairs={{0,4},{4,8},{8,12},{12,13},{13,9},{9,5},{5,1},{1,0},{2,6},{6,10},{... | collective-permute-start | bytes 786440 | tf_op jit(solution)/shard_map/ppermute | solution.py:180
  4.1 1.6 %collective-permute-start.3 = (bf16[64,2048]{1,0:T(8,128)(2,1)S(1)}, bf16[64,2048]{1,0:T(8,128)(2,1)S(1)}, u32[]{:S(2)}, u32[]{:S(2)}) collective-permute-start(bf16[64,2048]{1,0:T(8,128)(2,1)S(1)} %get-tuple-element.5), channel_id=1, source_target_pairs={{0,4},{4,8},{8,12},{12,13},{13,9},{9,5},{5,1},{1,0},{2,6},{6,10},{... | collective-permute-start | bytes 786440 | tf_op jit(solution)/shard_map/ppermute | solution.py:180
  5.7 2.3 %collective-permute-done.2.refs_1_ = bf16[64,2048]{1,0:T(8,128)(2,1)S(1)} collective-permute-done((bf16[64,2048]{1,0:T(8,128)(2,1)S(1)}, bf16[64,2048]{1,0:T(8,128)(2,1)S(1)}, u32[]{:S(2)}, u32[]{:S(2)}) %collective-permute-start.2) | collective-permute-done | bytes 262176 | tf_op jit(solution)/shard_map/ppermute | solution.py:180
  8.0 2.5 %collective-permute-start.6 = (bf16[64,2048]{1,0:T(8,128)(2,1)S(1)}, bf16[64,2048]{1,0:T(8,128)(2,1)S(1)}, u32[]{:S(2)}, u32[]{:S(2)}) collective-permute-start(bf16[64,2048]{1,0:T(8,128)(2,1)S(1)} %collective-permute-done.2.refs_1_), channel_id=1, source_target_pairs={{0,4},{4,8},{8,12},{12,13},{13,9},{9,5},{5,1},{1,0},{2,6},{6,10},{... | collective-permute-start | bytes 786440 | tf_op jit(solution)/shard_map/ppermute | solution.py:180
  10.8 2.5 %collective-permute-start.7 = (bf16[64,2048]{1,0:T(8,128)(2,1)S(1)}, bf16[64,2048]{1,0:T(8,128)(2,1)S(1)}, u32[]{:S(2)}, u32[]{:S(2)}) collective-permute-start(bf16[64,2048]{1,0:T(8,128)(2,1)S(1)} %collective-permute-done.3.refs_2_), channel_id=1, source_target_pairs={{0,4},{4,8},{8,12},{12,13},{13,9},{9,5},{5,1},{1,0},{2,6},{6,10},{... | collective-permute-start | bytes 786440 | tf_op jit(solution)/shard_map/ppermute | solution.py:180
  13.3 1.1 %collective-permute-done.6.refs_5_ = bf16[64,2048]{1,0:T(8,128)(2,1)S(1)} collective-permute-done((bf16[64,2048]{1,0:T(8,128)(2,1)S(1)}, bf16[64,2048]{1,0:T(8,128)(2,1)S(1)}, u32[]{:S(2)}, u32[]{:S(2)}) %collective-permute-start.6) | collective-permute-done | bytes 262176 | tf_op jit(solution)/shard_map/ppermute | solution.py:180
  14.4 2.5 %collective-permute-start.10 = (bf16[64,2048]{1,0:T(8,128)(2,1)S(1)}, bf16[64,2048]{1,0:T(8,128)(2,1)S(1)}, u32[]{:S(2)}, u32[]{:S(2)}) collective-permute-start(bf16[64,2048]{1,0:T(8,128)(2,1)S(1)} %collective-permute-done.6.refs_5_), channel_id=1, source_target_pairs={{0,4},{4,8},{8,12},{12,13},{13,9},{9,5},{5,1},{1,0},{2,6},{6,10},{... | collective-permute-start | bytes 786440 | tf_op jit(solution)/shard_map/ppermute | solution.py:180
  17.2 2.5 %collective-permute-start.11 = (bf16[64,2048]{1,0:T(8,128)(2,1)S(1)}, bf16[64,2048]{1,0:T(8,128)(2,1)S(1)}, u32[]{:S(2)}, u32[]{:S(2)}) collective-permute-start(bf16[64,2048]{1,0:T(8,128)(2,1)S(1)} %collective-permute-done.7.refs_6_), channel_id=1, source_target_pairs={{0,4},{4,8},{8,12},{12,13},{13,9},{9,5},{5,1},{1,0},{2,6},{6,10},{... | collective-permute-start | bytes 786440 | tf_op jit(solution)/shard_map/ppermute | solution.py:180
  19.7 0.7 %convert_element_type.3 = f32[1,128]{1,0:T(1,128)S(1)} convert(bf16[1,128]{1,0:T(2,128)(2,1)} %param.7) | non-fusion elementwise | flops 128 | bytes 768 | tf_op jit(solution)/shard_map/convert_element_type | solution.py:182
  20.3 1.6 %collective-permute-start = (f32[1,128]{1,0:T(1,128)S(1)}, f32[1,128]{1,0:T(1,128)S(1)}, u32[]{:S(2)}, u32[]{:S(2)}) collective-permute-start(f32[1,128]{1,0:T(1,128)S(1)} %convert_element_type.3), channel_id=1, source_target_pairs={{0,4},{4,0},{8,12},{12,8},{1,5},{5,1},{9,13},{13,9},{2,6},{6,2},{1... | collective-permute-start | bytes 1544 | tf_op jit(solution)/shard_map/ppermute | solution.py:185
  21.9 2.0 %collective-permute-done = f32[1,128]{1,0:T(1,128)S(1)} collective-permute-done((f32[1,128]{1,0:T(1,128)S(1)}, f32[1,128]{1,0:T(1,128)S(1)}, u32[]{:S(2)}, u32[]{:S(2)}) %collective-permute-start) | collective-permute-done | bytes 544 | tf_op jit(solution)/shard_map/ppermute | solution.py:185
  23.9 2.6 %collective-permute-start.1 = (f32[2,128]{1,0:T(2,128)S(1)}, f32[2,128]{1,0:T(2,128)S(1)}, u32[]{:S(2)}, u32[]{:S(2)}) collective-permute-start(f32[2,128]{1,0:T(2,128)S(1)} %pad_maximum_fusion.1), channel_id=1, source_target_pairs={{0,8},{4,12},{8,0},{12,4},{1,9},{5,13},{9,1},{13,5},{2,10},{6,14},... | collective-permute-start | bytes 3080 | tf_op jit(solution)/shard_map/ppermute | solution.py:185
  26.5 1.9 %collective-permute-done.1 = f32[2,128]{1,0:T(2,128)S(1)} collective-permute-done((f32[2,128]{1,0:T(2,128)S(1)}, f32[2,128]{1,0:T(2,128)S(1)}, u32[]{:S(2)}, u32[]{:S(2)}) %collective-permute-start.1) | collective-permute-done | bytes 1056 | tf_op jit(solution)/shard_map/ppermute | solution.py:185
  30.3 1.6 %copy-done = bf16[1,512,2048]{2,1,0:T(8,128)(2,1)S(1)} copy-done((bf16[1,512,2048]{2,1,0:T(8,128)(2,1)S(1)}, bf16[1,512,2048]{2,1,0:T(8,128)(2,1)}, u32[]{:S(2)}) %copy-start) | copy-done | bytes 2097176
  31.9 1.0 %copy-done.1 = bf16[1,128,2048]{2,1,0:T(8,128)(2,1)S(1)} copy-done((bf16[1,128,2048]{2,1,0:T(8,128)(2,1)S(1)}, bf16[1,128,2048]{2,1,0:T(8,128)(2,1)}, u32[]{:S(2)}) %copy-start.1) | copy-done | bytes 524312
  32.9 0.7 %copy-done.2 = s32[2,2]{1,0:T(2,128)S(1)} copy-done((s32[2,2]{1,0:T(2,128)S(1)}, s32[2,2]{1,0:T(2,128)}, u32[]{:S(2)}) %copy-start.2) | copy-done | bytes 40
  34.3 0.7 %shard_map.55 = f32[512,128]{1,0:T(8,128)S(1)} custom-call(s32[2,2]{1,0:T(2,128)S(1)} %copy-done.2, s32[4]{0:T(128)S(1)} %copy-done.3, f32[4,128]{1,0:T(4,128)S(1)} %pad_maximum_fusion.w_ref, bf16[512,2048]{1,0:T(8,128)(2,1)S(1)} %bitcast.6, bf16[128,2048]{1,0:T(8,128)(2,1)S(1)} %bitcast.9, bf16[64,2048]{1,0:T(8,128)(2,1)S(1)} %collective-permute-done.2.refs_1_, ...), custom_call_target="tpu_custom_call" | custom-call | flops 268435456 | bytes 2097152 | tf_op jit(solution)/shard_map/pallas_call | solution.py:196
  35.0 2.4 %collective-permute-start.14 = (f32[512,128]{1,0:T(8,128)S(1)}, f32[512,128]{1,0:T(8,128)S(1)}, u32[]{:S(2)}, u32[]{:S(2)}) collective-permute-start(f32[512,128]{1,0:T(8,128)S(1)} %shard_map.55), channel_id=1, source_target_pairs={{0,2},{2,0},{1,3},{3,1},{4,6},{6,4},{5,7},{7,5},{8,10},{10,8},{9,1... | collective-permute-start | bytes 786440 | tf_op jit(solution)/shard_map/ppermute | solution.py:205
  37.4 1.6 %shard_map.57 = f32[512,128]{1,0:T(8,128)S(1)} custom-call(s32[2,2]{1,0:T(2,128)S(1)} %copy-done.2, s32[4]{0:T(128)S(1)} %copy-done.3, f32[4,128]{1,0:T(4,128)S(1)} %pad_maximum_fusion.w_ref, bf16[512,2048]{1,0:T(8,128)(2,1)S(1)} %bitcast.7, bf16[128,2048]{1,0:T(8,128)(2,1)S(1)} %bitcast.10, bf16[64,2048]{1,0:T(8,128)(2,1)S(1)} %collective-permute-done.2.refs_1_, ...), custom_call_target="tpu_custom_call" | custom-call | flops 268435456 | bytes 2097152 | tf_op jit(solution)/shard_map/pallas_call | solution.py:196
  39.0 5.5 %collective-permute-done.14.refs_13_ = f32[512,128]{1,0:T(8,128)S(1)} collective-permute-done((f32[512,128]{1,0:T(8,128)S(1)}, f32[512,128]{1,0:T(8,128)S(1)}, u32[]{:S(2)}, u32[]{:S(2)}) %collective-permute-start.14) | collective-permute-done | bytes 262176 | tf_op jit(solution)/shard_map/ppermute | solution.py:205
  44.6 2.5 %shard_map.56.acc_ref = f32[512,256]{1,0:T(8,128)} custom-call(s32[2,2]{1,0:T(2,128)S(1)} %copy-done.2, s32[4]{0:T(128)S(1)} %copy-done.3, f32[4,128]{1,0:T(4,128)S(1)} %pad_maximum_fusion.w_ref, bf16[512,2048]{1,0:T(8,128)(2,1)S(1)} %bitcast.8, bf16[128,2048]{1,0:T(8,128)(2,1)S(1)} %bitcast.11, bf16[64,2048]{1,0:T(8,128)(2,1)S(1)} %collective-permute-done.2.refs_1_, ...), custom_call_target="tpu_custom_call" | custom-call | flops 536870912 | bytes 2097152 | tf_op jit(solution)/shard_map/pallas_call | solution.py:207
  47.1 2.1 %collective-permute-done.15.refs_0_ = f32[512,128]{1,0:T(8,128)S(1)} collective-permute-done((f32[512,128]{1,0:T(8,128)S(1)}, f32[512,128]{1,0:T(8,128)S(1)}, u32[]{:S(2)}, u32[]{:S(2)}) %collective-permute-start.15) | collective-permute-done | bytes 262176 | tf_op jit(solution)/shard_map/ppermute | solution.py:205
  49.2 2.2 %shard_map.58 = f32[512,256]{1,0:T(8,128)} custom-call(s32[4]{0:T(128)S(1)} %copy-done.3, f32[512,256]{1,0:T(8,128)} %shard_map.56.acc_ref, f32[512,128]{1,0:T(8,128)S(1)} %collective-permute-done.15.refs_0_), custom_call_target="tpu_custom_call", output_to_operand_aliasing={{}: (1, {})} | custom-call | tf_op jit(solution)/shard_map/pallas_call | solution.py:216
  (24 shorter events, 3.3 us)
Async XLA Ops:
  1.1 7.0 %collective-permute-start.2 = (bf16[64,2048]{1,0:T(8,128)(2,1)S(1)}, bf16[64,2048]{1,0:T(8,128)(2,1)S(1)}, u32[]{:S(2)}, u32[]{:S(2)}) collective-permute-start(bf16[64,2048]{1,0:T(8,128)(2,1)S(1)} %get-tuple-element.6), channel_id=1, source_target_pairs={{0,4},{4,8},{8,12},{12,13},{13,9},{9,5},{5,1},{1,0},{2,6},{6,10},{... | collective-permute-start | bytes 786440 | tf_op jit(solution)/shard_map/ppermute | solution.py:180
  4.1 6.7 %collective-permute-start.3 = (bf16[64,2048]{1,0:T(8,128)(2,1)S(1)}, bf16[64,2048]{1,0:T(8,128)(2,1)S(1)}, u32[]{:S(2)}, u32[]{:S(2)}) collective-permute-start(bf16[64,2048]{1,0:T(8,128)(2,1)S(1)} %get-tuple-element.5), channel_id=1, source_target_pairs={{0,4},{4,8},{8,12},{12,13},{13,9},{9,5},{5,1},{1,0},{2,6},{6,10},{... | collective-permute-start | bytes 786440 | tf_op jit(solution)/shard_map/ppermute | solution.py:180
  8.0 6.4 %collective-permute-start.6 = (bf16[64,2048]{1,0:T(8,128)(2,1)S(1)}, bf16[64,2048]{1,0:T(8,128)(2,1)S(1)}, u32[]{:S(2)}, u32[]{:S(2)}) collective-permute-start(bf16[64,2048]{1,0:T(8,128)(2,1)S(1)} %collective-permute-done.2.refs_1_), channel_id=1, source_target_pairs={{0,4},{4,8},{8,12},{12,13},{13,9},{9,5},{5,1},{1,0},{2,6},{6,10},{... | collective-permute-start | bytes 786440 | tf_op jit(solution)/shard_map/ppermute | solution.py:180
  10.8 6.4 %collective-permute-start.7 = (bf16[64,2048]{1,0:T(8,128)(2,1)S(1)}, bf16[64,2048]{1,0:T(8,128)(2,1)S(1)}, u32[]{:S(2)}, u32[]{:S(2)}) collective-permute-start(bf16[64,2048]{1,0:T(8,128)(2,1)S(1)} %collective-permute-done.3.refs_2_), channel_id=1, source_target_pairs={{0,4},{4,8},{8,12},{12,13},{13,9},{9,5},{5,1},{1,0},{2,6},{6,10},{... | collective-permute-start | bytes 786440 | tf_op jit(solution)/shard_map/ppermute | solution.py:180
  13.3 15.1 %collective-permute-start.4 = (bf16[64,2048]{1,0:T(8,128)(2,1)S(1)}, bf16[64,2048]{1,0:T(8,128)(2,1)S(1)}, u32[]{:S(2)}, u32[]{:S(2)}) collective-permute-start(bf16[64,2048]{1,0:T(8,128)(2,1)S(1)} %collective-permute-done.2.refs_1_), channel_id=1, source_target_pairs={{0,1},{1,0},{2,3},{3,2},{4,5},{5,4},{6,7},{7,6},{8,9},{9,8},{10,11... | collective-permute-start | bytes 786440 | tf_op jit(solution)/shard_map/ppermute | solution.py:181
  14.4 14.5 %collective-permute-start.10 = (bf16[64,2048]{1,0:T(8,128)(2,1)S(1)}, bf16[64,2048]{1,0:T(8,128)(2,1)S(1)}, u32[]{:S(2)}, u32[]{:S(2)}) collective-permute-start(bf16[64,2048]{1,0:T(8,128)(2,1)S(1)} %collective-permute-done.6.refs_5_), channel_id=1, source_target_pairs={{0,4},{4,8},{8,12},{12,13},{13,9},{9,5},{5,1},{1,0},{2,6},{6,10},{... | collective-permute-start | bytes 786440 | tf_op jit(solution)/shard_map/ppermute | solution.py:180
  17.2 11.8 %collective-permute-start.11 = (bf16[64,2048]{1,0:T(8,128)(2,1)S(1)}, bf16[64,2048]{1,0:T(8,128)(2,1)S(1)}, u32[]{:S(2)}, u32[]{:S(2)}) collective-permute-start(bf16[64,2048]{1,0:T(8,128)(2,1)S(1)} %collective-permute-done.7.refs_6_), channel_id=1, source_target_pairs={{0,4},{4,8},{8,12},{12,13},{13,9},{9,5},{5,1},{1,0},{2,6},{6,10},{... | collective-permute-start | bytes 786440 | tf_op jit(solution)/shard_map/ppermute | solution.py:180
  20.3 3.6 %collective-permute-start = (f32[1,128]{1,0:T(1,128)S(1)}, f32[1,128]{1,0:T(1,128)S(1)}, u32[]{:S(2)}, u32[]{:S(2)}) collective-permute-start(f32[1,128]{1,0:T(1,128)S(1)} %convert_element_type.3), channel_id=1, source_target_pairs={{0,4},{4,0},{8,12},{12,8},{1,5},{5,1},{9,13},{13,9},{2,6},{6,2},{1... | collective-permute-start | bytes 1544 | tf_op jit(solution)/shard_map/ppermute | solution.py:185
  23.9 4.5 %collective-permute-start.1 = (f32[2,128]{1,0:T(2,128)S(1)}, f32[2,128]{1,0:T(2,128)S(1)}, u32[]{:S(2)}, u32[]{:S(2)}) collective-permute-start(f32[2,128]{1,0:T(2,128)S(1)} %pad_maximum_fusion.1), channel_id=1, source_target_pairs={{0,8},{4,12},{8,0},{12,4},{1,9},{5,13},{9,1},{13,5},{2,10},{6,14},... | collective-permute-start | bytes 3080 | tf_op jit(solution)/shard_map/ppermute | solution.py:185
  26.5 2.9 %collective-permute-start.5 = (bf16[64,2048]{1,0:T(8,128)(2,1)S(1)}, bf16[64,2048]{1,0:T(8,128)(2,1)S(1)}, u32[]{:S(2)}, u32[]{:S(2)}) collective-permute-start(bf16[64,2048]{1,0:T(8,128)(2,1)S(1)} %collective-permute-done.3.refs_2_), channel_id=1, source_target_pairs={{0,1},{1,0},{2,3},{3,2},{4,5},{5,4},{6,7},{7,6},{8,9},{9,8},{10,11... | collective-permute-start | bytes 786440 | tf_op jit(solution)/shard_map/ppermute | solution.py:181
  28.4 1.5 %collective-permute-start.8 = (bf16[64,2048]{1,0:T(8,128)(2,1)S(1)}, bf16[64,2048]{1,0:T(8,128)(2,1)S(1)}, u32[]{:S(2)}, u32[]{:S(2)}) collective-permute-start(bf16[64,2048]{1,0:T(8,128)(2,1)S(1)} %collective-permute-done.6.refs_5_), channel_id=1, source_target_pairs={{0,1},{1,0},{2,3},{3,2},{4,5},{5,4},{6,7},{7,6},{8,9},{9,8},{10,11... | collective-permute-start | bytes 786440 | tf_op jit(solution)/shard_map/ppermute | solution.py:181
  28.4 1.9 %collective-permute-start.9 = (bf16[64,2048]{1,0:T(8,128)(2,1)S(1)}, bf16[64,2048]{1,0:T(8,128)(2,1)S(1)}, u32[]{:S(2)}, u32[]{:S(2)}) collective-permute-start(bf16[64,2048]{1,0:T(8,128)(2,1)S(1)} %collective-permute-done.7.refs_6_), channel_id=1, source_target_pairs={{0,1},{1,0},{2,3},{3,2},{4,5},{5,4},{6,7},{7,6},{8,9},{9,8},{10,11... | collective-permute-start | bytes 786440 | tf_op jit(solution)/shard_map/ppermute | solution.py:181
  28.9 8.5 %collective-permute-start.12 = (bf16[64,2048]{1,0:T(8,128)(2,1)S(1)}, bf16[64,2048]{1,0:T(8,128)(2,1)S(1)}, u32[]{:S(2)}, u32[]{:S(2)}) collective-permute-start(bf16[64,2048]{1,0:T(8,128)(2,1)S(1)} %collective-permute-done.10.refs_9_), channel_id=1, source_target_pairs={{0,1},{1,0},{2,3},{3,2},{4,5},{5,4},{6,7},{7,6},{8,9},{9,8},{10,11... | collective-permute-start | bytes 786440 | tf_op jit(solution)/shard_map/ppermute | solution.py:181
  29.0 8.4 %collective-permute-start.13 = (bf16[64,2048]{1,0:T(8,128)(2,1)S(1)}, bf16[64,2048]{1,0:T(8,128)(2,1)S(1)}, u32[]{:S(2)}, u32[]{:S(2)}) collective-permute-start(bf16[64,2048]{1,0:T(8,128)(2,1)S(1)} %collective-permute-done.11.refs_10_), channel_id=1, source_target_pairs={{0,1},{1,0},{2,3},{3,2},{4,5},{5,4},{6,7},{7,6},{8,9},{9,8},{10,11... | collective-permute-start | bytes 786440 | tf_op jit(solution)/shard_map/ppermute | solution.py:181
  30.3 1.6 %copy-start = (bf16[1,512,2048]{2,1,0:T(8,128)(2,1)S(1)}, bf16[1,512,2048]{2,1,0:T(8,128)(2,1)}, u32[]{:S(2)}) copy-start(bf16[1,512,2048]{2,1,0:T(8,128)(2,1)} %param.5) | copy-start | bytes 6291460
  31.9 1.0 %copy-start.1 = (bf16[1,128,2048]{2,1,0:T(8,128)(2,1)S(1)}, bf16[1,128,2048]{2,1,0:T(8,128)(2,1)}, u32[]{:S(2)}) copy-start(bf16[1,128,2048]{2,1,0:T(8,128)(2,1)} %param.6) | copy-start | bytes 1572868
  32.9 0.7 %copy-start.2 = (s32[2,2]{1,0:T(2,128)S(1)}, s32[2,2]{1,0:T(2,128)}, u32[]{:S(2)}) copy-start(s32[2,2]{1,0:T(2,128)} %pair_ref.5) | copy-start | bytes 52
  33.6 0.7 %copy-start.3 = (s32[4]{0:T(128)S(1)}, s32[4]{0:T(128)}, u32[]{:S(2)}) copy-start(s32[4]{0:T(128)} %owner_ref.7) | copy-start | bytes 52
  35.0 9.6 %collective-permute-start.14 = (f32[512,128]{1,0:T(8,128)S(1)}, f32[512,128]{1,0:T(8,128)S(1)}, u32[]{:S(2)}, u32[]{:S(2)}) collective-permute-start(f32[512,128]{1,0:T(8,128)S(1)} %shard_map.55), channel_id=1, source_target_pairs={{0,2},{2,0},{1,3},{3,1},{4,6},{6,4},{5,7},{7,5},{8,10},{10,8},{9,1... | collective-permute-start | bytes 786440 | tf_op jit(solution)/shard_map/ppermute | solution.py:205
  39.0 10.2 %collective-permute-start.15 = (f32[512,128]{1,0:T(8,128)S(1)}, f32[512,128]{1,0:T(8,128)S(1)}, u32[]{:S(2)}, u32[]{:S(2)}) collective-permute-start(f32[512,128]{1,0:T(8,128)S(1)} %shard_map.57), channel_id=1, source_target_pairs={{0,2},{2,0},{1,3},{3,1},{4,6},{6,4},{5,7},{7,5},{8,10},{10,8},{9,1... | collective-permute-start | bytes 786440 | tf_op jit(solution)/shard_map/ppermute | solution.py:205

commit v3 on v2

v3 whole, which is shorter than its diff:
```python
import functools

import jax
import jax.numpy as jnp
from jax import lax
from jax.experimental import pallas as pl
from jax.experimental.pallas import tpu as pltpu
from jax.sharding import PartitionSpec as P


CHUNKS = 2
ANY = pl.BlockSpec(memory_space=pl.ANY)
VMEM = pl.BlockSpec(memory_space=pltpu.VMEM)
SMEM = pl.BlockSpec(memory_space=pltpu.SMEM)
LIMIT = 20 * 2**20
STEPS = 32767.0
TAIL = 16


def fold_ring(n):
    order = [2 * z for z in range(n)] + [2 * z + 1 for z in reversed(range(n))]
    return [(order[i], order[(i + 1) % len(order)]) for i in range(len(order))]


def shift(n, by):
    return [(i, (i + by) % n) for i in range(n)]


def xor(n, bit):
    return [(i, i ^ bit) for i in range(n)]


def rank_of(block, z, owned):
    mine = jnp.abs(block - z)
    rank = jnp.int32(0)
    for other in owned:
        far = jnp.abs(other - z)
        nearer = (far < mine) | ((far == mine) & (other < block))
        rank = rank + nearer.astype(jnp.int32)
    return rank


def pick_ranked(owned, z, s):
    block = owned[0]
    for one in owned[1:]:
        block = jnp.where(rank_of(one, z, owned) == s, one, block)
    return block


def scalars(n, nb, cand, refs):
    pairs = [[refs[b * cand + k] for k in range(cand)] for b in range(nb)]
    return pairs, [refs[nb * cand + j] for j in range(n)]


def pick(values, index):
    got = values[0]
    for k in range(1, len(values)):
        got = jnp.where(index == k, values[k], got)
    return got


def listed(pairs, b, block):
    wanted = pairs[b][0] == block
    for one in pairs[b][1:]:
        wanted = wanted | (one == block)
    return wanted


def sources(dists, chunks, refs):
    z = lax.axis_index("blk")
    core = lax.axis_index("qry")
    at = 0
    found = []
    for d in dists:
        directions = (0,) if d == 0 else (-d, d)
        for there in directions:
            found.append((z + jnp.where(core == 0, there, -there), refs[at : at + chunks]))
            at += chunks
    return found


def fetch(block, pool, into, sem):
    for held, refs in pool:

        @pl.when(held == block)
        def _():
            piece = into.shape[0] // len(refs)
            for i, ref in enumerate(refs):
                pltpu.make_async_copy(ref, into.at[pl.ds(i * piece, piece)], sem).start()


def dot_rows(a, b):
    return lax.dot_general(a, b, (((1,), (1,)), ((), ())), preferred_element_type=jnp.float32)


def coded(tile):
    top = jnp.maximum(jnp.max(jnp.abs(tile), axis=0, keepdims=True), 1e-36)
    power = jnp.ceil(jnp.log2(top))
    steps = jnp.clip(jnp.round(tile * jnp.exp2(-power) * STEPS), -STEPS, STEPS)
    return steps.astype(jnp.int32).astype(jnp.int16), power


def decoded(part, b, span, count):
    power = part[pl.ds(count, TAIL), :].astype(jnp.int32).astype(jnp.float32)[b : b + 1]
    steps = part[span, :].astype(jnp.int32).astype(jnp.float32)
    return steps * (jnp.exp2(power) * (1.0 / STEPS))


def load_kernel(q_ref, out):
    out[...] = q_ref[: out.shape[0], : out.shape[1]]


def slot_kernel(sizes, s, dists, chunks, packed, w_ref, q_ref, loaded, *refs):
    n, ckpts, per, nb, cand = sizes
    ins = refs[: -(ckpts - 1) - 2]
    outs = refs[-(ckpts - 1) - 2 : -2]
    rows, sem = refs[-2:]
    z, c = lax.axis_index("blk"), lax.axis_index("ckpt")
    pairs, order = scalars(n, nb, cand, packed)
    count = q_ref.shape[0]
    qblk, width = count // nb, rows.shape[0]
    pool = sources(dists, chunks, ins)
    for r in range(1, ckpts):
        owner = lax.rem(c + r, ckpts)
        owned = [pick(order[k::per], owner) for k in range(per)]
        block = pick_ranked(owned, z, s)
        fetch(block, pool, rows, sem)
        pltpu.make_async_copy(rows, rows, sem).wait()
        weight = w_ref[pl.ds(block ^ z, 1), :]
        out = outs[r - 1]
        out[pl.ds(count, TAIL), :] = jnp.zeros((TAIL, width), jnp.int16)
        for b in range(nb):
            span = pl.ds(b * qblk, qblk)
            wanted = listed(pairs, b, block)

            @pl.when(wanted)
            def _():
                steps, power = coded(dot_rows(q_ref[span, :], rows[...]) * weight)
                out[span, :] = steps
                line = lax.broadcasted_iota(jnp.int32, (TAIL, width), 0)
                old = out[pl.ds(count, TAIL), :].astype(jnp.int32)
                out[pl.ds(count, TAIL), :] = jnp.where(line == b, power.astype(jnp.int32), old).astype(jnp.int16)

            @pl.when(jnp.logical_not(wanted))
            def _():
                out[span, :] = jnp.zeros((qblk, width), jnp.int16)


def own_kernel(sizes, dists, chunks, packed, w_ref, q_ref, *refs):
    n, ckpts, per, nb, cand = sizes
    early = (per - 1) * (ckpts - 1)
    ins, came = refs[: len(refs) - early - 5], refs[len(refs) - early - 5 : -5]
    out, last, rows, tiles, sems = refs[-5:]
    z, c = lax.axis_index("blk"), lax.axis_index("ckpt")
    pairs, order = scalars(n, nb, cand, packed)
    count = q_ref.shape[0]
    qblk, width = count // nb, rows.shape[1]
    pool = sources(dists, chunks, ins)
    owned = [pick(order[k::per], c) for k in range(per)]
    ranked = [pick_ranked(owned, z, s) for s in range(per)]
    for s, block in enumerate(ranked):
        fetch(block, pool, rows.at[s], sems.at[s])
    for s, block in enumerate(ranked):
        pltpu.make_async_copy(rows.at[s], rows.at[s], sems.at[s]).wait()
        weight = w_ref[pl.ds(block ^ z, 1), :]
        into = last if s == per - 1 else tiles.at[s]
        for b in range(nb):
            span = pl.ds(b * qblk, qblk)
            wanted = listed(pairs, b, block)

            @pl.when(wanted)
            def _():
                total = dot_rows(q_ref[span, :], rows[s]) * weight
                if s < per - 1:
                    for r in range(ckpts - 1):
                        total = total + decoded(came[s * (ckpts - 1) + r], b, span, count)
                into[span, :] = total

            @pl.when(jnp.logical_not(wanted))
            def _():
                into[span, :] = jnp.zeros((qblk, width), jnp.float32)

        if s < per - 1:
            put_columns(tiles.at[s], out, owned, block, sems.at[s]).start()
    for s, block in enumerate(ranked[:-1]):
        put_columns(tiles.at[s], out, owned, block, sems.at[s]).wait()


def put_columns(tile, out, owned, block, sem):
    width = tile.shape[1]
    slot = jnp.int32(0)
    for j, one in enumerate(owned):
        slot = jnp.where(one == block, j, slot)
    return pltpu.make_async_copy(tile, out.at[:, pl.ds(pl.multiple_of(slot * width, width), width)], sem)


def sum_kernel(sizes, packed, acc_ref, last_ref, *refs):
    n, _, per, nb, cand = sizes
    came, out, tile, sem = refs[:-3], refs[-3], refs[-2], refs[-1]
    z, c = lax.axis_index("blk"), lax.axis_index("ckpt")
    _, order = scalars(n, nb, cand, packed)
    count = last_ref.shape[0]
    qblk = count // nb
    owned = [pick(order[k::per], c) for k in range(per)]
    block = pick_ranked(owned, z, per - 1)
    for b in range(nb):
        span = pl.ds(b * qblk, qblk)
        total = last_ref[span, :]
        for part in came:
            total = total + decoded(part, b, span, count)
        tile[span, :] = total
    store = put_columns(tile, out, owned, block, sem)
    store.start()
    store.wait()


def per_device(query_feats, train_feats, loss_weights, pair_list, tile_owner):
    queries, own_rows = query_feats[0], train_feats[0]
    n, ckpts = lax.axis_size("blk"), lax.axis_size("ckpt")
    per = n // ckpts
    rows, feats = own_rows.shape
    count = queries.shape[0]
    lines = ("blk", "qry")
    ring, swap = fold_ring(n), shift(2, 1)
    chunks, piece = CHUNKS, rows // CHUNKS

    params = pltpu.CompilerParams(vmem_limit_bytes=LIMIT)
    nb, cand = pair_list.shape
    sizes = (n, ckpts, per, nb, cand)
    held = [own_rows[i * piece : (i + 1) * piece] for i in range(chunks)]
    loaded = pl.pallas_call(
        load_kernel,
        out_shape=jax.ShapeDtypeStruct((8, rows), queries.dtype),
        in_specs=[VMEM],
        out_specs=VMEM,
        compiler_params=params,
    )(queries)
    packed = jnp.concatenate([pair_list.reshape(nb * cand), tile_owner])
    near = {0: held}
    weights = loss_weights
    for step in range(1, n):
        held = [lax.ppermute(part, lines, ring) for part in held]
        near[step] = held + [lax.ppermute(part, "qry", swap) for part in held]
    bit = 1
    while bit < n:
        weights = jnp.concatenate([weights, lax.ppermute(weights, "blk", xor(n, bit))], axis=0)
        bit *= 2
    weights = weights.astype(jnp.float32)

    sent = jax.ShapeDtypeStruct((count + TAIL, rows), jnp.int16)
    tile = jax.ShapeDtypeStruct((count, rows), jnp.float32)
    acc = jax.ShapeDtypeStruct((count, per * rows), jnp.float32)
    flops = 2 * count * rows * feats
    came = []
    for s in range(per):
        dists = tuple(range(n - per + s + 1))
        pool = [ref for d in dists for ref in near[d]]
        terms = pl.pallas_call(
            functools.partial(slot_kernel, sizes, s, dists, chunks),
            out_shape=[sent] * (ckpts - 1),
            in_specs=[SMEM, VMEM, VMEM, ANY] + [ANY] * len(pool),
            out_specs=[VMEM] * (ckpts - 1),
            scratch_shapes=[pltpu.VMEM((rows, feats), jnp.bfloat16), pltpu.SemaphoreType.DMA],
            compiler_params=params,
            cost_estimate=pl.CostEstimate(flops=flops * (ckpts - 1), bytes_accessed=count * feats * 2, transcendentals=0),
        )(packed, weights, queries, loaded, *pool)
        came.append([lax.ppermute(terms[r - 1], "ckpt", shift(ckpts, r)) for r in range(1, ckpts)])
    early = [part for parts in came[:-1] for part in parts]
    total, last = pl.pallas_call(
        functools.partial(own_kernel, sizes, dists, chunks),
        out_shape=[acc, tile],
        in_specs=[SMEM, VMEM, VMEM] + [ANY] * len(pool) + [VMEM] * len(early),
        out_specs=[ANY, VMEM],
        scratch_shapes=[
            pltpu.VMEM((per, rows, feats), jnp.bfloat16),
            pltpu.VMEM((max(per - 1, 1), count, rows), jnp.float32),
            pltpu.SemaphoreType.DMA((per,)),
        ],
        compiler_params=params,
        cost_estimate=pl.CostEstimate(flops=flops * per, bytes_accessed=count * feats * 2, transcendentals=0),
    )(packed, weights, queries, *pool, *early)
    return pl.pallas_call(
        functools.partial(sum_kernel, sizes),
        out_shape=acc,
        in_specs=[SMEM, ANY, VMEM] + [VMEM] * (ckpts - 1),
        out_specs=ANY,
        input_output_aliases={1: 0},
        scratch_shapes=[pltpu.VMEM((count, rows), jnp.float32), pltpu.SemaphoreType.DMA],
        compiler_params=params,
    )(packed, total, last, *came[-1])


def solution(mesh):
    return jax.shard_map(
        per_device,
        mesh=mesh,
        in_specs=(
            P("ckpt", ("shard", "blk", "qry"), None),
            P("ckpt", ("shard", "blk"), None),
            P("ckpt", ("shard", "blk")),
            P(("shard", "blk", "qry"), None),
            P("shard"),
        ),
        out_specs=P(("shard", "blk", "qry"), "ckpt"),
        check_vma=False,
    )
```

time: 51.8 us -> 43.7 us (0.84)
  waiting for transfers between devices: 16.4 us -> 10.9 us
  local copies, waits for them, and re-layouts: 5.03 us -> 3.45 us
  Pallas kernels: 6.99 us -> 5.94 us
    ppermute x2, waiting for transfers between devices: 7.64 us -> 2.66 us  [per_device(): lax.ppermute(terms[r - 1], 'ckpt', shift(ckpts, r))]
    unnamed x8 -> x6, local copies, waits for them, and re-layouts: 3.97 us -> 1.6 us
    pallas_call x4 -> x5, Pallas kernels: 6.99 us -> 5.94 us  [the longest x1 2.33 us: per_device(): pl.pallas_call(functools.partial(own_kernel, sizes, dists, chunks), out_s...]
    ppermute x6, waiting for transfers between devices: 0.87 us -> 0.02 us  [per_device(): near[step] = held + [lax.ppermute(part, 'qry', swap) for part in held]]
    reshape x0 -> x1, local copies, waits for them, and re-layouts: none -> 0.76 us  [per_device(): packed = jnp.concatenate([pair_list.reshape(nb * cand), tile_owner])]
    convert_element_type x1, other arithmetic: 0.66 us -> 0.01 us  [per_device(): weights = weights.astype(jnp.float32)]
    concatenate x2 -> x1, other arithmetic: 0.02 us -> 0.66 us  [per_device(): jnp.concatenate([weights, lax.ppermute(weights, 'blk', xor(n, bit))], axi...]
  transfers between devices with their start and end apart: 16 -> 16, of which waited for: 10 -> 8; matrix products, arithmetic and copies ran while one was open for 1% -> 3% of each run, Pallas kernels for 9% -> 11%
where the time goes in v3:
time: 43.7 us; the launch traced here: 43.5 us
  starting transfers between devices  22.4 us (51%)
  waiting for transfers between devices  10.9 us (25%)
  Pallas kernels  5.94 us (14%)
  local copies, waits for them, and re-layouts  3.45 us (8%)
  other arithmetic  0.75 us (2%)
    ppermute x6, starting transfers between devices, per_device(): held = [lax.ppermute(part, lines, ring) for part in held]  14.6 us
    ppermute x2, starting transfers between devices, per_device(): lax.ppermute(weights, 'blk', xor(n, bit))  4.21 us
    ppermute x2, waiting for transfers between devices, per_device(): lax.ppermute(weights, 'blk', xor(n, bit))  4.18 us
    ppermute x6, waiting for transfers between devices, per_device(): held = [lax.ppermute(part, lines, ring) for part in held]  4.05 us
    ppermute x2, waiting for transfers between devices, per_device(): lax.ppermute(terms[r - 1], 'ckpt', shift(ckpts, r))  2.66 us
    ppermute x2, starting transfers between devices, per_device(): lax.ppermute(terms[r - 1], 'ckpt', shift(ckpts, r))  2.58 us
    pallas_call x1, Pallas kernels, per_device(): pl.pallas_call(functools.partial(own_kernel, sizes, dists, chunks), out_s...  2.33 us
    pallas_call x2, Pallas kernels, per_device(): pl.pallas_call(functools.partial(slot_kernel, sizes, s, dists, chunks), o...  2.32 us
  transfers between devices with their start and end apart: 16, of which 8 were waited for; matrix products, arithmetic and copies ran while one was open for 3% of the time, Pallas kernels for 11%

profile of v3, /device:TPU:0, one launch (start us, length us, event | category | flops | bytes accessed | tf_op | source)
XLA Modules:
  0.0 43.5 jit_solution(16778685032440973418)
XLA Ops:
  0.0 1.1 %slice_bitcast_fusion = (bf16[64,2048]{1,0:T(8,128)(2,1)S(1)}, bf16[64,2048]{1,0:T(8,128)(2,1)S(1)}) fusion(bf16[1,128,2048]{2,1,0:T(8,128)(2,1)} %param.6), kind=kLoop, calls=%fused_computation | loop fusion | bytes 1048576 | tf_op jit(solution)/shard_map/slice | solution.py:230
  1.1 3.1 %collective-permute-start.2 = (bf16[64,2048]{1,0:T(8,128)(2,1)S(1)}, bf16[64,2048]{1,0:T(8,128)(2,1)S(1)}, u32[]{:S(2)}, u32[]{:S(2)}) collective-permute-start(bf16[64,2048]{1,0:T(8,128)(2,1)S(1)} %get-tuple-element.10.refs_0_), channel_id=1, source_target_pairs={{0,4},{4,8},{8,12},{12,13},{13,9},{9,5},{5,1},{1,0},{2,6},{6,10},{... | collective-permute-start | bytes 786440 | tf_op jit(solution)/shard_map/ppermute | solution.py:242
  4.2 1.6 %collective-permute-start.3 = (bf16[64,2048]{1,0:T(8,128)(2,1)S(1)}, bf16[64,2048]{1,0:T(8,128)(2,1)S(1)}, u32[]{:S(2)}, u32[]{:S(2)}) collective-permute-start(bf16[64,2048]{1,0:T(8,128)(2,1)S(1)} %get-tuple-element.9.refs_1_), channel_id=1, source_target_pairs={{0,4},{4,8},{8,12},{12,13},{13,9},{9,5},{5,1},{1,0},{2,6},{6,10},{... | collective-permute-start | bytes 786440 | tf_op jit(solution)/shard_map/ppermute | solution.py:242
  5.7 2.3 %collective-permute-done.2.refs_2_ = bf16[64,2048]{1,0:T(8,128)(2,1)S(1)} collective-permute-done((bf16[64,2048]{1,0:T(8,128)(2,1)S(1)}, bf16[64,2048]{1,0:T(8,128)(2,1)S(1)}, u32[]{:S(2)}, u32[]{:S(2)}) %collective-permute-start.2) | collective-permute-done | bytes 262176 | tf_op jit(solution)/shard_map/ppermute | solution.py:242
  8.1 2.5 %collective-permute-start.6 = (bf16[64,2048]{1,0:T(8,128)(2,1)S(1)}, bf16[64,2048]{1,0:T(8,128)(2,1)S(1)}, u32[]{:S(2)}, u32[]{:S(2)}) collective-permute-start(bf16[64,2048]{1,0:T(8,128)(2,1)S(1)} %collective-permute-done.2.refs_2_), channel_id=1, source_target_pairs={{0,4},{4,8},{8,12},{12,13},{13,9},{9,5},{5,1},{1,0},{2,6},{6,10},{... | collective-permute-start | bytes 786440 | tf_op jit(solution)/shard_map/ppermute | solution.py:242
  10.9 2.5 %collective-permute-start.7 = (bf16[64,2048]{1,0:T(8,128)(2,1)S(1)}, bf16[64,2048]{1,0:T(8,128)(2,1)S(1)}, u32[]{:S(2)}, u32[]{:S(2)}) collective-permute-start(bf16[64,2048]{1,0:T(8,128)(2,1)S(1)} %collective-permute-done.3.refs_3_), channel_id=1, source_target_pairs={{0,4},{4,8},{8,12},{12,13},{13,9},{9,5},{5,1},{1,0},{2,6},{6,10},{... | collective-permute-start | bytes 786440 | tf_op jit(solution)/shard_map/ppermute | solution.py:242
  13.4 1.1 %collective-permute-done.6.refs_6_ = bf16[64,2048]{1,0:T(8,128)(2,1)S(1)} collective-permute-done((bf16[64,2048]{1,0:T(8,128)(2,1)S(1)}, bf16[64,2048]{1,0:T(8,128)(2,1)S(1)}, u32[]{:S(2)}, u32[]{:S(2)}) %collective-permute-start.6) | collective-permute-done | bytes 262176 | tf_op jit(solution)/shard_map/ppermute | solution.py:242
  14.4 2.5 %collective-permute-start.10 = (bf16[64,2048]{1,0:T(8,128)(2,1)S(1)}, bf16[64,2048]{1,0:T(8,128)(2,1)S(1)}, u32[]{:S(2)}, u32[]{:S(2)}) collective-permute-start(bf16[64,2048]{1,0:T(8,128)(2,1)S(1)} %collective-permute-done.6.refs_6_), channel_id=1, source_target_pairs={{0,4},{4,8},{8,12},{12,13},{13,9},{9,5},{5,1},{1,0},{2,6},{6,10},{... | collective-permute-start | bytes 786440 | tf_op jit(solution)/shard_map/ppermute | solution.py:242
  17.2 2.5 %collective-permute-start.11 = (bf16[64,2048]{1,0:T(8,128)(2,1)S(1)}, bf16[64,2048]{1,0:T(8,128)(2,1)S(1)}, u32[]{:S(2)}, u32[]{:S(2)}) collective-permute-start(bf16[64,2048]{1,0:T(8,128)(2,1)S(1)} %collective-permute-done.7.refs_7_), channel_id=1, source_target_pairs={{0,4},{4,8},{8,12},{12,13},{13,9},{9,5},{5,1},{1,0},{2,6},{6,10},{... | collective-permute-start | bytes 786440 | tf_op jit(solution)/shard_map/ppermute | solution.py:242
  19.7 1.6 %collective-permute-start = (bf16[1,128]{1,0:T(2,128)(2,1)}, bf16[1,128]{1,0:T(2,128)(2,1)S(1)}, u32[]{:S(2)}, u32[]{:S(2)}) collective-permute-start(bf16[1,128]{1,0:T(2,128)(2,1)} %param.7), channel_id=1, source_target_pairs={{0,4},{4,0},{8,12},{12,8},{1,5},{5,1},{9,13},{13,9},{2,6},{6,2},{1... | collective-permute-start | bytes 776 | tf_op jit(solution)/shard_map/ppermute | solution.py:246
  21.3 2.4 %collective-permute-done = bf16[1,128]{1,0:T(2,128)(2,1)S(1)} collective-permute-done((bf16[1,128]{1,0:T(2,128)(2,1)}, bf16[1,128]{1,0:T(2,128)(2,1)S(1)}, u32[]{:S(2)}, u32[]{:S(2)}) %collective-permute-start) | collective-permute-done | bytes 288 | tf_op jit(solution)/shard_map/ppermute | solution.py:246
  23.7 0.7 %pad_maximum_fusion = bf16[2,128]{1,0:T(2,128)(2,1)S(1)} fusion(bf16[1,128]{1,0:T(2,128)(2,1)S(1)} %collective-permute-done, bf16[1,128]{1,0:T(2,128)(2,1)} %param.7), kind=kLoop, calls=%fused_computation.4 | loop fusion | flops 1024 | bytes 1024 | tf_op jit(solution)/shard_map/concatenate | solution.py:246
  24.3 2.6 %collective-permute-start.1 = (bf16[2,128]{1,0:T(2,128)(2,1)S(1)}, bf16[2,128]{1,0:T(2,128)(2,1)S(1)}, u32[]{:S(2)}, u32[]{:S(2)}) collective-permute-start(bf16[2,128]{1,0:T(2,128)(2,1)S(1)} %pad_maximum_fusion), channel_id=1, source_target_pairs={{0,8},{4,12},{8,0},{12,4},{1,9},{5,13},{9,1},{13,5},{2,10},{6,14},... | collective-permute-start | bytes 1544 | tf_op jit(solution)/shard_map/ppermute | solution.py:246
  27.0 1.8 %collective-permute-done.1 = bf16[2,128]{1,0:T(2,128)(2,1)S(1)} collective-permute-done((bf16[2,128]{1,0:T(2,128)(2,1)S(1)}, bf16[2,128]{1,0:T(2,128)(2,1)S(1)}, u32[]{:S(2)}, u32[]{:S(2)}) %collective-permute-start.1) | collective-permute-done | bytes 544 | tf_op jit(solution)/shard_map/ppermute | solution.py:246
  28.8 0.5 %collective-permute-start.9 = (bf16[64,2048]{1,0:T(8,128)(2,1)S(1)}, bf16[64,2048]{1,0:T(8,128)(2,1)S(1)}, u32[]{:S(2)}, u32[]{:S(2)}) collective-permute-start(bf16[64,2048]{1,0:T(8,128)(2,1)S(1)} %collective-permute-done.7.refs_7_), channel_id=1, source_target_pairs={{0,1},{1,0},{2,3},{3,2},{4,5},{5,4},{6,7},{7,6},{8,9},{9,8},{10,11... | collective-permute-start | bytes 786440 | tf_op jit(solution)/shard_map/ppermute | solution.py:243
  29.3 0.8 %reshape.5 = s32[4]{0:T(128)S(1)} reshape(s32[2,2]{1,0:T(2,128)} %param.8) | data formatting | bytes 32 | tf_op jit(solution)/shard_map/reshape | solution.py:238
  30.1 1.6 %copy-done = bf16[1,512,2048]{2,1,0:T(8,128)(2,1)S(1)} copy-done((bf16[1,512,2048]{2,1,0:T(8,128)(2,1)S(1)}, bf16[1,512,2048]{2,1,0:T(8,128)(2,1)}, u32[]{:S(2)}) %copy-start) | copy-done | bytes 2097176
  32.3 0.7 %shard_map.56 = s16[528,128]{1,0:T(8,128)(2,1)S(1)} custom-call(s32[8]{0:T(128)S(1)} %pad_add_fusion.packed, f32[4,128]{1,0:T(4,128)S(1)} %maximum_convert_fusion.w_ref, bf16[512,2048]{1,0:T(8,128)(2,1)S(1)} %bitcast.6, bf16[8,128]{1,0:T(8,128)(2,1)S(1)} %shard_map.55.loaded, bf16[64,2048]{1,0:T(8,128)(2,1)S(1)} %get-tuple-element.10.refs_0_, ...), custom_call_target="tpu_custom_call" | custom-call | flops 268435456 | bytes 2097152 | tf_op jit(solution)/shard_map/pallas_call | solution.py:258
  33.0 2.5 %collective-permute-start.14 = (s16[528,128]{1,0:T(8,128)(2,1)S(1)}, s16[528,128]{1,0:T(8,128)(2,1)S(1)}, u32[]{:S(2)}, u32[]{:S(2)}) collective-permute-start(s16[528,128]{1,0:T(8,128)(2,1)S(1)} %shard_map.56), channel_id=1, source_target_pairs={{0,2},{2,0},{1,3},{3,1},{4,6},{6,4},{5,7},{7,5},{8,10},{10,8},{9,1... | collective-permute-start | bytes 405512 | tf_op jit(solution)/shard_map/ppermute | solution.py:267
  35.5 1.6 %shard_map.58 = s16[528,128]{1,0:T(8,128)(2,1)S(1)} custom-call(s32[8]{0:T(128)S(1)} %pad_add_fusion.packed, f32[4,128]{1,0:T(4,128)S(1)} %maximum_convert_fusion.w_ref, bf16[512,2048]{1,0:T(8,128)(2,1)S(1)} %bitcast.7, bf16[8,128]{1,0:T(8,128)(2,1)S(1)} %shard_map.55.loaded, bf16[64,2048]{1,0:T(8,128)(2,1)S(1)} %get-tuple-element.10.refs_0_, ...), custom_call_target="tpu_custom_call" | custom-call | flops 268435456 | bytes 2097152 | tf_op jit(solution)/shard_map/pallas_call | solution.py:258
  37.2 2.0 %collective-permute-done.14.refs_14_ = s16[528,128]{1,0:T(8,128)(2,1)S(1)} collective-permute-done((s16[528,128]{1,0:T(8,128)(2,1)S(1)}, s16[528,128]{1,0:T(8,128)(2,1)S(1)}, u32[]{:S(2)}, u32[]{:S(2)}) %collective-permute-start.14) | collective-permute-done | bytes 135200 | tf_op jit(solution)/shard_map/ppermute | solution.py:267
  39.2 2.3 %shard_map.57 = (f32[512,256]{1,0:T(8,128)}, f32[512,128]{1,0:T(8,128)S(1)}) custom-call(s32[8]{0:T(128)S(1)} %pad_add_fusion.packed, f32[4,128]{1,0:T(4,128)S(1)} %maximum_convert_fusion.w_ref, bf16[512,2048]{1,0:T(8,128)(2,1)S(1)} %bitcast.8, bf16[64,2048]{1,0:T(8,128)(2,1)S(1)} %get-tuple-element.10.refs_0_, ...), custom_call_target="tpu_custom_call" | custom-call | flops 536870912 | bytes 2097152 | tf_op jit(solution)/shard_map/pallas_call | solution.py:269
  41.5 0.7 %collective-permute-done.15.refs_0_ = s16[528,128]{1,0:T(8,128)(2,1)S(1)} collective-permute-done((s16[528,128]{1,0:T(8,128)(2,1)S(1)}, s16[528,128]{1,0:T(8,128)(2,1)S(1)}, u32[]{:S(2)}, u32[]{:S(2)}) %collective-permute-start.15) | collective-permute-done | bytes 135200 | tf_op jit(solution)/shard_map/ppermute | solution.py:267
  42.2 1.3 %shard_map.59 = f32[512,256]{1,0:T(8,128)} custom-call(s32[8]{0:T(128)S(1)} %pad_add_fusion.packed, f32[512,256]{1,0:T(8,128)} %get-tuple-element.7.acc_ref, f32[512,128]{1,0:T(8,128)S(1)} %get-tuple-element.8.last_ref, s16[528,128]{1,0:T(8,128)(2,1)S(1)} %collective-permute-done.15.refs_0_), custom_call_target="tpu_custom_call", output_to_operand_aliasing={{}: (1, {})} | custom-call | tf_op jit(solution)/shard_map/pallas_call | solution.py:282
  (24 shorter events, 1.4 us)
Async XLA Ops:
  0.0 32.3 %copy-start.1 = (bf16[1,128]{1,0:T(2,128)(2,1)S(1)}, bf16[1,128]{1,0:T(2,128)(2,1)}, u32[]{:S(2)}) copy-start(bf16[1,128]{1,0:T(2,128)(2,1)} %param.7) | copy-start | bytes 772
  0.0 32.2 %copy-start.2 = (s32[4]{0:T(128)S(1)}, s32[4]{0:T(128)}, u32[]{:S(2)}) copy-start(s32[4]{0:T(128)} %param.9) | copy-start | bytes 52
  1.1 7.0 %collective-permute-start.2 = (bf16[64,2048]{1,0:T(8,128)(2,1)S(1)}, bf16[64,2048]{1,0:T(8,128)(2,1)S(1)}, u32[]{:S(2)}, u32[]{:S(2)}) collective-permute-start(bf16[64,2048]{1,0:T(8,128)(2,1)S(1)} %get-tuple-element.10.refs_0_), channel_id=1, source_target_pairs={{0,4},{4,8},{8,12},{12,13},{13,9},{9,5},{5,1},{1,0},{2,6},{6,10},{... | collective-permute-start | bytes 786440 | tf_op jit(solution)/shard_map/ppermute | solution.py:242
  4.2 6.7 %collective-permute-start.3 = (bf16[64,2048]{1,0:T(8,128)(2,1)S(1)}, bf16[64,2048]{1,0:T(8,128)(2,1)S(1)}, u32[]{:S(2)}, u32[]{:S(2)}) collective-permute-start(bf16[64,2048]{1,0:T(8,128)(2,1)S(1)} %get-tuple-element.9.refs_1_), channel_id=1, source_target_pairs={{0,4},{4,8},{8,12},{12,13},{13,9},{9,5},{5,1},{1,0},{2,6},{6,10},{... | collective-permute-start | bytes 786440 | tf_op jit(solution)/shard_map/ppermute | solution.py:242
  8.1 6.4 %collective-permute-start.6 = (bf16[64,2048]{1,0:T(8,128)(2,1)S(1)}, bf16[64,2048]{1,0:T(8,128)(2,1)S(1)}, u32[]{:S(2)}, u32[]{:S(2)}) collective-permute-start(bf16[64,2048]{1,0:T(8,128)(2,1)S(1)} %collective-permute-done.2.refs_2_), channel_id=1, source_target_pairs={{0,4},{4,8},{8,12},{12,13},{13,9},{9,5},{5,1},{1,0},{2,6},{6,10},{... | collective-permute-start | bytes 786440 | tf_op jit(solution)/shard_map/ppermute | solution.py:242
  10.9 6.4 %collective-permute-start.7 = (bf16[64,2048]{1,0:T(8,128)(2,1)S(1)}, bf16[64,2048]{1,0:T(8,128)(2,1)S(1)}, u32[]{:S(2)}, u32[]{:S(2)}) collective-permute-start(bf16[64,2048]{1,0:T(8,128)(2,1)S(1)} %collective-permute-done.3.refs_3_), channel_id=1, source_target_pairs={{0,4},{4,8},{8,12},{12,13},{13,9},{9,5},{5,1},{1,0},{2,6},{6,10},{... | collective-permute-start | bytes 786440 | tf_op jit(solution)/shard_map/ppermute | solution.py:242
  13.3 15.4 %collective-permute-start.4 = (bf16[64,2048]{1,0:T(8,128)(2,1)S(1)}, bf16[64,2048]{1,0:T(8,128)(2,1)S(1)}, u32[]{:S(2)}, u32[]{:S(2)}) collective-permute-start(bf16[64,2048]{1,0:T(8,128)(2,1)S(1)} %collective-permute-done.2.refs_2_), channel_id=1, source_target_pairs={{0,1},{1,0},{2,3},{3,2},{4,5},{5,4},{6,7},{7,6},{8,9},{9,8},{10,11... | collective-permute-start | bytes 786440 | tf_op jit(solution)/shard_map/ppermute | solution.py:243
  14.4 17.2 %collective-permute-start.10 = (bf16[64,2048]{1,0:T(8,128)(2,1)S(1)}, bf16[64,2048]{1,0:T(8,128)(2,1)S(1)}, u32[]{:S(2)}, u32[]{:S(2)}) collective-permute-start(bf16[64,2048]{1,0:T(8,128)(2,1)S(1)} %collective-permute-done.6.refs_6_), channel_id=1, source_target_pairs={{0,4},{4,8},{8,12},{12,13},{13,9},{9,5},{5,1},{1,0},{2,6},{6,10},{... | collective-permute-start | bytes 786440 | tf_op jit(solution)/shard_map/ppermute | solution.py:242
  17.2 14.4 %collective-permute-start.11 = (bf16[64,2048]{1,0:T(8,128)(2,1)S(1)}, bf16[64,2048]{1,0:T(8,128)(2,1)S(1)}, u32[]{:S(2)}, u32[]{:S(2)}) collective-permute-start(bf16[64,2048]{1,0:T(8,128)(2,1)S(1)} %collective-permute-done.7.refs_7_), channel_id=1, source_target_pairs={{0,4},{4,8},{8,12},{12,13},{13,9},{9,5},{5,1},{1,0},{2,6},{6,10},{... | collective-permute-start | bytes 786440 | tf_op jit(solution)/shard_map/ppermute | solution.py:242
  19.7 3.9 %collective-permute-start = (bf16[1,128]{1,0:T(2,128)(2,1)}, bf16[1,128]{1,0:T(2,128)(2,1)S(1)}, u32[]{:S(2)}, u32[]{:S(2)}) collective-permute-start(bf16[1,128]{1,0:T(2,128)(2,1)} %param.7), channel_id=1, source_target_pairs={{0,4},{4,0},{8,12},{12,8},{1,5},{5,1},{9,13},{13,9},{2,6},{6,2},{1... | collective-permute-start | bytes 776 | tf_op jit(solution)/shard_map/ppermute | solution.py:246
  24.3 4.5 %collective-permute-start.1 = (bf16[2,128]{1,0:T(2,128)(2,1)S(1)}, bf16[2,128]{1,0:T(2,128)(2,1)S(1)}, u32[]{:S(2)}, u32[]{:S(2)}) collective-permute-start(bf16[2,128]{1,0:T(2,128)(2,1)S(1)} %pad_maximum_fusion), channel_id=1, source_target_pairs={{0,8},{4,12},{8,0},{12,4},{1,9},{5,13},{9,1},{13,5},{2,10},{6,14},... | collective-permute-start | bytes 1544 | tf_op jit(solution)/shard_map/ppermute | solution.py:246
  27.0 5.3 %collective-permute-start.5 = (bf16[64,2048]{1,0:T(8,128)(2,1)S(1)}, bf16[64,2048]{1,0:T(8,128)(2,1)S(1)}, u32[]{:S(2)}, u32[]{:S(2)}) collective-permute-start(bf16[64,2048]{1,0:T(8,128)(2,1)S(1)} %collective-permute-done.3.refs_3_), channel_id=1, source_target_pairs={{0,1},{1,0},{2,3},{3,2},{4,5},{5,4},{6,7},{7,6},{8,9},{9,8},{10,11... | collective-permute-start | bytes 786440 | tf_op jit(solution)/shard_map/ppermute | solution.py:243
  28.8 3.5 %collective-permute-start.8 = (bf16[64,2048]{1,0:T(8,128)(2,1)S(1)}, bf16[64,2048]{1,0:T(8,128)(2,1)S(1)}, u32[]{:S(2)}, u32[]{:S(2)}) collective-permute-start(bf16[64,2048]{1,0:T(8,128)(2,1)S(1)} %collective-permute-done.6.refs_6_), channel_id=1, source_target_pairs={{0,1},{1,0},{2,3},{3,2},{4,5},{5,4},{6,7},{7,6},{8,9},{9,8},{10,11... | collective-permute-start | bytes 786440 | tf_op jit(solution)/shard_map/ppermute | solution.py:243
  28.8 3.5 %collective-permute-start.9 = (bf16[64,2048]{1,0:T(8,128)(2,1)S(1)}, bf16[64,2048]{1,0:T(8,128)(2,1)S(1)}, u32[]{:S(2)}, u32[]{:S(2)}) collective-permute-start(bf16[64,2048]{1,0:T(8,128)(2,1)S(1)} %collective-permute-done.7.refs_7_), channel_id=1, source_target_pairs={{0,1},{1,0},{2,3},{3,2},{4,5},{5,4},{6,7},{7,6},{8,9},{9,8},{10,11... | collective-permute-start | bytes 786440 | tf_op jit(solution)/shard_map/ppermute | solution.py:243
  30.1 1.6 %copy-start = (bf16[1,512,2048]{2,1,0:T(8,128)(2,1)S(1)}, bf16[1,512,2048]{2,1,0:T(8,128)(2,1)}, u32[]{:S(2)}) copy-start(bf16[1,512,2048]{2,1,0:T(8,128)(2,1)} %param.5) | copy-start | bytes 6291460
  31.7 3.8 %collective-permute-start.12 = (bf16[64,2048]{1,0:T(8,128)(2,1)S(1)}, bf16[64,2048]{1,0:T(8,128)(2,1)S(1)}, u32[]{:S(2)}, u32[]{:S(2)}) collective-permute-start(bf16[64,2048]{1,0:T(8,128)(2,1)S(1)} %collective-permute-done.10.refs_10_), channel_id=1, source_target_pairs={{0,1},{1,0},{2,3},{3,2},{4,5},{5,4},{6,7},{7,6},{8,9},{9,8},{10,11... | collective-permute-start | bytes 786440 | tf_op jit(solution)/shard_map/ppermute | solution.py:243
  31.7 3.8 %collective-permute-start.13 = (bf16[64,2048]{1,0:T(8,128)(2,1)S(1)}, bf16[64,2048]{1,0:T(8,128)(2,1)S(1)}, u32[]{:S(2)}, u32[]{:S(2)}) collective-permute-start(bf16[64,2048]{1,0:T(8,128)(2,1)S(1)} %collective-permute-done.11.refs_11_), channel_id=1, source_target_pairs={{0,1},{1,0},{2,3},{3,2},{4,5},{5,4},{6,7},{7,6},{8,9},{9,8},{10,11... | collective-permute-start | bytes 786440 | tf_op jit(solution)/shard_map/ppermute | solution.py:243
  33.0 6.2 %collective-permute-start.14 = (s16[528,128]{1,0:T(8,128)(2,1)S(1)}, s16[528,128]{1,0:T(8,128)(2,1)S(1)}, u32[]{:S(2)}, u32[]{:S(2)}) collective-permute-start(s16[528,128]{1,0:T(8,128)(2,1)S(1)} %shard_map.56), channel_id=1, source_target_pairs={{0,2},{2,0},{1,3},{3,1},{4,6},{6,4},{5,7},{7,5},{8,10},{10,8},{9,1... | collective-permute-start | bytes 405512 | tf_op jit(solution)/shard_map/ppermute | solution.py:267
  37.2 5.1 %collective-permute-start.15 = (s16[528,128]{1,0:T(8,128)(2,1)S(1)}, s16[528,128]{1,0:T(8,128)(2,1)S(1)}, u32[]{:S(2)}, u32[]{:S(2)}) collective-permute-start(s16[528,128]{1,0:T(8,128)(2,1)S(1)} %shard_map.58), channel_id=1, source_target_pairs={{0,2},{2,0},{1,3},{3,1},{4,6},{6,4},{5,7},{7,5},{8,10},{10,8},{9,1... | collective-permute-start | bytes 405512 | tf_op jit(solution)/shard_map/ppermute | solution.py:267

commit v4 on v3

v4 whole, which is shorter than its diff:
```python
import functools

import jax
import jax.numpy as jnp
from jax import lax
from jax.experimental import pallas as pl
from jax.experimental.pallas import tpu as pltpu
from jax.sharding import PartitionSpec as P


SPLIT = (1, 1)
ANY = pl.BlockSpec(memory_space=pl.ANY)
VMEM = pl.BlockSpec(memory_space=pltpu.VMEM)
SMEM = pl.BlockSpec(memory_space=pltpu.SMEM)
LIMIT = 20 * 2**20
STEPS = 32767.0
TAIL = 16


def fold_ring(n):
    order = [2 * z for z in range(n)] + [2 * z + 1 for z in reversed(range(n))]
    return [(order[i], order[(i + 1) % len(order)]) for i in range(len(order))]


def cuts(rows):
    unit = rows // sum(SPLIT)
    ends = [unit * sum(SPLIT[:i]) for i in range(len(SPLIT) + 1)]
    return [(a, b - a) for a, b in zip(ends, ends[1:])]


def shift(n, by):
    return [(i, (i + by) % n) for i in range(n)]


def rank_of(block, z, owned):
    mine = jnp.abs(block - z)
    rank = jnp.int32(0)
    for other in owned:
        far = jnp.abs(other - z)
        nearer = (far < mine) | ((far == mine) & (other < block))
        rank = rank + nearer.astype(jnp.int32)
    return rank


def pick_ranked(owned, z, s):
    block = owned[0]
    for one in owned[1:]:
        block = jnp.where(rank_of(one, z, owned) == s, one, block)
    return block


def scalars(n, nb, cand, refs):
    pairs = [[refs[b * cand + k] for k in range(cand)] for b in range(nb)]
    return pairs, [refs[nb * cand + j] for j in range(n)]


def pick(values, index):
    got = values[0]
    for k in range(1, len(values)):
        got = jnp.where(index == k, values[k], got)
    return got


def listed(pairs, b, block):
    wanted = pairs[b][0] == block
    for one in pairs[b][1:]:
        wanted = wanted | (one == block)
    return wanted


def sources(dists, chunks, refs):
    z = lax.axis_index("blk")
    core = lax.axis_index("qry")
    at = 0
    found = []
    for d in dists:
        directions = (0,) if d == 0 else (-d, d)
        for there in directions:
            found.append((z + jnp.where(core == 0, there, -there), refs[at : at + chunks]))
            at += chunks
    return found


def fetch(block, pool, into, w_into, sems):
    feats = into.shape[1]
    for held, refs in pool:

        @pl.when(held == block)
        def _():
            at = 0
            for ref in refs:
                rows = ref if ref.shape[1] == feats else ref.at[:, pl.ds(0, feats)]
                pltpu.make_async_copy(rows, into.at[pl.ds(at, ref.shape[0])], sems.at[0]).start()
                at += ref.shape[0]
            tail = refs[-1].at[pl.ds(0, TAIL), pl.ds(feats, w_into.shape[1])]
            pltpu.make_async_copy(tail, w_into, sems.at[1]).start()


def fetched(into, w_into, sems):
    pltpu.make_async_copy(into, into, sems.at[0]).wait()
    pltpu.make_async_copy(w_into, w_into, sems.at[1]).wait()
    return w_into[...].astype(jnp.float32)[:1]


def dot_rows(a, b):
    return lax.dot_general(a, b, (((1,), (1,)), ((), ())), preferred_element_type=jnp.float32)


def coded(tile):
    top = jnp.maximum(jnp.max(jnp.abs(tile), axis=0, keepdims=True), 1e-36)
    power = jnp.ceil(jnp.log2(top))
    steps = jnp.clip(jnp.round(tile * jnp.exp2(-power) * STEPS), -STEPS, STEPS)
    return steps.astype(jnp.int32).astype(jnp.int16), power


def decoded(part, b, span, count):
    power = part[pl.ds(count, TAIL), :].astype(jnp.int32).astype(jnp.float32)[b : b + 1]
    steps = part[span, :].astype(jnp.int32).astype(jnp.float32)
    return steps * (jnp.exp2(power) * (1.0 / STEPS))


def slot_kernel(sizes, s, dists, chunks, packed, *refs):
    n, ckpts, per, nb, cand = sizes
    qs, ins = refs[:nb], refs[nb : -(ckpts - 1) - 3]
    outs = refs[-(ckpts - 1) - 3 : -3]
    rows, w_rows, sems = refs[-3:]
    z, c = lax.axis_index("blk"), lax.axis_index("ckpt")
    pairs, order = scalars(n, nb, cand, packed)
    qblk, width = qs[0].shape[0], rows.shape[0]
    count = nb * qblk
    pool = sources(dists, chunks, ins)
    for r in range(1, ckpts):
        owner = lax.rem(c + r, ckpts)
        owned = [pick(order[k::per], owner) for k in range(per)]
        block = pick_ranked(owned, z, s)
        fetch(block, pool, rows, w_rows, sems)
        weight = fetched(rows, w_rows, sems)
        out = outs[r - 1]
        out[pl.ds(count, TAIL), :] = jnp.zeros((TAIL, width), jnp.int16)
        for b in range(nb):
            span = pl.ds(b * qblk, qblk)
            wanted = listed(pairs, b, block)

            @pl.when(wanted)
            def _():
                steps, power = coded(dot_rows(qs[b][...], rows[...]) * weight)
                out[span, :] = steps
                line = lax.broadcasted_iota(jnp.int32, (TAIL, width), 0)
                old = out[pl.ds(count, TAIL), :].astype(jnp.int32)
                out[pl.ds(count, TAIL), :] = jnp.where(line == b, power.astype(jnp.int32), old).astype(jnp.int16)

            @pl.when(jnp.logical_not(wanted))
            def _():
                out[span, :] = jnp.zeros((qblk, width), jnp.int16)


def own_kernel(sizes, dists, chunks, packed, *refs):
    n, ckpts, per, nb, cand = sizes
    early = (per - 1) * (ckpts - 1)
    qs, ins, came = refs[:nb], refs[nb : len(refs) - early - 6], refs[len(refs) - early - 6 : -6]
    out, last, rows, w_rows, tiles, sems = refs[-6:]
    z, c = lax.axis_index("blk"), lax.axis_index("ckpt")
    pairs, order = scalars(n, nb, cand, packed)
    qblk, width = qs[0].shape[0], rows.shape[1]
    count = nb * qblk
    pool = sources(dists, chunks, ins)
    owned = [pick(order[k::per], c) for k in range(per)]
    ranked = [pick_ranked(owned, z, s) for s in range(per)]
    for s, block in enumerate(ranked):
        fetch(block, pool, rows.at[s], w_rows.at[s], sems.at[s])
    for s, block in enumerate(ranked):
        weight = fetched(rows.at[s], w_rows.at[s], sems.at[s])
        into = last if s == per - 1 else tiles.at[s]
        for b in range(nb):
            span = pl.ds(b * qblk, qblk)
            wanted = listed(pairs, b, block)

            @pl.when(wanted)
            def _():
                total = dot_rows(qs[b][...], rows[s]) * weight
                if s < per - 1:
                    for r in range(ckpts - 1):
                        total = total + decoded(came[s * (ckpts - 1) + r], b, span, count)
                into[span, :] = total

            @pl.when(jnp.logical_not(wanted))
            def _():
                into[span, :] = jnp.zeros((qblk, width), jnp.float32)

        if s < per - 1:
            put_columns(tiles.at[s], out, owned, block, sems.at[s, 0]).start()
    for s, block in enumerate(ranked[:-1]):
        put_columns(tiles.at[s], out, owned, block, sems.at[s, 0]).wait()


def put_columns(tile, out, owned, block, sem, span=slice(None)):
    width = tile.shape[1]
    slot = jnp.int32(0)
    for j, one in enumerate(owned):
        slot = jnp.where(one == block, j, slot)
    columns = pl.ds(pl.multiple_of(slot * width, width), width)
    return pltpu.make_async_copy(tile.at[span, :], out.at[span, columns], sem)


def sum_kernel(sizes, packed, acc_ref, last_ref, *refs):
    n, _, per, nb, cand = sizes
    came, out, tile, sems = refs[:-3], refs[-3], refs[-2], refs[-1]
    z, c = lax.axis_index("blk"), lax.axis_index("ckpt")
    _, order = scalars(n, nb, cand, packed)
    count = last_ref.shape[0]
    qblk = count // nb
    owned = [pick(order[k::per], c) for k in range(per)]
    block = pick_ranked(owned, z, per - 1)
    stores = []
    for b in range(nb):
        span = pl.ds(b * qblk, qblk)
        total = last_ref[span, :]
        for part in came:
            total = total + decoded(part, b, span, count)
        tile[span, :] = total
        stores.append(put_columns(tile, out, owned, block, sems.at[b], span))
        stores[-1].start()
    for store in stores:
        store.wait()


def per_device(query_feats, train_feats, loss_weights, pair_list, tile_owner):
    queries, own_rows = query_feats[0], train_feats[0]
    n, ckpts = lax.axis_size("blk"), lax.axis_size("ckpt")
    per = n // ckpts
    rows, feats = own_rows.shape
    count = queries.shape[0]
    lines = ("blk", "qry")
    ring, swap = fold_ring(n), shift(2, 1)
    chunks = len(SPLIT)

    params = pltpu.CompilerParams(vmem_limit_bytes=LIMIT)
    nb, cand = pair_list.shape
    sizes = (n, ckpts, per, nb, cand)
    held = [own_rows[a : a + length] for a, length in cuts(rows)]
    tagged = jnp.broadcast_to(loss_weights, (held[-1].shape[0], rows))
    held[-1] = jnp.concatenate([held[-1], tagged], axis=1)
    packed = jnp.concatenate([pair_list.reshape(nb * cand), tile_owner])
    qblk = count // nb
    asked = []
    for b in range(nb):
        asked.append(queries[b * qblk : (b + 1) * qblk])
    near = {0: held}
    for step in range(1, n):
        held = [lax.ppermute(part, lines, ring) for part in held]
        near[step] = held + [lax.ppermute(part, "qry", swap) for part in held]
    sent = jax.ShapeDtypeStruct((count + TAIL, rows), jnp.int16)
    tile = jax.ShapeDtypeStruct((count, rows), jnp.float32)
    acc = jax.ShapeDtypeStruct((count, per * rows), jnp.float32)
    flops = 2 * count * rows * feats
    came = []
    for s in range(per):
        dists = tuple(range(n - per + s + 1))
        pool = [ref for d in dists for ref in near[d]]
        terms = pl.pallas_call(
            functools.partial(slot_kernel, sizes, s, dists, chunks),
            out_shape=[sent] * (ckpts - 1),
            in_specs=[SMEM] + [VMEM] * nb + [ANY] * len(pool),
            out_specs=[VMEM] * (ckpts - 1),
            scratch_shapes=[
                pltpu.VMEM((rows, feats), jnp.bfloat16),
                pltpu.VMEM((TAIL, rows), jnp.bfloat16),
                pltpu.SemaphoreType.DMA((2,)),
            ],
            compiler_params=params,
            cost_estimate=pl.CostEstimate(flops=flops * (ckpts - 1), bytes_accessed=count * feats * 2, transcendentals=0),
        )(packed, *asked, *pool)
        came.append([lax.ppermute(terms[r - 1], "ckpt", shift(ckpts, r)) for r in range(1, ckpts)])
    early = [part for parts in came[:-1] for part in parts]
    total, last = pl.pallas_call(
        functools.partial(own_kernel, sizes, dists, chunks),
        out_shape=[acc, tile],
        in_specs=[SMEM] + [VMEM] * nb + [ANY] * len(pool) + [VMEM] * len(early),
        out_specs=[ANY, VMEM],
        scratch_shapes=[
            pltpu.VMEM((per, rows, feats), jnp.bfloat16),
            pltpu.VMEM((per, TAIL, rows), jnp.bfloat16),
            pltpu.VMEM((max(per - 1, 1), count, rows), jnp.float32),
            pltpu.SemaphoreType.DMA((per, 2)),
        ],
        compiler_params=params,
        cost_estimate=pl.CostEstimate(flops=flops * per, bytes_accessed=count * feats * 2, transcendentals=0),
    )(packed, *asked, *pool, *early)
    return pl.pallas_call(
        functools.partial(sum_kernel, sizes),
        out_shape=acc,
        in_specs=[SMEM, ANY, VMEM] + [VMEM] * (ckpts - 1),
        out_specs=ANY,
        input_output_aliases={1: 0},
        scratch_shapes=[pltpu.VMEM((count, rows), jnp.float32), pltpu.SemaphoreType.DMA((nb,))],
        compiler_params=params,
    )(packed, total, last, *came[-1])


def solution(mesh):
    return jax.shard_map(
        per_device,
        mesh=mesh,
        in_specs=(
            P("ckpt", ("shard", "blk", "qry"), None),
            P("ckpt", ("shard", "blk"), None),
            P("ckpt", ("shard", "blk")),
            P(("shard", "blk", "qry"), None),
            P("shard"),
        ),
        out_specs=P(("shard", "blk", "qry"), "ckpt"),
        check_vma=False,
    )
```

time: 43.7 us -> 41.8 us (0.957)
  starting transfers between devices: 22.4 us -> 17.9 us
  local copies, waits for them, and re-layouts: 3.45 us -> 6.79 us
  waiting for transfers between devices: 10.9 us -> 9.77 us
  Pallas kernels: 5.94 us -> 6.89 us
  other arithmetic: 0.75 us -> 0.12 us
    ppermute x2 -> x0, starting transfers between devices: 4.21 us -> none  [per_device(): lax.ppermute(weights, 'blk', xor(n, bit))]
    ppermute x2 -> x0, waiting for transfers between devices: 4.18 us -> none  [per_device(): lax.ppermute(weights, 'blk', xor(n, bit))]
    ppermute x6, waiting for transfers between devices: 4.05 us -> 7.06 us  [per_device(): held = [lax.ppermute(part, lines, ring) for part in held]]
    unnamed x6 -> x12, local copies, waits for them, and re-layouts: 1.6 us -> 3.3 us
    slice x1 -> x2, local copies, waits for them, and re-layouts: 1.09 us -> 2.74 us  [the longest x1 1.68 us: per_device(): asked.append(queries[b * qblk:(b + 1) * qblk])]
    pallas_call x2, Pallas kernels: 2.32 us -> 3.32 us  [per_device(): pl.pallas_call(functools.partial(slot_kernel, sizes, s, dists, chunks), o...]
    reshape x1, local copies, waits for them, and re-layouts: 0.76 us -> 0.08 us  [per_device(): packed = jnp.concatenate([pair_list.reshape(nb * cand), tile_owner])]
    concatenate x0 -> x1, local copies, waits for them, and re-layouts: none -> 0.66 us  [per_device(): held[-1] = jnp.concatenate([held[-1], tagged], axis=1)]
  transfers between devices with their start and end apart: 16 -> 14, of which waited for: 8 -> 6; matrix products, arithmetic and copies ran while one was open for 3% -> 4% of each run, Pallas kernels for 11% -> 13%
where the time goes in v4:
time: 41.8 us; the launch traced here: 41.6 us
  starting transfers between devices  17.9 us (43%)
  waiting for transfers between devices  9.77 us (23%)
  Pallas kernels  6.89 us (16%)
  local copies, waits for them, and re-layouts  6.79 us (16%)
    ppermute x6, starting transfers between devices, per_device(): held = [lax.ppermute(part, lines, ring) for part in held]  14.3 us
    ppermute x6, waiting for transfers between devices, per_device(): held = [lax.ppermute(part, lines, ring) for part in held]  7.06 us
    pallas_call x2, Pallas kernels, per_device(): pl.pallas_call(functools.partial(slot_kernel, sizes, s, dists, chunks), o...  3.32 us
    unnamed x12, local copies, waits for them, and re-layouts  3.3 us
    ppermute x2, waiting for transfers between devices, per_device(): lax.ppermute(terms[r - 1], 'ckpt', shift(ckpts, r))  2.69 us
    ppermute x2, starting transfers between devices, per_device(): lax.ppermute(terms[r - 1], 'ckpt', shift(ckpts, r))  2.58 us
    pallas_call x1, Pallas kernels, per_device(): pl.pallas_call(functools.partial(own_kernel, sizes, dists, chunks), out_s...  2.3 us
    slice x1, local copies, waits for them, and re-layouts, per_device(): asked.append(queries[b * qblk:(b + 1) * qblk])  1.68 us
  transfers between devices with their start and end apart: 14, of which 6 were waited for; matrix products, arithmetic and copies ran while one was open for 4% of the time, Pallas kernels for 13%

profile of v4, /device:TPU:0, one launch (start us, length us, event | category | flops | bytes accessed | tf_op | source)
XLA Modules:
  0.0 41.6 jit_solution(16843479668965474676)
XLA Ops:
  0.0 1.1 %slice_bitcast_fusion.2 = (bf16[64,2048]{1,0:T(8,128)(2,1)S(1)}, bf16[64,2048]{1,0:T(8,128)(2,1)S(1)}) fusion(bf16[1,128,2048]{2,1,0:T(8,128)(2,1)} %param.6), kind=kLoop, calls=%fused_computation.3 | loop fusion | bytes 1048576 | tf_op jit(solution)/shard_map/slice | solution.py:240
  1.1 0.7 %pad.1.clone = bf16[2176]{0:T(1024)(128)(2,1)S(1)} pad(bf16[128]{0:T(256)(128)(2,1)} %bitcast.9, bf16[]{:T(256)} %constant.4), padding=2048_0 | pad | bytes 4610 | tf_op jit(solution)/shard_map/concatenate | solution.py:242
  1.8 3.1 %collective-permute-start.1 = (bf16[64,2176]{1,0:T(8,128)(2,1)S(1)}, bf16[64,2176]{1,0:T(8,128)(2,1)S(1)}, u32[]{:S(2)}, u32[]{:S(2)}) collective-permute-start(bf16[64,2176]{1,0:T(8,128)(2,1)S(1)} %pad_maximum_fusion.refs_3_), channel_id=1, source_target_pairs={{0,4},{4,8},{8,12},{12,13},{13,9},{9,5},{5,1},{1,0},{2,6},{6,10},{... | collective-permute-start | bytes 835592 | tf_op jit(solution)/shard_map/ppermute | solution.py:250
  4.9 1.6 %collective-permute-start = (bf16[64,2048]{1,0:T(8,128)(2,1)S(1)}, bf16[64,2048]{1,0:T(8,128)(2,1)S(1)}, u32[]{:S(2)}, u32[]{:S(2)}) collective-permute-start(bf16[64,2048]{1,0:T(8,128)(2,1)S(1)} %get-tuple-element.12.refs_2_), channel_id=1, source_target_pairs={{0,4},{4,8},{8,12},{12,13},{13,9},{9,5},{5,1},{1,0},{2,6},{6,10},{... | collective-permute-start | bytes 786440 | tf_op jit(solution)/shard_map/ppermute | solution.py:250
  6.4 2.5 %collective-permute-done.1.refs_5_ = bf16[64,2176]{1,0:T(8,128)(2,1)S(1)} collective-permute-done((bf16[64,2176]{1,0:T(8,128)(2,1)S(1)}, bf16[64,2176]{1,0:T(8,128)(2,1)S(1)}, u32[]{:S(2)}, u32[]{:S(2)}) %collective-permute-start.1) | collective-permute-done | bytes 278560 | tf_op jit(solution)/shard_map/ppermute | solution.py:250
  8.9 2.5 %collective-permute-start.5 = (bf16[64,2176]{1,0:T(8,128)(2,1)S(1)}, bf16[64,2176]{1,0:T(8,128)(2,1)S(1)}, u32[]{:S(2)}, u32[]{:S(2)}) collective-permute-start(bf16[64,2176]{1,0:T(8,128)(2,1)S(1)} %collective-permute-done.1.refs_5_), channel_id=1, source_target_pairs={{0,4},{4,8},{8,12},{12,13},{13,9},{9,5},{5,1},{1,0},{2,6},{6,10},{... | collective-permute-start | bytes 835592 | tf_op jit(solution)/shard_map/ppermute | solution.py:250
  11.7 2.5 %collective-permute-start.4 = (bf16[64,2048]{1,0:T(8,128)(2,1)S(1)}, bf16[64,2048]{1,0:T(8,128)(2,1)}, u32[]{:S(2)}, u32[]{:S(2)}) collective-permute-start(bf16[64,2048]{1,0:T(8,128)(2,1)S(1)} %collective-permute-done.refs_4_), channel_id=1, source_target_pairs={{0,4},{4,8},{8,12},{12,13},{13,9},{9,5},{5,1},{1,0},{2,6},{6,10},{... | collective-permute-start | bytes 786440 | tf_op jit(solution)/shard_map/ppermute | solution.py:250
  14.2 1.3 %collective-permute-done.5.refs_9_ = bf16[64,2176]{1,0:T(8,128)(2,1)S(1)} collective-permute-done((bf16[64,2176]{1,0:T(8,128)(2,1)S(1)}, bf16[64,2176]{1,0:T(8,128)(2,1)S(1)}, u32[]{:S(2)}, u32[]{:S(2)}) %collective-permute-start.5) | collective-permute-done | bytes 278560 | tf_op jit(solution)/shard_map/ppermute | solution.py:250
  15.5 2.5 %collective-permute-start.9 = (bf16[64,2176]{1,0:T(8,128)(2,1)S(1)}, bf16[64,2176]{1,0:T(8,128)(2,1)}, u32[]{:S(2)}, u32[]{:S(2)}) collective-permute-start(bf16[64,2176]{1,0:T(8,128)(2,1)S(1)} %collective-permute-done.5.refs_9_), channel_id=1, source_target_pairs={{0,4},{4,8},{8,12},{12,13},{13,9},{9,5},{5,1},{1,0},{2,6},{6,10},{... | collective-permute-start | bytes 835592 | tf_op jit(solution)/shard_map/ppermute | solution.py:250
  18.0 0.7 %copy-done = bf16[64,2048]{1,0:T(8,128)(2,1)} copy-done((bf16[64,2048]{1,0:T(8,128)(2,1)}, bf16[64,2048]{1,0:T(8,128)(2,1)S(1)}, u32[]{:S(2)}) %copy-start) | copy-done | bytes 262168
  18.7 2.2 %collective-permute-start.8 = (bf16[64,2048]{1,0:T(8,128)(2,1)}, bf16[64,2048]{1,0:T(8,128)(2,1)}, u32[]{:S(2)}, u32[]{:S(2)}) collective-permute-start(bf16[64,2048]{1,0:T(8,128)(2,1)} %collective-permute-done.4.refs_8_), channel_id=1, source_target_pairs={{0,4},{4,8},{8,12},{12,13},{13,9},{9,5},{5,1},{1,0},{2,6},{6,10},{... | collective-permute-start | bytes 786440 | tf_op jit(solution)/shard_map/ppermute | solution.py:250
  21.4 0.7 %copy-done.2 = bf16[64,2048]{1,0:T(8,128)(2,1)} copy-done((bf16[64,2048]{1,0:T(8,128)(2,1)}, bf16[64,2048]{1,0:T(8,128)(2,1)S(1)}, u32[]{:S(2)}) %copy-start.2) | copy-done | bytes 262168
  22.1 3.0 %collective-permute-done.8.refs_12_ = bf16[64,2048]{1,0:T(8,128)(2,1)} collective-permute-done((bf16[64,2048]{1,0:T(8,128)(2,1)}, bf16[64,2048]{1,0:T(8,128)(2,1)}, u32[]{:S(2)}, u32[]{:S(2)}) %collective-permute-start.8) | collective-permute-done | bytes 262176 | tf_op jit(solution)/shard_map/ppermute | solution.py:250
  25.1 0.5 %collective-permute-start.11 = (bf16[64,2176]{1,0:T(8,128)(2,1)}, bf16[64,2176]{1,0:T(8,128)(2,1)}, u32[]{:S(2)}, u32[]{:S(2)}) collective-permute-start(bf16[64,2176]{1,0:T(8,128)(2,1)} %collective-permute-done.9.refs_13_), channel_id=1, source_target_pairs={{0,1},{1,0},{2,3},{3,2},{4,5},{5,4},{6,7},{7,6},{8,9},{9,8},{10,11... | collective-permute-start | bytes 835592 | tf_op jit(solution)/shard_map/ppermute | solution.py:251
  25.6 1.7 %slice_bitcast_fusion = (bf16[256,2048]{1,0:T(8,128)(2,1)S(1)}, bf16[256,2048]{1,0:T(8,128)(2,1)S(1)}) fusion(bf16[1,512,2048]{2,1,0:T(8,128)(2,1)} %param.5), kind=kLoop, calls=%fused_computation | loop fusion | bytes 4194304 | tf_op jit(solution)/shard_map/slice | solution.py:247
  27.5 0.9 %copy-done.1 = bf16[64,2048]{1,0:T(8,128)(2,1)S(1)} copy-done((bf16[64,2048]{1,0:T(8,128)(2,1)S(1)}, bf16[64,2048]{1,0:T(8,128)(2,1)}, u32[]{:S(2)}) %copy-start.1) | copy-done | bytes 262168
  28.4 0.9 %copy-done.3 = bf16[64,2048]{1,0:T(8,128)(2,1)S(1)} copy-done((bf16[64,2048]{1,0:T(8,128)(2,1)S(1)}, bf16[64,2048]{1,0:T(8,128)(2,1)}, u32[]{:S(2)}) %copy-start.3) | copy-done | bytes 262168
  29.4 0.7 %shard_map.55 = s16[528,128]{1,0:T(8,128)(2,1)S(1)} custom-call(s32[8]{0:T(128)S(1)} %pad_add_fusion.packed, bf16[256,2048]{1,0:T(8,128)(2,1)S(1)} %get-tuple-element.10.refs_0_, bf16[256,2048]{1,0:T(8,128)(2,1)S(1)} %get-tuple-element.9.refs_1_, bf16[64,2048]{1,0:T(8,128)(2,1)S(1)} %get-tuple-element.12.refs_2_, ...), custom_call_target="tpu_custom_call" | custom-call | flops 268435456 | bytes 2097152 | tf_op jit(solution)/shard_map/pallas_call | solution.py:260
  30.1 2.5 %collective-permute-start.12 = (s16[528,128]{1,0:T(8,128)(2,1)S(1)}, s16[528,128]{1,0:T(8,128)(2,1)S(1)}, u32[]{:S(2)}, u32[]{:S(2)}) collective-permute-start(s16[528,128]{1,0:T(8,128)(2,1)S(1)} %shard_map.55), channel_id=1, source_target_pairs={{0,2},{2,0},{1,3},{3,1},{4,6},{6,4},{5,7},{7,5},{8,10},{10,8},{9,1... | collective-permute-start | bytes 405512 | tf_op jit(solution)/shard_map/ppermute | solution.py:273
  32.6 2.6 %shard_map.57 = s16[528,128]{1,0:T(8,128)(2,1)S(1)} custom-call(s32[8]{0:T(128)S(1)} %pad_add_fusion.packed, bf16[256,2048]{1,0:T(8,128)(2,1)S(1)} %get-tuple-element.10.refs_0_, bf16[256,2048]{1,0:T(8,128)(2,1)S(1)} %get-tuple-element.9.refs_1_, bf16[64,2048]{1,0:T(8,128)(2,1)S(1)} %get-tuple-element.12.refs_2_, ...), custom_call_target="tpu_custom_call" | custom-call | flops 268435456 | bytes 2097152 | tf_op jit(solution)/shard_map/pallas_call | solution.py:260
  35.3 0.5 %collective-permute-done.12.refs_16_ = s16[528,128]{1,0:T(8,128)(2,1)S(1)} collective-permute-done((s16[528,128]{1,0:T(8,128)(2,1)S(1)}, s16[528,128]{1,0:T(8,128)(2,1)S(1)}, u32[]{:S(2)}, u32[]{:S(2)}) %collective-permute-start.12) | collective-permute-done | bytes 135200 | tf_op jit(solution)/shard_map/ppermute | solution.py:273
  35.8 2.3 %shard_map.56 = (f32[512,256]{1,0:T(8,128)}, f32[512,128]{1,0:T(8,128)S(1)}) custom-call(s32[8]{0:T(128)S(1)} %pad_add_fusion.packed, bf16[256,2048]{1,0:T(8,128)(2,1)S(1)} %get-tuple-element.10.refs_0_, bf16[256,2048]{1,0:T(8,128)(2,1)S(1)} %get-tuple-element.9.refs_1_, bf16[64,2048]{1,0:T(8,128)(2,1)S(1)} %get-tuple-element.12.refs_2_, ...), custom_call_target="tpu_custom_call" | custom-call | flops 536870912 | bytes 2097152 | tf_op jit(solution)/shard_map/pallas_call | solution.py:275
  38.1 2.1 %collective-permute-done.13.refs_0_ = s16[528,128]{1,0:T(8,128)(2,1)S(1)} collective-permute-done((s16[528,128]{1,0:T(8,128)(2,1)S(1)}, s16[528,128]{1,0:T(8,128)(2,1)S(1)}, u32[]{:S(2)}, u32[]{:S(2)}) %collective-permute-start.13) | collective-permute-done | bytes 135200 | tf_op jit(solution)/shard_map/ppermute | solution.py:273
  40.3 1.3 %shard_map.58 = f32[512,256]{1,0:T(8,128)} custom-call(s32[8]{0:T(128)S(1)} %pad_add_fusion.packed, f32[512,256]{1,0:T(8,128)} %get-tuple-element.7.acc_ref, f32[512,128]{1,0:T(8,128)S(1)} %get-tuple-element.8.last_ref, s16[528,128]{1,0:T(8,128)(2,1)S(1)} %collective-permute-done.13.refs_0_), custom_call_target="tpu_custom_call", output_to_operand_aliasing={{}: (1, {})} | custom-call | tf_op jit(solution)/shard_map/pallas_call | solution.py:289
  (26 shorter events, 1.2 us)
Async XLA Ops:
  1.8 7.1 %collective-permute-start.1 = (bf16[64,2176]{1,0:T(8,128)(2,1)S(1)}, bf16[64,2176]{1,0:T(8,128)(2,1)S(1)}, u32[]{:S(2)}, u32[]{:S(2)}) collective-permute-start(bf16[64,2176]{1,0:T(8,128)(2,1)S(1)} %pad_maximum_fusion.refs_3_), channel_id=1, source_target_pairs={{0,4},{4,8},{8,12},{12,13},{13,9},{9,5},{5,1},{1,0},{2,6},{6,10},{... | collective-permute-start | bytes 835592 | tf_op jit(solution)/shard_map/ppermute | solution.py:250
  4.9 22.4 %copy-start.4 = (s32[2,2]{1,0:T(2,128)S(1)}, s32[2,2]{1,0:T(2,128)}, u32[]{:S(2)}) copy-start(s32[2,2]{1,0:T(2,128)} %param.8) | copy-start | bytes 52
  4.9 22.5 %copy-start.5 = (s32[4]{0:T(128)S(1)}, s32[4]{0:T(128)}, u32[]{:S(2)}) copy-start(s32[4]{0:T(128)} %param.9) | copy-start | bytes 52
  4.9 6.9 %collective-permute-start = (bf16[64,2048]{1,0:T(8,128)(2,1)S(1)}, bf16[64,2048]{1,0:T(8,128)(2,1)S(1)}, u32[]{:S(2)}, u32[]{:S(2)}) collective-permute-start(bf16[64,2048]{1,0:T(8,128)(2,1)S(1)} %get-tuple-element.12.refs_2_), channel_id=1, source_target_pairs={{0,4},{4,8},{8,12},{12,13},{13,9},{9,5},{5,1},{1,0},{2,6},{6,10},{... | collective-permute-start | bytes 786440 | tf_op jit(solution)/shard_map/ppermute | solution.py:250
  8.9 6.5 %collective-permute-start.5 = (bf16[64,2176]{1,0:T(8,128)(2,1)S(1)}, bf16[64,2176]{1,0:T(8,128)(2,1)S(1)}, u32[]{:S(2)}, u32[]{:S(2)}) collective-permute-start(bf16[64,2176]{1,0:T(8,128)(2,1)S(1)} %collective-permute-done.1.refs_5_), channel_id=1, source_target_pairs={{0,4},{4,8},{8,12},{12,13},{13,9},{9,5},{5,1},{1,0},{2,6},{6,10},{... | collective-permute-start | bytes 835592 | tf_op jit(solution)/shard_map/ppermute | solution.py:250
  11.7 6.9 %collective-permute-start.4 = (bf16[64,2048]{1,0:T(8,128)(2,1)S(1)}, bf16[64,2048]{1,0:T(8,128)(2,1)}, u32[]{:S(2)}, u32[]{:S(2)}) collective-permute-start(bf16[64,2048]{1,0:T(8,128)(2,1)S(1)} %collective-permute-done.refs_4_), channel_id=1, source_target_pairs={{0,4},{4,8},{8,12},{12,13},{13,9},{9,5},{5,1},{1,0},{2,6},{6,10},{... | collective-permute-start | bytes 786440 | tf_op jit(solution)/shard_map/ppermute | solution.py:250
  15.5 9.6 %collective-permute-start.9 = (bf16[64,2176]{1,0:T(8,128)(2,1)S(1)}, bf16[64,2176]{1,0:T(8,128)(2,1)}, u32[]{:S(2)}, u32[]{:S(2)}) collective-permute-start(bf16[64,2176]{1,0:T(8,128)(2,1)S(1)} %collective-permute-done.5.refs_9_), channel_id=1, source_target_pairs={{0,4},{4,8},{8,12},{12,13},{13,9},{9,5},{5,1},{1,0},{2,6},{6,10},{... | collective-permute-start | bytes 835592 | tf_op jit(solution)/shard_map/ppermute | solution.py:250
  18.0 3.4 %collective-permute-start.2 = (bf16[64,2048]{1,0:T(8,128)(2,1)S(1)}, bf16[64,2048]{1,0:T(8,128)(2,1)S(1)}, u32[]{:S(2)}, u32[]{:S(2)}) collective-permute-start(bf16[64,2048]{1,0:T(8,128)(2,1)S(1)} %collective-permute-done.refs_4_), channel_id=1, source_target_pairs={{0,1},{1,0},{2,3},{3,2},{4,5},{5,4},{6,7},{7,6},{8,9},{9,8},{10,11... | collective-permute-start | bytes 786440 | tf_op jit(solution)/shard_map/ppermute | solution.py:251
  18.0 0.7 %copy-start = (bf16[64,2048]{1,0:T(8,128)(2,1)}, bf16[64,2048]{1,0:T(8,128)(2,1)S(1)}, u32[]{:S(2)}) copy-start(bf16[64,2048]{1,0:T(8,128)(2,1)S(1)} %collective-permute-done.refs_4_) | copy-start | bytes 786436
  18.7 6.4 %collective-permute-start.8 = (bf16[64,2048]{1,0:T(8,128)(2,1)}, bf16[64,2048]{1,0:T(8,128)(2,1)}, u32[]{:S(2)}, u32[]{:S(2)}) collective-permute-start(bf16[64,2048]{1,0:T(8,128)(2,1)} %collective-permute-done.4.refs_8_), channel_id=1, source_target_pairs={{0,4},{4,8},{8,12},{12,13},{13,9},{9,5},{5,1},{1,0},{2,6},{6,10},{... | collective-permute-start | bytes 786440 | tf_op jit(solution)/shard_map/ppermute | solution.py:250
  20.9 6.6 %collective-permute-start.3 = (bf16[64,2176]{1,0:T(8,128)(2,1)S(1)}, bf16[64,2176]{1,0:T(8,128)(2,1)S(1)}, u32[]{:S(2)}, u32[]{:S(2)}) collective-permute-start(bf16[64,2176]{1,0:T(8,128)(2,1)S(1)} %collective-permute-done.1.refs_5_), channel_id=1, source_target_pairs={{0,1},{1,0},{2,3},{3,2},{4,5},{5,4},{6,7},{7,6},{8,9},{9,8},{10,11... | collective-permute-start | bytes 835592 | tf_op jit(solution)/shard_map/ppermute | solution.py:251
  20.9 6.6 %collective-permute-start.6 = (bf16[64,2048]{1,0:T(8,128)(2,1)}, bf16[64,2048]{1,0:T(8,128)(2,1)}, u32[]{:S(2)}, u32[]{:S(2)}) collective-permute-start(bf16[64,2048]{1,0:T(8,128)(2,1)} %collective-permute-done.4.refs_8_), channel_id=1, source_target_pairs={{0,1},{1,0},{2,3},{3,2},{4,5},{5,4},{6,7},{7,6},{8,9},{9,8},{10,11... | collective-permute-start | bytes 786440 | tf_op jit(solution)/shard_map/ppermute | solution.py:251
  21.4 0.7 %copy-start.2 = (bf16[64,2048]{1,0:T(8,128)(2,1)}, bf16[64,2048]{1,0:T(8,128)(2,1)S(1)}, u32[]{:S(2)}) copy-start(bf16[64,2048]{1,0:T(8,128)(2,1)S(1)} %collective-permute-done.2.refs_6_) | copy-start | bytes 786436
  22.1 5.4 %collective-permute-start.7 = (bf16[64,2176]{1,0:T(8,128)(2,1)S(1)}, bf16[64,2176]{1,0:T(8,128)(2,1)}, u32[]{:S(2)}, u32[]{:S(2)}) collective-permute-start(bf16[64,2176]{1,0:T(8,128)(2,1)S(1)} %collective-permute-done.5.refs_9_), channel_id=1, source_target_pairs={{0,1},{1,0},{2,3},{3,2},{4,5},{5,4},{6,7},{7,6},{8,9},{9,8},{10,11... | collective-permute-start | bytes 835592 | tf_op jit(solution)/shard_map/ppermute | solution.py:251
  25.1 7.5 %collective-permute-start.10 = (bf16[64,2048]{1,0:T(8,128)(2,1)}, bf16[64,2048]{1,0:T(8,128)(2,1)}, u32[]{:S(2)}, u32[]{:S(2)}) collective-permute-start(bf16[64,2048]{1,0:T(8,128)(2,1)} %collective-permute-done.8.refs_12_), channel_id=1, source_target_pairs={{0,1},{1,0},{2,3},{3,2},{4,5},{5,4},{6,7},{7,6},{8,9},{9,8},{10,11... | collective-permute-start | bytes 786440 | tf_op jit(solution)/shard_map/ppermute | solution.py:251
  25.1 7.5 %collective-permute-start.11 = (bf16[64,2176]{1,0:T(8,128)(2,1)}, bf16[64,2176]{1,0:T(8,128)(2,1)}, u32[]{:S(2)}, u32[]{:S(2)}) collective-permute-start(bf16[64,2176]{1,0:T(8,128)(2,1)} %collective-permute-done.9.refs_13_), channel_id=1, source_target_pairs={{0,1},{1,0},{2,3},{3,2},{4,5},{5,4},{6,7},{7,6},{8,9},{9,8},{10,11... | collective-permute-start | bytes 835592 | tf_op jit(solution)/shard_map/ppermute | solution.py:251
  27.5 1.0 %copy-start.1 = (bf16[64,2048]{1,0:T(8,128)(2,1)S(1)}, bf16[64,2048]{1,0:T(8,128)(2,1)}, u32[]{:S(2)}) copy-start(bf16[64,2048]{1,0:T(8,128)(2,1)} %copy-done) | copy-start | bytes 786436
  28.4 0.9 %copy-start.3 = (bf16[64,2048]{1,0:T(8,128)(2,1)S(1)}, bf16[64,2048]{1,0:T(8,128)(2,1)}, u32[]{:S(2)}) copy-start(bf16[64,2048]{1,0:T(8,128)(2,1)} %copy-done.2) | copy-start | bytes 786436
  30.1 5.8 %collective-permute-start.12 = (s16[528,128]{1,0:T(8,128)(2,1)S(1)}, s16[528,128]{1,0:T(8,128)(2,1)S(1)}, u32[]{:S(2)}, u32[]{:S(2)}) collective-permute-start(s16[528,128]{1,0:T(8,128)(2,1)S(1)} %shard_map.55), channel_id=1, source_target_pairs={{0,2},{2,0},{1,3},{3,1},{4,6},{6,4},{5,7},{7,5},{8,10},{10,8},{9,1... | collective-permute-start | bytes 405512 | tf_op jit(solution)/shard_map/ppermute | solution.py:273
  35.2 5.1 %collective-permute-start.13 = (s16[528,128]{1,0:T(8,128)(2,1)S(1)}, s16[528,128]{1,0:T(8,128)(2,1)S(1)}, u32[]{:S(2)}, u32[]{:S(2)}) collective-permute-start(s16[528,128]{1,0:T(8,128)(2,1)S(1)} %shard_map.57), channel_id=1, source_target_pairs={{0,2},{2,0},{1,3},{3,1},{4,6},{6,4},{5,7},{7,5},{8,10},{10,8},{9,1... | collective-permute-start | bytes 405512 | tf_op jit(solution)/shard_map/ppermute | solution.py:273

commit v5 on v4

--- a/solution.py
+++ b/solution.py
@@ -11,14 +11,13 @@
 SPLIT = (1, 1)
 ANY = pl.BlockSpec(memory_space=pl.ANY)
 VMEM = pl.BlockSpec(memory_space=pltpu.VMEM)
-SMEM = pl.BlockSpec(memory_space=pltpu.SMEM)
 LIMIT = 20 * 2**20
 STEPS = 32767.0
 TAIL = 16
 
 
 def fold_ring(n):
-    order = [2 * z for z in range(n)] + [2 * z + 1 for z in reversed(range(n))]
+    order = [2 * z + 1 for z in range(n)] + [2 * z for z in reversed(range(n))]
     return [(order[i], order[(i + 1) % len(order)]) for i in range(len(order))]
 
 
@@ -50,8 +49,8 @@
 
 
 def scalars(n, nb, cand, refs):
-    pairs = [[refs[b * cand + k] for k in range(cand)] for b in range(nb)]
-    return pairs, [refs[nb * cand + j] for j in range(n)]
+    pairs = [[refs[0, b * cand + k] for k in range(cand)] for b in range(nb)]
+    return pairs, [refs[0, nb * cand + j] for j in range(n)]
 
 
 def pick(values, index):
@@ -76,7 +75,7 @@
     for d in dists:
         directions = (0,) if d == 0 else (-d, d)
         for there in directions:
-            found.append((z + jnp.where(core == 0, there, -there), refs[at : at + chunks]))
+            found.append((z + jnp.where(core == 0, -there, there), refs[at : at + chunks]))
             at += chunks
     return found
 
@@ -240,7 +239,7 @@
     held = [own_rows[a : a + length] for a, length in cuts(rows)]
     tagged = jnp.broadcast_to(loss_weights, (held[-1].shape[0], rows))
     held[-1] = jnp.concatenate([held[-1], tagged], axis=1)
-    packed = jnp.concatenate([pair_list.reshape(nb * cand), tile_owner])
+    packed = jnp.concatenate([pair_list.reshape(1, nb * cand), tile_owner[None, :]], axis=1)
     qblk = count // nb
     asked = []
     for b in range(nb):
@@ -260,7 +259,7 @@
         terms = pl.pallas_call(
             functools.partial(slot_kernel, sizes, s, dists, chunks),
             out_shape=[sent] * (ckpts - 1),
-            in_specs=[SMEM] + [VMEM] * nb + [ANY] * len(pool),
+            in_specs=[VMEM] + [VMEM] * nb + [ANY] * len(pool),
             out_specs=[VMEM] * (ckpts - 1),
             scratch_shapes=[
                 pltpu.VMEM((rows, feats), jnp.bfloat16),
@@ -275,7 +274,7 @@
     total, last = pl.pallas_call(
         functools.partial(own_kernel, sizes, dists, chunks),
         out_shape=[acc, tile],
-        in_specs=[SMEM] + [VMEM] * nb + [ANY] * len(pool) + [VMEM] * len(early),
+        in_specs=[VMEM] + [VMEM] * nb + [ANY] * len(pool) + [VMEM] * len(early),
         out_specs=[ANY, VMEM],
         scratch_shapes=[
             pltpu.VMEM((per, rows, feats), jnp.bfloat16),
@@ -289,7 +288,7 @@
     return pl.pallas_call(
         functools.partial(sum_kernel, sizes),
         out_shape=acc,
-        in_specs=[SMEM, ANY, VMEM] + [VMEM] * (ckpts - 1),
+        in_specs=[VMEM, ANY, VMEM] + [VMEM] * (ckpts - 1),
         out_specs=ANY,
         input_output_aliases={1: 0},
         scratch_shapes=[pltpu.VMEM((count, rows), jnp.float32), pltpu.SemaphoreType.DMA((nb,))],

time: 41.8 us -> 41.4 us (level)
  waiting for transfers between devices: 9.77 us -> 22.3 us
  starting transfers between devices: 17.9 us -> 6.73 us
  Pallas kernels: 6.89 us -> 5.1 us
    ppermute x6, waiting for transfers between devices: 7.06 us -> 19.1 us  [per_device(): held = [lax.ppermute(part, lines, ring) for part in held]]
    ppermute x6, starting transfers between devices: 14.3 us -> 2.63 us  [per_device(): held = [lax.ppermute(part, lines, ring) for part in held]]
    pallas_call x2, Pallas kernels: 3.32 us -> 2.4 us  [per_device(): pl.pallas_call(functools.partial(slot_kernel, sizes, s, dists, chunks), o...]
    pallas_call x1, Pallas kernels: 1.28 us -> 0.83 us  [per_device(): pl.pallas_call(functools.partial(sum_kernel, sizes), out_shape=acc, in_sp...]
    ppermute x2, starting transfers between devices: 2.58 us -> 3.02 us  [per_device(): lax.ppermute(terms[r - 1], 'ckpt', shift(ckpts, r))]
    ppermute x2, waiting for transfers between devices: 2.69 us -> 3.12 us  [per_device(): lax.ppermute(terms[r - 1], 'ckpt', shift(ckpts, r))]
    pallas_call x1, Pallas kernels: 2.3 us -> 1.87 us  [per_device(): pl.pallas_call(functools.partial(own_kernel, sizes, dists, chunks), out_s...]
  transfers between devices with their start and end apart: 14 -> 14, of which waited for: 6 -> 7; matrix products, arithmetic and copies ran while one was open for 4% -> 4% of each run, Pallas kernels for 13% -> 10%
where the time goes in v5:
time: 41.4 us; the launch traced here: 41.1 us
  waiting for transfers between devices  22.3 us (54%)
  local copies, waits for them, and re-layouts  6.79 us (16%)
  starting transfers between devices  6.73 us (16%)
  Pallas kernels  5.1 us (12%)
    ppermute x6, waiting for transfers between devices, per_device(): held = [lax.ppermute(part, lines, ring) for part in held]  19.1 us
    unnamed x12, local copies, waits for them, and re-layouts  3.3 us
    ppermute x2, waiting for transfers between devices, per_device(): lax.ppermute(terms[r - 1], 'ckpt', shift(ckpts, r))  3.12 us
    ppermute x2, starting transfers between devices, per_device(): lax.ppermute(terms[r - 1], 'ckpt', shift(ckpts, r))  3.02 us
    ppermute x6, starting transfers between devices, per_device(): held = [lax.ppermute(part, lines, ring) for part in held]  2.63 us
    pallas_call x2, Pallas kernels, per_device(): pl.pallas_call(functools.partial(slot_kernel, sizes, s, dists, chunks), o...  2.4 us
    pallas_call x1, Pallas kernels, per_device(): pl.pallas_call(functools.partial(own_kernel, sizes, dists, chunks), out_s...  1.87 us
    slice x1, local copies, waits for them, and re-layouts, per_device(): asked.append(queries[b * qblk:(b + 1) * qblk])  1.68 us
  transfers between devices with their start and end apart: 14, of which 7 were waited for; matrix products, arithmetic and copies ran while one was open for 4% of the time, Pallas kernels for 10%

profile of v5, /device:TPU:0, one launch (start us, length us, event | category | flops | bytes accessed | tf_op | source)
XLA Modules:
  0.0 41.1 jit_solution(14582509077689260637)
XLA Ops:
  0.0 1.1 %slice_bitcast_fusion.2 = (bf16[64,2048]{1,0:T(8,128)(2,1)S(1)}, bf16[64,2048]{1,0:T(8,128)(2,1)S(1)}) fusion(bf16[1,128,2048]{2,1,0:T(8,128)(2,1)} %param.6), kind=kLoop, calls=%fused_computation.3 | loop fusion | bytes 1048576 | tf_op jit(solution)/shard_map/slice | solution.py:239
  1.1 0.7 %pad.1.clone = bf16[2176]{0:T(1024)(128)(2,1)S(1)} pad(bf16[128]{0:T(256)(128)(2,1)} %bitcast.10, bf16[]{:T(256)} %constant.4), padding=2048_0 | pad | bytes 4610 | tf_op jit(solution)/shard_map/concatenate | solution.py:241
  1.8 0.5 %collective-permute-start.1 = (bf16[64,2176]{1,0:T(8,128)(2,1)S(1)}, bf16[64,2176]{1,0:T(8,128)(2,1)S(1)}, u32[]{:S(2)}, u32[]{:S(2)}) collective-permute-start(bf16[64,2176]{1,0:T(8,128)(2,1)S(1)} %pad_maximum_fusion.refs_3_), channel_id=1, source_target_pairs={{1,5},{5,9},{9,13},{13,12},{12,8},{8,4},{4,0},{0,1},{3,7},{7,11},{... | collective-permute-start | bytes 835592 | tf_op jit(solution)/shard_map/ppermute | solution.py:249
  2.3 2.1 %collective-permute-start = (bf16[64,2048]{1,0:T(8,128)(2,1)S(1)}, bf16[64,2048]{1,0:T(8,128)(2,1)S(1)}, u32[]{:S(2)}, u32[]{:S(2)}) collective-permute-start(bf16[64,2048]{1,0:T(8,128)(2,1)S(1)} %get-tuple-element.12.refs_2_), channel_id=1, source_target_pairs={{1,5},{5,9},{9,13},{13,12},{12,8},{8,4},{4,0},{0,1},{3,7},{7,11},{... | collective-permute-start | bytes 786440 | tf_op jit(solution)/shard_map/ppermute | solution.py:249
  4.4 5.0 %collective-permute-done.1.refs_5_ = bf16[64,2176]{1,0:T(8,128)(2,1)S(1)} collective-permute-done((bf16[64,2176]{1,0:T(8,128)(2,1)S(1)}, bf16[64,2176]{1,0:T(8,128)(2,1)S(1)}, u32[]{:S(2)}, u32[]{:S(2)}) %collective-permute-start.1) | collective-permute-done | bytes 278560 | tf_op jit(solution)/shard_map/ppermute | solution.py:249
  9.4 2.8 %collective-permute-done.refs_4_ = bf16[64,2048]{1,0:T(8,128)(2,1)S(1)} collective-permute-done((bf16[64,2048]{1,0:T(8,128)(2,1)S(1)}, bf16[64,2048]{1,0:T(8,128)(2,1)S(1)}, u32[]{:S(2)}, u32[]{:S(2)}) %collective-permute-start) | collective-permute-done | bytes 262176 | tf_op jit(solution)/shard_map/ppermute | solution.py:249
  12.2 3.7 %collective-permute-done.5.refs_9_ = bf16[64,2176]{1,0:T(8,128)(2,1)S(1)} collective-permute-done((bf16[64,2176]{1,0:T(8,128)(2,1)S(1)}, bf16[64,2176]{1,0:T(8,128)(2,1)S(1)}, u32[]{:S(2)}, u32[]{:S(2)}) %collective-permute-start.5) | collective-permute-done | bytes 278560 | tf_op jit(solution)/shard_map/ppermute | solution.py:249
  15.9 0.7 %copy-done = bf16[64,2048]{1,0:T(8,128)(2,1)} copy-done((bf16[64,2048]{1,0:T(8,128)(2,1)}, bf16[64,2048]{1,0:T(8,128)(2,1)S(1)}, u32[]{:S(2)}) %copy-start) | copy-done | bytes 262168
  16.6 2.2 %collective-permute-done.4.refs_8_ = bf16[64,2048]{1,0:T(8,128)(2,1)} collective-permute-done((bf16[64,2048]{1,0:T(8,128)(2,1)S(1)}, bf16[64,2048]{1,0:T(8,128)(2,1)}, u32[]{:S(2)}, u32[]{:S(2)}) %collective-permute-start.4) | collective-permute-done | bytes 262176 | tf_op jit(solution)/shard_map/ppermute | solution.py:249
  18.9 0.5 %collective-permute-start.6 = (bf16[64,2048]{1,0:T(8,128)(2,1)}, bf16[64,2048]{1,0:T(8,128)(2,1)}, u32[]{:S(2)}, u32[]{:S(2)}) collective-permute-start(bf16[64,2048]{1,0:T(8,128)(2,1)} %collective-permute-done.4.refs_8_), channel_id=1, source_target_pairs={{0,1},{1,0},{2,3},{3,2},{4,5},{5,4},{6,7},{7,6},{8,9},{9,8},{10,11... | collective-permute-start | bytes 786440 | tf_op jit(solution)/shard_map/ppermute | solution.py:250
  19.4 0.7 %copy-done.2 = bf16[64,2048]{1,0:T(8,128)(2,1)} copy-done((bf16[64,2048]{1,0:T(8,128)(2,1)}, bf16[64,2048]{1,0:T(8,128)(2,1)S(1)}, u32[]{:S(2)}) %copy-start.2) | copy-done | bytes 262168
  20.1 5.4 %collective-permute-done.8.refs_12_ = bf16[64,2048]{1,0:T(8,128)(2,1)} collective-permute-done((bf16[64,2048]{1,0:T(8,128)(2,1)}, bf16[64,2048]{1,0:T(8,128)(2,1)}, u32[]{:S(2)}, u32[]{:S(2)}) %collective-permute-start.8) | collective-permute-done | bytes 262176 | tf_op jit(solution)/shard_map/ppermute | solution.py:249
  25.5 0.5 %collective-permute-start.11 = (bf16[64,2176]{1,0:T(8,128)(2,1)}, bf16[64,2176]{1,0:T(8,128)(2,1)}, u32[]{:S(2)}, u32[]{:S(2)}) collective-permute-start(bf16[64,2176]{1,0:T(8,128)(2,1)} %collective-permute-done.9.refs_13_), channel_id=1, source_target_pairs={{0,1},{1,0},{2,3},{3,2},{4,5},{5,4},{6,7},{7,6},{8,9},{9,8},{10,11... | collective-permute-start | bytes 835592 | tf_op jit(solution)/shard_map/ppermute | solution.py:250
  26.1 1.7 %slice_bitcast_fusion = (bf16[256,2048]{1,0:T(8,128)(2,1)S(1)}, bf16[256,2048]{1,0:T(8,128)(2,1)S(1)}) fusion(bf16[1,512,2048]{2,1,0:T(8,128)(2,1)} %param.5), kind=kLoop, calls=%fused_computation | loop fusion | bytes 4194304 | tf_op jit(solution)/shard_map/slice | solution.py:246
  27.7 0.1 reshape.7
  27.9 0.9 %copy-done.1 = bf16[64,2048]{1,0:T(8,128)(2,1)S(1)} copy-done((bf16[64,2048]{1,0:T(8,128)(2,1)S(1)}, bf16[64,2048]{1,0:T(8,128)(2,1)}, u32[]{:S(2)}) %copy-start.1) | copy-done | bytes 262168
  28.9 0.9 %copy-done.3 = bf16[64,2048]{1,0:T(8,128)(2,1)S(1)} copy-done((bf16[64,2048]{1,0:T(8,128)(2,1)S(1)}, bf16[64,2048]{1,0:T(8,128)(2,1)}, u32[]{:S(2)}) %copy-start.3) | copy-done | bytes 262168
  29.8 0.2 shard_map.55
  30.1 3.0 %collective-permute-start.12 = (s16[528,128]{1,0:T(8,128)(2,1)S(1)}, s16[528,128]{1,0:T(8,128)(2,1)S(1)}, u32[]{:S(2)}, u32[]{:S(2)}) collective-permute-start(s16[528,128]{1,0:T(8,128)(2,1)S(1)} %shard_map.55), channel_id=1, source_target_pairs={{0,2},{2,0},{1,3},{3,1},{4,6},{6,4},{5,7},{7,5},{8,10},{10,8},{9,1... | collective-permute-start | bytes 405512 | tf_op jit(solution)/shard_map/ppermute | solution.py:272
  33.0 2.2 %shard_map.57 = s16[528,128]{1,0:T(8,128)(2,1)S(1)} custom-call(s32[1,8]{1,0:T(1,128)S(1)} %pad_add_fusion.packed, bf16[256,2048]{1,0:T(8,128)(2,1)S(1)} %get-tuple-element.10.refs_0_, bf16[256,2048]{1,0:T(8,128)(2,1)S(1)} %get-tuple-element.9.refs_1_, bf16[64,2048]{1,0:T(8,128)(2,1)S(1)} %get-tuple-element.12.refs_2_, ...), custom_call_target="tpu_custom_call" | custom-call | flops 268435456 | bytes 2097152 | tf_op jit(solution)/shard_map/pallas_call | solution.py:259
  35.3 1.0 %collective-permute-done.12.refs_16_ = s16[528,128]{1,0:T(8,128)(2,1)S(1)} collective-permute-done((s16[528,128]{1,0:T(8,128)(2,1)S(1)}, s16[528,128]{1,0:T(8,128)(2,1)S(1)}, u32[]{:S(2)}, u32[]{:S(2)}) %collective-permute-start.12) | collective-permute-done | bytes 135200 | tf_op jit(solution)/shard_map/ppermute | solution.py:272
  36.3 1.9 %shard_map.56 = (f32[512,256]{1,0:T(8,128)}, f32[512,128]{1,0:T(8,128)S(1)}) custom-call(s32[1,8]{1,0:T(1,128)S(1)} %pad_add_fusion.packed, bf16[256,2048]{1,0:T(8,128)(2,1)S(1)} %get-tuple-element.10.refs_0_, bf16[256,2048]{1,0:T(8,128)(2,1)S(1)} %get-tuple-element.9.refs_1_, bf16[64,2048]{1,0:T(8,128)(2,1)S(1)} %get-tuple-element.12.refs_2_, ...), custom_call_target="tpu_custom_call" | custom-call | flops 536870912 | bytes 2097152 | tf_op jit(solution)/shard_map/pallas_call | solution.py:274
  38.2 2.1 %collective-permute-done.13.refs_0_ = s16[528,128]{1,0:T(8,128)(2,1)S(1)} collective-permute-done((s16[528,128]{1,0:T(8,128)(2,1)S(1)}, s16[528,128]{1,0:T(8,128)(2,1)S(1)}, u32[]{:S(2)}, u32[]{:S(2)}) %collective-permute-start.13) | collective-permute-done | bytes 135200 | tf_op jit(solution)/shard_map/ppermute | solution.py:272
  40.3 0.8 %shard_map.58 = f32[512,256]{1,0:T(8,128)} custom-call(s32[1,8]{1,0:T(1,128)S(1)} %pad_add_fusion.packed, f32[512,256]{1,0:T(8,128)} %get-tuple-element.7.acc_ref, f32[512,128]{1,0:T(8,128)S(1)} %get-tuple-element.8.last_ref, s16[528,128]{1,0:T(8,128)(2,1)S(1)} %collective-permute-done.13.refs_0_), custom_call_target="tpu_custom_call", output_to_operand_aliasing={{}: (1, {})} | custom-call | tf_op jit(solution)/shard_map/pallas_call | solution.py:288
  (26 shorter events, 0.3 us)
Async XLA Ops:
  1.8 7.6 %collective-permute-start.1 = (bf16[64,2176]{1,0:T(8,128)(2,1)S(1)}, bf16[64,2176]{1,0:T(8,128)(2,1)S(1)}, u32[]{:S(2)}, u32[]{:S(2)}) collective-permute-start(bf16[64,2176]{1,0:T(8,128)(2,1)S(1)} %pad_maximum_fusion.refs_3_), channel_id=1, source_target_pairs={{1,5},{5,9},{9,13},{13,12},{12,8},{8,4},{4,0},{0,1},{3,7},{7,11},{... | collective-permute-start | bytes 835592 | tf_op jit(solution)/shard_map/ppermute | solution.py:249
  2.3 25.4 %copy-start.4 = (s32[2,2]{1,0:T(2,128)S(1)}, s32[2,2]{1,0:T(2,128)}, u32[]{:S(2)}) copy-start(s32[2,2]{1,0:T(2,128)} %param.8) | copy-start | bytes 52
  2.3 25.5 %copy-start.5 = (s32[4]{0:T(128)S(1)}, s32[4]{0:T(128)}, u32[]{:S(2)}) copy-start(s32[4]{0:T(128)} %param.9) | copy-start | bytes 52
  2.3 9.9 %collective-permute-start = (bf16[64,2048]{1,0:T(8,128)(2,1)S(1)}, bf16[64,2048]{1,0:T(8,128)(2,1)S(1)}, u32[]{:S(2)}, u32[]{:S(2)}) collective-permute-start(bf16[64,2048]{1,0:T(8,128)(2,1)S(1)} %get-tuple-element.12.refs_2_), channel_id=1, source_target_pairs={{1,5},{5,9},{9,13},{13,12},{12,8},{8,4},{4,0},{0,1},{3,7},{7,11},{... | collective-permute-start | bytes 786440 | tf_op jit(solution)/shard_map/ppermute | solution.py:249
  9.4 6.5 %collective-permute-start.5 = (bf16[64,2176]{1,0:T(8,128)(2,1)S(1)}, bf16[64,2176]{1,0:T(8,128)(2,1)S(1)}, u32[]{:S(2)}, u32[]{:S(2)}) collective-permute-start(bf16[64,2176]{1,0:T(8,128)(2,1)S(1)} %collective-permute-done.1.refs_5_), channel_id=1, source_target_pairs={{1,5},{5,9},{9,13},{13,12},{12,8},{8,4},{4,0},{0,1},{3,7},{7,11},{... | collective-permute-start | bytes 835592 | tf_op jit(solution)/shard_map/ppermute | solution.py:249
  12.2 6.7 %collective-permute-start.4 = (bf16[64,2048]{1,0:T(8,128)(2,1)S(1)}, bf16[64,2048]{1,0:T(8,128)(2,1)}, u32[]{:S(2)}, u32[]{:S(2)}) collective-permute-start(bf16[64,2048]{1,0:T(8,128)(2,1)S(1)} %collective-permute-done.refs_4_), channel_id=1, source_target_pairs={{1,5},{5,9},{9,13},{13,12},{12,8},{8,4},{4,0},{0,1},{3,7},{7,11},{... | collective-permute-start | bytes 786440 | tf_op jit(solution)/shard_map/ppermute | solution.py:249
  15.9 9.6 %collective-permute-start.9 = (bf16[64,2176]{1,0:T(8,128)(2,1)S(1)}, bf16[64,2176]{1,0:T(8,128)(2,1)}, u32[]{:S(2)}, u32[]{:S(2)}) collective-permute-start(bf16[64,2176]{1,0:T(8,128)(2,1)S(1)} %collective-permute-done.5.refs_9_), channel_id=1, source_target_pairs={{1,5},{5,9},{9,13},{13,12},{12,8},{8,4},{4,0},{0,1},{3,7},{7,11},{... | collective-permute-start | bytes 835592 | tf_op jit(solution)/shard_map/ppermute | solution.py:249
  15.9 3.4 %collective-permute-start.2 = (bf16[64,2048]{1,0:T(8,128)(2,1)S(1)}, bf16[64,2048]{1,0:T(8,128)(2,1)S(1)}, u32[]{:S(2)}, u32[]{:S(2)}) collective-permute-start(bf16[64,2048]{1,0:T(8,128)(2,1)S(1)} %collective-permute-done.refs_4_), channel_id=1, source_target_pairs={{0,1},{1,0},{2,3},{3,2},{4,5},{5,4},{6,7},{7,6},{8,9},{9,8},{10,11... | collective-permute-start | bytes 786440 | tf_op jit(solution)/shard_map/ppermute | solution.py:250
  15.9 0.7 %copy-start = (bf16[64,2048]{1,0:T(8,128)(2,1)}, bf16[64,2048]{1,0:T(8,128)(2,1)S(1)}, u32[]{:S(2)}) copy-start(bf16[64,2048]{1,0:T(8,128)(2,1)S(1)} %collective-permute-done.refs_4_) | copy-start | bytes 786436
  18.8 6.7 %collective-permute-start.8 = (bf16[64,2048]{1,0:T(8,128)(2,1)}, bf16[64,2048]{1,0:T(8,128)(2,1)}, u32[]{:S(2)}, u32[]{:S(2)}) collective-permute-start(bf16[64,2048]{1,0:T(8,128)(2,1)} %collective-permute-done.4.refs_8_), channel_id=1, source_target_pairs={{1,5},{5,9},{9,13},{13,12},{12,8},{8,4},{4,0},{0,1},{3,7},{7,11},{... | collective-permute-start | bytes 786440 | tf_op jit(solution)/shard_map/ppermute | solution.py:249
  18.9 9.1 %collective-permute-start.3 = (bf16[64,2176]{1,0:T(8,128)(2,1)S(1)}, bf16[64,2176]{1,0:T(8,128)(2,1)S(1)}, u32[]{:S(2)}, u32[]{:S(2)}) collective-permute-start(bf16[64,2176]{1,0:T(8,128)(2,1)S(1)} %collective-permute-done.1.refs_5_), channel_id=1, source_target_pairs={{0,1},{1,0},{2,3},{3,2},{4,5},{5,4},{6,7},{7,6},{8,9},{9,8},{10,11... | collective-permute-start | bytes 835592 | tf_op jit(solution)/shard_map/ppermute | solution.py:250
  18.9 9.0 %collective-permute-start.6 = (bf16[64,2048]{1,0:T(8,128)(2,1)}, bf16[64,2048]{1,0:T(8,128)(2,1)}, u32[]{:S(2)}, u32[]{:S(2)}) collective-permute-start(bf16[64,2048]{1,0:T(8,128)(2,1)} %collective-permute-done.4.refs_8_), channel_id=1, source_target_pairs={{0,1},{1,0},{2,3},{3,2},{4,5},{5,4},{6,7},{7,6},{8,9},{9,8},{10,11... | collective-permute-start | bytes 786440 | tf_op jit(solution)/shard_map/ppermute | solution.py:250
  19.4 0.7 %copy-start.2 = (bf16[64,2048]{1,0:T(8,128)(2,1)}, bf16[64,2048]{1,0:T(8,128)(2,1)S(1)}, u32[]{:S(2)}) copy-start(bf16[64,2048]{1,0:T(8,128)(2,1)S(1)} %collective-permute-done.2.refs_6_) | copy-start | bytes 786436
  20.1 7.8 %collective-permute-start.7 = (bf16[64,2176]{1,0:T(8,128)(2,1)S(1)}, bf16[64,2176]{1,0:T(8,128)(2,1)}, u32[]{:S(2)}, u32[]{:S(2)}) collective-permute-start(bf16[64,2176]{1,0:T(8,128)(2,1)S(1)} %collective-permute-done.5.refs_9_), channel_id=1, source_target_pairs={{0,1},{1,0},{2,3},{3,2},{4,5},{5,4},{6,7},{7,6},{8,9},{9,8},{10,11... | collective-permute-start | bytes 835592 | tf_op jit(solution)/shard_map/ppermute | solution.py:250
  25.5 7.5 %collective-permute-start.10 = (bf16[64,2048]{1,0:T(8,128)(2,1)}, bf16[64,2048]{1,0:T(8,128)(2,1)}, u32[]{:S(2)}, u32[]{:S(2)}) collective-permute-start(bf16[64,2048]{1,0:T(8,128)(2,1)} %collective-permute-done.8.refs_12_), channel_id=1, source_target_pairs={{0,1},{1,0},{2,3},{3,2},{4,5},{5,4},{6,7},{7,6},{8,9},{9,8},{10,11... | collective-permute-start | bytes 786440 | tf_op jit(solution)/shard_map/ppermute | solution.py:250
  25.5 7.5 %collective-permute-start.11 = (bf16[64,2176]{1,0:T(8,128)(2,1)}, bf16[64,2176]{1,0:T(8,128)(2,1)}, u32[]{:S(2)}, u32[]{:S(2)}) collective-permute-start(bf16[64,2176]{1,0:T(8,128)(2,1)} %collective-permute-done.9.refs_13_), channel_id=1, source_target_pairs={{0,1},{1,0},{2,3},{3,2},{4,5},{5,4},{6,7},{7,6},{8,9},{9,8},{10,11... | collective-permute-start | bytes 835592 | tf_op jit(solution)/shard_map/ppermute | solution.py:250
  27.9 1.0 %copy-start.1 = (bf16[64,2048]{1,0:T(8,128)(2,1)S(1)}, bf16[64,2048]{1,0:T(8,128)(2,1)}, u32[]{:S(2)}) copy-start(bf16[64,2048]{1,0:T(8,128)(2,1)} %copy-done) | copy-start | bytes 786436
  28.9 0.9 %copy-start.3 = (bf16[64,2048]{1,0:T(8,128)(2,1)S(1)}, bf16[64,2048]{1,0:T(8,128)(2,1)}, u32[]{:S(2)}) copy-start(bf16[64,2048]{1,0:T(8,128)(2,1)} %copy-done.2) | copy-start | bytes 786436
  30.1 6.2 %collective-permute-start.12 = (s16[528,128]{1,0:T(8,128)(2,1)S(1)}, s16[528,128]{1,0:T(8,128)(2,1)S(1)}, u32[]{:S(2)}, u32[]{:S(2)}) collective-permute-start(s16[528,128]{1,0:T(8,128)(2,1)S(1)} %shard_map.55), channel_id=1, source_target_pairs={{0,2},{2,0},{1,3},{3,1},{4,6},{6,4},{5,7},{7,5},{8,10},{10,8},{9,1... | collective-permute-start | bytes 405512 | tf_op jit(solution)/shard_map/ppermute | solution.py:272
  35.2 5.1 %collective-permute-start.13 = (s16[528,128]{1,0:T(8,128)(2,1)S(1)}, s16[528,128]{1,0:T(8,128)(2,1)S(1)}, u32[]{:S(2)}, u32[]{:S(2)}) collective-permute-start(s16[528,128]{1,0:T(8,128)(2,1)S(1)} %shard_map.57), channel_id=1, source_target_pairs={{0,2},{2,0},{1,3},{3,1},{4,6},{6,4},{5,7},{7,5},{8,10},{10,8},{9,1... | collective-permute-start | bytes 405512 | tf_op jit(solution)/shard_map/ppermute | solution.py:272

commit v6 on v5

--- a/solution.py
+++ b/solution.py
@@ -14,6 +14,7 @@
 LIMIT = 20 * 2**20
 STEPS = 32767.0
 TAIL = 16
+WEIGHT_STEPS = 16384.0
 
 
 def fold_ring(n):
@@ -118,6 +119,30 @@
     return steps * (jnp.exp2(power) * (1.0 / STEPS))
 
 
+def put_coded(out, b, span, count, tile):
+    steps, power = coded(tile)
+    out[span, :] = steps
+    line = lax.broadcasted_iota(jnp.int32, (TAIL, tile.shape[1]), 0)
+    old = out[pl.ds(count, TAIL), :].astype(jnp.int32)
+    out[pl.ds(count, TAIL), :] = jnp.where(line == b, power.astype(jnp.int32), old).astype(jnp.int16)
+
+
+def score_slot(pairs, block, qs, rows, weight, out):
+    qblk, count = qs[0].shape[0], len(qs) * qs[0].shape[0]
+    out[pl.ds(count, TAIL), :] = jnp.zeros((TAIL, out.shape[1]), jnp.int16)
+    for b in range(len(qs)):
+        span = pl.ds(b * qblk, qblk)
+        wanted = listed(pairs, b, block)
+
+        @pl.when(wanted)
+        def _():
+            put_coded(out, b, span, count, dot_rows(qs[b][...], rows[...]) * weight)
+
+        @pl.when(jnp.logical_not(wanted))
+        def _():
+            out[span, :] = jnp.zeros((qblk, out.shape[1]), jnp.int16)
+
+
 def slot_kernel(sizes, s, dists, chunks, packed, *refs):
     n, ckpts, per, nb, cand = sizes
     qs, ins = refs[:nb], refs[nb : -(ckpts - 1) - 3]
@@ -125,32 +150,166 @@
     rows, w_rows, sems = refs[-3:]
     z, c = lax.axis_index("blk"), lax.axis_index("ckpt")
     pairs, order = scalars(n, nb, cand, packed)
-    qblk, width = qs[0].shape[0], rows.shape[0]
-    count = nb * qblk
     pool = sources(dists, chunks, ins)
     for r in range(1, ckpts):
         owner = lax.rem(c + r, ckpts)
-        owned = [pick(order[k::per], owner) for k in range(per)]
-        block = pick_ranked(owned, z, s)
-        fetch(block, pool, rows, w_rows, sems)
-        weight = fetched(rows, w_rows, sems)
-        out = outs[r - 1]
-        out[pl.ds(count, TAIL), :] = jnp.zeros((TAIL, width), jnp.int16)
-        for b in range(nb):
-            span = pl.ds(b * qblk, qblk)
-            wanted = listed(pairs, b, block)
-
-            @pl.when(wanted)
-            def _():
-                steps, power = coded(dot_rows(qs[b][...], rows[...]) * weight)
-                out[span, :] = steps
-                line = lax.broadcasted_iota(jnp.int32, (TAIL, width), 0)
-                old = out[pl.ds(count, TAIL), :].astype(jnp.int32)
-                out[pl.ds(count, TAIL), :] = jnp.where(line == b, power.astype(jnp.int32), old).astype(jnp.int16)
-
-            @pl.when(jnp.logical_not(wanted))
-            def _():
-                out[span, :] = jnp.zeros((qblk, width), jnp.int16)
+        block = pick_ranked([pick(order[k::per], owner) for k in range(per)], z, s)
+
+        @pl.when(jnp.abs(block - z) <= dists[-1])
+        def _():
+            fetch(block, pool, rows, w_rows, sems)
+            weight = fetched(rows, w_rows, sems)
+            score_slot(pairs, block, qs, rows, weight, outs[r - 1])
+
+
+def late_kernel(sizes, s, dist, chunks, packed, *refs):
+    n, ckpts, per, nb, cand = sizes
+    qs, ins = refs[:nb], refs[nb : nb + 2 * chunks]
+    before, outs, rows = refs[nb + 2 * chunks : -ckpts], refs[-ckpts:-1], refs[-1]
+    z, c = lax.axis_index("blk"), lax.axis_index("ckpt")
+    pairs, order = scalars(n, nb, cand, packed)
+    feats = rows.shape[1]
+    for r in range(1, ckpts):
+        owner = lax.rem(c + r, ckpts)
+        block = pick_ranked([pick(order[k::per], owner) for k in range(per)], z, s)
+        late = jnp.abs(block - z) == dist
+
+        @pl.when(late)
+        def _():
+            weight = jnp.zeros((1, outs[0].shape[1]), jnp.float32)
+            for held, parts in sources((dist,), chunks, ins):
+
+                @pl.when(held == block)
+                def _():
+                    at = 0
+                    for part in parts:
+                        rows[pl.ds(at, part.shape[0]), :] = part[:, pl.ds(0, feats)]
+                        at += part.shape[0]
+
+                tail = parts[-1][pl.ds(0, TAIL), pl.ds(feats, outs[0].shape[1])].astype(jnp.float32)[:1]
+                weight = jnp.where(held == block, tail, weight)
+            score_slot(pairs, block, qs, rows, weight, outs[r - 1])
+
+        @pl.when(jnp.logical_not(late))
+        def _():
+            outs[r - 1][...] = before[r - 1][...]
+
+
+def regroup(tiles, index, width):
+    group = lax.broadcasted_iota(jnp.int32, tiles[0].shape, 1) // width
+    total = jnp.zeros_like(tiles[0])
+    for k, tile in enumerate(tiles):
+        by = (k - index) * width % tile.shape[1]
+        total = total + jnp.where(group == k, pltpu.roll(tile, by, 1) if by else tile, 0.0)
+    return total
+
+
+def put_piece(tiles, out, weight):
+    qblk = tiles[0].shape[0]
+    tail = jnp.broadcast_to(jnp.round(weight * WEIGHT_STEPS), (TAIL, weight.shape[1])).astype(jnp.int32)
+    line = lax.broadcasted_iota(jnp.int32, tail.shape, 0)
+    for k, tile in enumerate(tiles):
+        steps, power = coded(tile)
+        out[pl.ds(k * qblk, qblk), :] = steps
+        tail = jnp.where(line == k, power.astype(jnp.int32), tail)
+    out[pl.ds(len(tiles) * qblk, TAIL), :] = tail.astype(jnp.int16)
+
+
+def packed_pieces(part_refs, nb):
+    chunks, width = len(part_refs), part_refs[0].shape[1]
+    groups = nb // chunks
+    qblk = (part_refs[0].shape[0] - TAIL) // groups
+    tails = [ref[pl.ds(groups * qblk, TAIL), :].astype(jnp.int32).astype(jnp.float32) for ref in part_refs]
+    weight = tails[-1][TAIL - 1 :] * (1.0 / WEIGHT_STEPS)
+    found = []
+    for b in range(nb):
+        k = b // chunks
+        tiles = []
+        for ref, tail in zip(part_refs, tails):
+            steps = ref[pl.ds(k * qblk, qblk), :].astype(jnp.int32).astype(jnp.float32)
+            tiles.append(steps * (jnp.exp2(tail[k : k + 1]) * (1.0 / STEPS)))
+        found.append(regroup(tiles, b % chunks, width // chunks) * weight)
+    return found
+
+
+def far_kernel(sizes, dists, chunks, packed, *refs):
+    n, ckpts, per, nb, cand = sizes
+    many = (ckpts - 1) * chunks
+    qs, ins, outs = refs[:nb], refs[nb : -many - 4], refs[-many - 4 : -4]
+    rows, w_rows, tiles, sems = refs[-4:]
+    z, c = lax.axis_index("blk"), lax.axis_index("ckpt")
+    pairs, order = scalars(n, nb, cand, packed)
+    pool = sources(dists, chunks, ins)
+    for r in range(1, ckpts):
+        owner = lax.rem(c + r, ckpts)
+        block = pick_ranked([pick(order[k::per], owner) for k in range(per)], z, per - 1)
+
+        @pl.when(jnp.abs(block - z) <= dists[-1])
+        def _():
+            fetch(block, pool, rows, w_rows, sems)
+            weight = fetched(rows, w_rows, sems)
+            score_tiles(pairs, block, qs, rows, tiles)
+            for i in range(chunks):
+                groups = [
+                    regroup([tiles[k * chunks + j] for j in range(chunks)], i, rows.shape[0] // chunks)
+                    for k in range(nb // chunks)
+                ]
+                put_piece(groups, outs[(r - 1) * chunks + i], weight)
+
+
+def score_tiles(pairs, block, qs, rows, tiles):
+    for b in range(len(qs)):
+        wanted = listed(pairs, b, block)
+
+        @pl.when(wanted)
+        def _():
+            tiles[b] = dot_rows(qs[b][...], rows[...])
+
+        @pl.when(jnp.logical_not(wanted))
+        def _():
+            tiles[b] = jnp.zeros_like(tiles[b])
+
+
+def piece_kernel(sizes, i, dist, chunks, packed, *refs):
+    n, ckpts, per, nb, cand = sizes
+    qs, ins = refs[:nb], refs[nb : nb + 2]
+    before, outs = refs[nb + 2 : nb + 1 + ckpts], refs[nb + 1 + ckpts : -2]
+    rows, tiles = refs[-2:]
+    z, c = lax.axis_index("blk"), lax.axis_index("ckpt")
+    pairs, order = scalars(n, nb, cand, packed)
+    width, feats = rows.shape
+    piece = width // chunks
+    for r in range(1, ckpts):
+        owner = lax.rem(c + r, ckpts)
+        block = pick_ranked([pick(order[k::per], owner) for k in range(per)], z, per - 1)
+        late = jnp.abs(block - z) == dist
+
+        @pl.when(late)
+        def _():
+            weight = jnp.ones((1, width), jnp.float32)
+            for held, (part,) in sources((dist,), 1, ins):
+
+                @pl.when(held == block)
+                def _():
+                    for j in range(chunks):
+                        rows[pl.ds(j * piece, piece), :] = part[:, pl.ds(0, feats)]
+
+                if i == chunks - 1:
+                    tag = part[pl.ds(0, TAIL), pl.ds(feats, width)].astype(jnp.float32)[:1]
+                    weight = jnp.where(held == block, tag, weight)
+            score_tiles(pairs, block, qs, rows, tiles)
+            group = lax.broadcasted_iota(jnp.int32, tiles.shape[1:], 1) // piece
+            groups = []
+            for k in range(nb // chunks):
+                total = tiles[k * chunks]
+                for j in range(1, chunks):
+                    total = jnp.where(group == j, tiles[k * chunks + j], total)
+                groups.append(total)
+            put_piece(groups, outs[r - 1], weight)
+
+        @pl.when(jnp.logical_not(late))
+        def _():
+            outs[r - 1][...] = before[r - 1][...]
 
 
 def own_kernel(sizes, dists, chunks, packed, *refs):
@@ -202,7 +361,7 @@
 
 
 def sum_kernel(sizes, packed, acc_ref, last_ref, *refs):
-    n, _, per, nb, cand = sizes
+    n, ckpts, per, nb, cand = sizes
     came, out, tile, sems = refs[:-3], refs[-3], refs[-2], refs[-1]
     z, c = lax.axis_index("blk"), lax.axis_index("ckpt")
     _, order = scalars(n, nb, cand, packed)
@@ -211,11 +370,13 @@
     owned = [pick(order[k::per], c) for k in range(per)]
     block = pick_ranked(owned, z, per - 1)
     stores = []
+    chunks = len(came) // (ckpts - 1)
+    parts = [packed_pieces(came[r * chunks : (r + 1) * chunks], nb) for r in range(ckpts - 1)]
     for b in range(nb):
         span = pl.ds(b * qblk, qblk)
         total = last_ref[span, :]
-        for part in came:
-            total = total + decoded(part, b, span, count)
+        for part in parts:
+            total = total + part[b]
         tile[span, :] = total
         stores.append(put_columns(tile, out, owned, block, sems.at[b], span))
         stores[-1].start()
@@ -253,8 +414,10 @@
     acc = jax.ShapeDtypeStruct((count, per * rows), jnp.float32)
     flops = 2 * count * rows * feats
     came = []
-    for s in range(per):
-        dists = tuple(range(n - per + s + 1))
+    cost = pl.CostEstimate(flops=flops * (ckpts - 1), bytes_accessed=count * feats * 2, transcendentals=0)
+    for s in range(per - 1):
+        seen = n - per + max(s - 1, 0)
+        dists = tuple(range(seen + 1))
         pool = [ref for d in dists for ref in near[d]]
         terms = pl.pallas_call(
             functools.partial(slot_kernel, sizes, s, dists, chunks),
@@ -267,9 +430,54 @@
                 pltpu.SemaphoreType.DMA((2,)),
             ],
             compiler_params=params,
-            cost_estimate=pl.CostEstimate(flops=flops * (ckpts - 1), bytes_accessed=count * feats * 2, transcendentals=0),
+            cost_estimate=cost,
         )(packed, *asked, *pool)
+        if s > 0:
+            terms = pl.pallas_call(
+                functools.partial(late_kernel, sizes, s, seen + 1, chunks),
+                out_shape=[sent] * (ckpts - 1),
+                in_specs=[VMEM] + [VMEM] * (nb + 2 * chunks + ckpts - 1),
+                out_specs=[VMEM] * (ckpts - 1),
+                scratch_shapes=[pltpu.VMEM((rows, feats), jnp.bfloat16)],
+                compiler_params=params,
+                cost_estimate=cost,
+            )(packed, *asked, *near[seen + 1], *terms)
         came.append([lax.ppermute(terms[r - 1], "ckpt", shift(ckpts, r)) for r in range(1, ckpts)])
+    seen = n - 2
+    dists = tuple(range(seen + 1))
+    pool = [ref for d in dists for ref in near[d]]
+    sent = jax.ShapeDtypeStruct((count // chunks + TAIL, rows), jnp.int16)
+    tiles = pltpu.VMEM((nb, qblk, rows), jnp.float32)
+    terms = pl.pallas_call(
+        functools.partial(far_kernel, sizes, dists, chunks),
+        out_shape=[sent] * ((ckpts - 1) * chunks),
+        in_specs=[VMEM] * (1 + nb) + [ANY] * len(pool),
+        out_specs=[VMEM] * ((ckpts - 1) * chunks),
+        scratch_shapes=[
+            pltpu.VMEM((rows, feats), jnp.bfloat16),
+            pltpu.VMEM((TAIL, rows), jnp.bfloat16),
+            tiles,
+            pltpu.SemaphoreType.DMA((2,)),
+        ],
+        compiler_params=params,
+        cost_estimate=cost,
+    )(packed, *asked, *pool)
+    pieces = {}
+    for i in range(chunks):
+        done = pl.pallas_call(
+            functools.partial(piece_kernel, sizes, i, seen + 1, chunks),
+            out_shape=[sent] * (ckpts - 1),
+            in_specs=[VMEM] * (1 + nb + 2 + ckpts - 1),
+            out_specs=[VMEM] * (ckpts - 1),
+            scratch_shapes=[pltpu.VMEM((rows, feats), jnp.bfloat16), tiles],
+            compiler_params=params,
+            cost_estimate=cost,
+        )(packed, *asked, near[seen + 1][i], near[seen + 1][chunks + i], *terms[i::chunks])
+        for r in range(1, ckpts):
+            pieces[r, i] = lax.ppermute(done[r - 1], "ckpt", shift(ckpts, r))
+    came.append([pieces[r, i] for r in range(1, ckpts) for i in range(chunks)])
+    dists = tuple(range(n))
+    pool = [ref for d in dists for ref in near[d]]
     early = [part for parts in came[:-1] for part in parts]
     total, last = pl.pallas_call(
         functools.partial(own_kernel, sizes, dists, chunks),
@@ -288,7 +496,7 @@
     return pl.pallas_call(
         functools.partial(sum_kernel, sizes),
         out_shape=acc,
-        in_specs=[VMEM, ANY, VMEM] + [VMEM] * (ckpts - 1),
+        in_specs=[VMEM, ANY, VMEM] + [VMEM] * len(came[-1]),
         out_specs=ANY,
         input_output_aliases={1: 0},
         scratch_shapes=[pltpu.VMEM((count, rows), jnp.float32), pltpu.SemaphoreType.DMA((nb,))],

time: 41.4 us -> 43.3 us (1.046)
  Pallas kernels: 5.1 us -> 7.36 us
  waiting for transfers between devices: 22.3 us -> 20.8 us
  starting transfers between devices: 6.73 us -> 7.83 us
    pallas_call x0 -> x3, Pallas kernels: none -> 4.41 us  [the longest x2 4.27 us: per_device(): pl.pallas_call(functools.partial(piece_kernel, sizes, i, seen + 1, chunks...]
    ppermute x2 -> x1, waiting for transfers between devices: 3.12 us -> 0.01 us  [per_device(): lax.ppermute(terms[r - 1], 'ckpt', shift(ckpts, r))]
    pallas_call x2 -> x1, Pallas kernels: 2.4 us -> 0.24 us  [per_device(): pl.pallas_call(functools.partial(slot_kernel, sizes, s, dists, chunks), o...]
    ppermute x0 -> x2, waiting for transfers between devices: none -> 1.62 us  [per_device(): pieces[r, i] = lax.ppermute(done[r - 1], 'ckpt', shift(ckpts, r))]
    ppermute x0 -> x2, starting transfers between devices: none -> 1.18 us  [per_device(): pieces[r, i] = lax.ppermute(done[r - 1], 'ckpt', shift(ckpts, r))]
    ppermute x2 -> x1, starting transfers between devices: 3.02 us -> 2.95 us  [per_device(): lax.ppermute(terms[r - 1], 'ckpt', shift(ckpts, r))]
  transfers between devices with their start and end apart: 14 -> 15, of which waited for: 7 -> 6; matrix products, arithmetic and copies ran while one was open for 4% -> 4% of each run, Pallas kernels for 10% -> 15%
where the time goes in v6:
time: 43.3 us; the launch traced here: 43 us
  waiting for transfers between devices  20.8 us (48%)
  starting transfers between devices  7.83 us (18%)
  Pallas kernels  7.36 us (17%)
  local copies, waits for them, and re-layouts  6.78 us (16%)
    ppermute x6, waiting for transfers between devices, per_device(): held = [lax.ppermute(part, lines, ring) for part in held]  19.1 us
    pallas_call x2, Pallas kernels, per_device(): pl.pallas_call(functools.partial(piece_kernel, sizes, i, seen + 1, chunks...  4.27 us
    unnamed x12, local copies, waits for them, and re-layouts  3.3 us
    ppermute x1, starting transfers between devices, per_device(): lax.ppermute(terms[r - 1], 'ckpt', shift(ckpts, r))  2.95 us
    ppermute x6, starting transfers between devices, per_device(): held = [lax.ppermute(part, lines, ring) for part in held]  2.63 us
    pallas_call x1, Pallas kernels, per_device(): pl.pallas_call(functools.partial(own_kernel, sizes, dists, chunks), out_s...  1.87 us
    slice x1, local copies, waits for them, and re-layouts, per_device(): asked.append(queries[b * qblk:(b + 1) * qblk])  1.68 us
    ppermute x2, waiting for transfers between devices, per_device(): pieces[r, i] = lax.ppermute(done[r - 1], 'ckpt', shift(ckpts, r))  1.62 us
  transfers between devices with their start and end apart: 15, of which 6 were waited for; matrix products, arithmetic and copies ran while one was open for 4% of the time, Pallas kernels for 15%

profile of v6, /device:TPU:0, one launch (start us, length us, event | category | flops | bytes accessed | tf_op | source)
XLA Modules:
  0.0 43.0 jit_solution(11863654512449441613)
XLA Ops:
  0.0 1.1 %slice_bitcast_fusion.2 = (bf16[64,2048]{1,0:T(8,128)(2,1)S(1)}, bf16[64,2048]{1,0:T(8,128)(2,1)S(1)}) fusion(bf16[1,128,2048]{2,1,0:T(8,128)(2,1)} %param.6), kind=kLoop, calls=%fused_computation.3 | loop fusion | bytes 1048576 | tf_op jit(solution)/shard_map/slice | solution.py:400
  1.1 0.7 %pad.1.clone = bf16[2176]{0:T(1024)(128)(2,1)S(1)} pad(bf16[128]{0:T(256)(128)(2,1)} %bitcast.10, bf16[]{:T(256)} %constant.4), padding=2048_0 | pad | bytes 4610 | tf_op jit(solution)/shard_map/concatenate | solution.py:402
  1.8 0.5 %collective-permute-start.1 = (bf16[64,2176]{1,0:T(8,128)(2,1)S(1)}, bf16[64,2176]{1,0:T(8,128)(2,1)S(1)}, u32[]{:S(2)}, u32[]{:S(2)}) collective-permute-start(bf16[64,2176]{1,0:T(8,128)(2,1)S(1)} %pad_maximum_fusion.refs_3_), channel_id=1, source_target_pairs={{1,5},{5,9},{9,13},{13,12},{12,8},{8,4},{4,0},{0,1},{3,7},{7,11},{... | collective-permute-start | bytes 835592 | tf_op jit(solution)/shard_map/ppermute | solution.py:410
  2.3 2.1 %collective-permute-start = (bf16[64,2048]{1,0:T(8,128)(2,1)S(1)}, bf16[64,2048]{1,0:T(8,128)(2,1)S(1)}, u32[]{:S(2)}, u32[]{:S(2)}) collective-permute-start(bf16[64,2048]{1,0:T(8,128)(2,1)S(1)} %get-tuple-element.16.refs_2_), channel_id=1, source_target_pairs={{1,5},{5,9},{9,13},{13,12},{12,8},{8,4},{4,0},{0,1},{3,7},{7,11},{... | collective-permute-start | bytes 786440 | tf_op jit(solution)/shard_map/ppermute | solution.py:410
  4.4 5.0 %collective-permute-done.1.refs_5_ = bf16[64,2176]{1,0:T(8,128)(2,1)S(1)} collective-permute-done((bf16[64,2176]{1,0:T(8,128)(2,1)S(1)}, bf16[64,2176]{1,0:T(8,128)(2,1)S(1)}, u32[]{:S(2)}, u32[]{:S(2)}) %collective-permute-start.1) | collective-permute-done | bytes 278560 | tf_op jit(solution)/shard_map/ppermute | solution.py:410
  9.4 2.8 %collective-permute-done.refs_4_ = bf16[64,2048]{1,0:T(8,128)(2,1)S(1)} collective-permute-done((bf16[64,2048]{1,0:T(8,128)(2,1)S(1)}, bf16[64,2048]{1,0:T(8,128)(2,1)S(1)}, u32[]{:S(2)}, u32[]{:S(2)}) %collective-permute-start) | collective-permute-done | bytes 262176 | tf_op jit(solution)/shard_map/ppermute | solution.py:410
  12.2 3.7 %collective-permute-done.5.refs_9_ = bf16[64,2176]{1,0:T(8,128)(2,1)S(1)} collective-permute-done((bf16[64,2176]{1,0:T(8,128)(2,1)S(1)}, bf16[64,2176]{1,0:T(8,128)(2,1)S(1)}, u32[]{:S(2)}, u32[]{:S(2)}) %collective-permute-start.5) | collective-permute-done | bytes 278560 | tf_op jit(solution)/shard_map/ppermute | solution.py:410
  15.9 0.7 %copy-done = bf16[64,2048]{1,0:T(8,128)(2,1)} copy-done((bf16[64,2048]{1,0:T(8,128)(2,1)}, bf16[64,2048]{1,0:T(8,128)(2,1)S(1)}, u32[]{:S(2)}) %copy-start) | copy-done | bytes 262168
  16.6 2.2 %collective-permute-done.4.refs_8_ = bf16[64,2048]{1,0:T(8,128)(2,1)} collective-permute-done((bf16[64,2048]{1,0:T(8,128)(2,1)S(1)}, bf16[64,2048]{1,0:T(8,128)(2,1)}, u32[]{:S(2)}, u32[]{:S(2)}) %collective-permute-start.4) | collective-permute-done | bytes 262176 | tf_op jit(solution)/shard_map/ppermute | solution.py:410
  18.9 0.5 %collective-permute-start.6 = (bf16[64,2048]{1,0:T(8,128)(2,1)}, bf16[64,2048]{1,0:T(8,128)(2,1)}, u32[]{:S(2)}, u32[]{:S(2)}) collective-permute-start(bf16[64,2048]{1,0:T(8,128)(2,1)} %collective-permute-done.4.refs_8_), channel_id=1, source_target_pairs={{0,1},{1,0},{2,3},{3,2},{4,5},{5,4},{6,7},{7,6},{8,9},{9,8},{10,11... | collective-permute-start | bytes 786440 | tf_op jit(solution)/shard_map/ppermute | solution.py:411
  19.4 0.7 %copy-done.2 = bf16[64,2048]{1,0:T(8,128)(2,1)} copy-done((bf16[64,2048]{1,0:T(8,128)(2,1)}, bf16[64,2048]{1,0:T(8,128)(2,1)S(1)}, u32[]{:S(2)}) %copy-start.2) | copy-done | bytes 262168
  20.1 5.4 %collective-permute-done.8.refs_12_.refs_2_ = bf16[64,2048]{1,0:T(8,128)(2,1)} collective-permute-done((bf16[64,2048]{1,0:T(8,128)(2,1)}, bf16[64,2048]{1,0:T(8,128)(2,1)}, u32[]{:S(2)}, u32[]{:S(2)}) %collective-permute-start.8) | collective-permute-done | bytes 262176 | tf_op jit(solution)/shard_map/ppermute | solution.py:410
  25.5 0.5 %collective-permute-start.11 = (bf16[64,2176]{1,0:T(8,128)(2,1)}, bf16[64,2176]{1,0:T(8,128)(2,1)}, u32[]{:S(2)}, u32[]{:S(2)}) collective-permute-start(bf16[64,2176]{1,0:T(8,128)(2,1)} %collective-permute-done.9.refs_13_.refs_2_), channel_id=1, source_target_pairs={{0,1},{1,0},{2,3},{3,2},{4,5},{5,4},{6,7},{7,6},{8,9},{9,8},{10,11... | collective-permute-start | bytes 835592 | tf_op jit(solution)/shard_map/ppermute | solution.py:411
  26.1 1.7 %slice_bitcast_fusion = (bf16[256,2048]{1,0:T(8,128)(2,1)S(1)}, bf16[256,2048]{1,0:T(8,128)(2,1)S(1)}) fusion(bf16[1,512,2048]{2,1,0:T(8,128)(2,1)} %param.5), kind=kLoop, calls=%fused_computation | loop fusion | bytes 4194304 | tf_op jit(solution)/shard_map/slice | solution.py:407
  27.9 0.9 %copy-done.1 = bf16[64,2048]{1,0:T(8,128)(2,1)S(1)} copy-done((bf16[64,2048]{1,0:T(8,128)(2,1)S(1)}, bf16[64,2048]{1,0:T(8,128)(2,1)}, u32[]{:S(2)}) %copy-start.1) | copy-done | bytes 262168
  28.9 0.9 %copy-done.3 = bf16[64,2048]{1,0:T(8,128)(2,1)S(1)} copy-done((bf16[64,2048]{1,0:T(8,128)(2,1)S(1)}, bf16[64,2048]{1,0:T(8,128)(2,1)}, u32[]{:S(2)}) %copy-start.3) | copy-done | bytes 262168
  30.1 2.9 %collective-permute-start.12 = (s16[528,128]{1,0:T(8,128)(2,1)S(1)}, s16[528,128]{1,0:T(8,128)(2,1)S(1)}, u32[]{:S(2)}, u32[]{:S(2)}) collective-permute-start(s16[528,128]{1,0:T(8,128)(2,1)S(1)} %shard_map.55), channel_id=1, source_target_pairs={{0,2},{2,0},{1,3},{3,1},{4,6},{6,4},{5,7},{7,5},{8,10},{10,8},{9,1... | collective-permute-start | bytes 405512 | tf_op jit(solution)/shard_map/ppermute | solution.py:445
  33.2 2.1 %shard_map.58 = s16[272,128]{1,0:T(8,128)(2,1)S(1)} custom-call(s32[1,8]{1,0:T(1,128)S(1)} %pad_add_fusion.packed, bf16[256,2048]{1,0:T(8,128)(2,1)S(1)} %get-tuple-element.14.refs_0_, bf16[256,2048]{1,0:T(8,128)(2,1)S(1)} %get-tuple-element.13.refs_1_, bf16[64,2048]{1,0:T(8,128)(2,1)} %collective-permute-done.8.refs_12_.refs_2_, ...), custom_call_target="tpu_custom_call" | custom-call | flops 268435456 | bytes 2097152 | tf_op jit(solution)/shard_map/pallas_call | solution.py:467
  35.3 0.3 collective-permute-start.13
  35.6 2.1 %shard_map.59 = s16[272,128]{1,0:T(8,128)(2,1)S(1)} custom-call(s32[1,8]{1,0:T(1,128)S(1)} %pad_add_fusion.packed, bf16[256,2048]{1,0:T(8,128)(2,1)S(1)} %get-tuple-element.14.refs_0_, bf16[256,2048]{1,0:T(8,128)(2,1)S(1)} %get-tuple-element.13.refs_1_, bf16[64,2176]{1,0:T(8,128)(2,1)} %collective-permute-done.9.refs_13_.refs_2_, ...), custom_call_target="tpu_custom_call" | custom-call | flops 268435456 | bytes 2097152 | tf_op jit(solution)/shard_map/pallas_call | solution.py:467
  37.8 0.9 %collective-permute-start.14 = (s16[272,128]{1,0:T(8,128)(2,1)S(1)}, s16[272,128]{1,0:T(8,128)(2,1)S(1)}, u32[]{:S(2)}, u32[]{:S(2)}) collective-permute-start(s16[272,128]{1,0:T(8,128)(2,1)S(1)} %shard_map.59), channel_id=1, source_target_pairs={{0,2},{2,0},{1,3},{3,1},{4,6},{6,4},{5,7},{7,5},{8,10},{10,8},{9,1... | collective-permute-start | bytes 208904 | tf_op jit(solution)/shard_map/ppermute | solution.py:477
  38.6 1.9 %shard_map.56 = (f32[512,256]{1,0:T(8,128)}, f32[512,128]{1,0:T(8,128)S(1)}) custom-call(s32[1,8]{1,0:T(1,128)S(1)} %pad_add_fusion.packed, bf16[256,2048]{1,0:T(8,128)(2,1)S(1)} %get-tuple-element.14.refs_0_, bf16[256,2048]{1,0:T(8,128)(2,1)S(1)} %get-tuple-element.13.refs_1_, bf16[64,2048]{1,0:T(8,128)(2,1)S(1)} %get-tuple-element.16.refs_2_, ...), custom_call_target="tpu_custom_call" | custom-call | flops 536870912 | bytes 2097152 | tf_op jit(solution)/shard_map/pallas_call | solution.py:482
  40.5 1.6 %collective-permute-done.14.refs_1_ = s16[272,128]{1,0:T(8,128)(2,1)S(1)} collective-permute-done((s16[272,128]{1,0:T(8,128)(2,1)S(1)}, s16[272,128]{1,0:T(8,128)(2,1)S(1)}, u32[]{:S(2)}, u32[]{:S(2)}) %collective-permute-start.14) | collective-permute-done | bytes 69664 | tf_op jit(solution)/shard_map/ppermute | solution.py:477
  42.1 0.8 %shard_map.60 = f32[512,256]{1,0:T(8,128)} custom-call(s32[1,8]{1,0:T(1,128)S(1)} %pad_add_fusion.packed, f32[512,256]{1,0:T(8,128)} %get-tuple-element.9.acc_ref, f32[512,128]{1,0:T(8,128)S(1)} %get-tuple-element.10.last_ref, s16[272,128]{1,0:T(8,128)(2,1)S(1)} %collective-permute-done.13.refs_0_, ...), custom_call_target="tpu_custom_call", output_to_operand_aliasing={{}: (1, {})} | custom-call | tf_op jit(solution)/shard_map/pallas_call | solution.py:496
  (30 shorter events, 0.7 us)
Async XLA Ops:
  1.8 7.6 %collective-permute-start.1 = (bf16[64,2176]{1,0:T(8,128)(2,1)S(1)}, bf16[64,2176]{1,0:T(8,128)(2,1)S(1)}, u32[]{:S(2)}, u32[]{:S(2)}) collective-permute-start(bf16[64,2176]{1,0:T(8,128)(2,1)S(1)} %pad_maximum_fusion.refs_3_), channel_id=1, source_target_pairs={{1,5},{5,9},{9,13},{13,12},{12,8},{8,4},{4,0},{0,1},{3,7},{7,11},{... | collective-permute-start | bytes 835592 | tf_op jit(solution)/shard_map/ppermute | solution.py:410
  2.3 25.4 %copy-start.4 = (s32[2,2]{1,0:T(2,128)S(1)}, s32[2,2]{1,0:T(2,128)}, u32[]{:S(2)}) copy-start(s32[2,2]{1,0:T(2,128)} %param.8) | copy-start | bytes 52
  2.3 25.5 %copy-start.5 = (s32[4]{0:T(128)S(1)}, s32[4]{0:T(128)}, u32[]{:S(2)}) copy-start(s32[4]{0:T(128)} %param.9) | copy-start | bytes 52
  2.3 9.9 %collective-permute-start = (bf16[64,2048]{1,0:T(8,128)(2,1)S(1)}, bf16[64,2048]{1,0:T(8,128)(2,1)S(1)}, u32[]{:S(2)}, u32[]{:S(2)}) collective-permute-start(bf16[64,2048]{1,0:T(8,128)(2,1)S(1)} %get-tuple-element.16.refs_2_), channel_id=1, source_target_pairs={{1,5},{5,9},{9,13},{13,12},{12,8},{8,4},{4,0},{0,1},{3,7},{7,11},{... | collective-permute-start | bytes 786440 | tf_op jit(solution)/shard_map/ppermute | solution.py:410
  9.4 6.5 %collective-permute-start.5 = (bf16[64,2176]{1,0:T(8,128)(2,1)S(1)}, bf16[64,2176]{1,0:T(8,128)(2,1)S(1)}, u32[]{:S(2)}, u32[]{:S(2)}) collective-permute-start(bf16[64,2176]{1,0:T(8,128)(2,1)S(1)} %collective-permute-done.1.refs_5_), channel_id=1, source_target_pairs={{1,5},{5,9},{9,13},{13,12},{12,8},{8,4},{4,0},{0,1},{3,7},{7,11},{... | collective-permute-start | bytes 835592 | tf_op jit(solution)/shard_map/ppermute | solution.py:410
  12.2 6.7 %collective-permute-start.4 = (bf16[64,2048]{1,0:T(8,128)(2,1)S(1)}, bf16[64,2048]{1,0:T(8,128)(2,1)}, u32[]{:S(2)}, u32[]{:S(2)}) collective-permute-start(bf16[64,2048]{1,0:T(8,128)(2,1)S(1)} %collective-permute-done.refs_4_), channel_id=1, source_target_pairs={{1,5},{5,9},{9,13},{13,12},{12,8},{8,4},{4,0},{0,1},{3,7},{7,11},{... | collective-permute-start | bytes 786440 | tf_op jit(solution)/shard_map/ppermute | solution.py:410
  15.9 9.6 %collective-permute-start.9 = (bf16[64,2176]{1,0:T(8,128)(2,1)S(1)}, bf16[64,2176]{1,0:T(8,128)(2,1)}, u32[]{:S(2)}, u32[]{:S(2)}) collective-permute-start(bf16[64,2176]{1,0:T(8,128)(2,1)S(1)} %collective-permute-done.5.refs_9_), channel_id=1, source_target_pairs={{1,5},{5,9},{9,13},{13,12},{12,8},{8,4},{4,0},{0,1},{3,7},{7,11},{... | collective-permute-start | bytes 835592 | tf_op jit(solution)/shard_map/ppermute | solution.py:410
  15.9 3.4 %collective-permute-start.2 = (bf16[64,2048]{1,0:T(8,128)(2,1)S(1)}, bf16[64,2048]{1,0:T(8,128)(2,1)S(1)}, u32[]{:S(2)}, u32[]{:S(2)}) collective-permute-start(bf16[64,2048]{1,0:T(8,128)(2,1)S(1)} %collective-permute-done.refs_4_), channel_id=1, source_target_pairs={{0,1},{1,0},{2,3},{3,2},{4,5},{5,4},{6,7},{7,6},{8,9},{9,8},{10,11... | collective-permute-start | bytes 786440 | tf_op jit(solution)/shard_map/ppermute | solution.py:411
  15.9 0.7 %copy-start = (bf16[64,2048]{1,0:T(8,128)(2,1)}, bf16[64,2048]{1,0:T(8,128)(2,1)S(1)}, u32[]{:S(2)}) copy-start(bf16[64,2048]{1,0:T(8,128)(2,1)S(1)} %collective-permute-done.refs_4_) | copy-start | bytes 786436
  18.8 6.7 %collective-permute-start.8 = (bf16[64,2048]{1,0:T(8,128)(2,1)}, bf16[64,2048]{1,0:T(8,128)(2,1)}, u32[]{:S(2)}, u32[]{:S(2)}) collective-permute-start(bf16[64,2048]{1,0:T(8,128)(2,1)} %collective-permute-done.4.refs_8_), channel_id=1, source_target_pairs={{1,5},{5,9},{9,13},{13,12},{12,8},{8,4},{4,0},{0,1},{3,7},{7,11},{... | collective-permute-start | bytes 786440 | tf_op jit(solution)/shard_map/ppermute | solution.py:410
  18.9 9.1 %collective-permute-start.3 = (bf16[64,2176]{1,0:T(8,128)(2,1)S(1)}, bf16[64,2176]{1,0:T(8,128)(2,1)S(1)}, u32[]{:S(2)}, u32[]{:S(2)}) collective-permute-start(bf16[64,2176]{1,0:T(8,128)(2,1)S(1)} %collective-permute-done.1.refs_5_), channel_id=1, source_target_pairs={{0,1},{1,0},{2,3},{3,2},{4,5},{5,4},{6,7},{7,6},{8,9},{9,8},{10,11... | collective-permute-start | bytes 835592 | tf_op jit(solution)/shard_map/ppermute | solution.py:411
  18.9 9.0 %collective-permute-start.6 = (bf16[64,2048]{1,0:T(8,128)(2,1)}, bf16[64,2048]{1,0:T(8,128)(2,1)}, u32[]{:S(2)}, u32[]{:S(2)}) collective-permute-start(bf16[64,2048]{1,0:T(8,128)(2,1)} %collective-permute-done.4.refs_8_), channel_id=1, source_target_pairs={{0,1},{1,0},{2,3},{3,2},{4,5},{5,4},{6,7},{7,6},{8,9},{9,8},{10,11... | collective-permute-start | bytes 786440 | tf_op jit(solution)/shard_map/ppermute | solution.py:411
  19.4 0.7 %copy-start.2 = (bf16[64,2048]{1,0:T(8,128)(2,1)}, bf16[64,2048]{1,0:T(8,128)(2,1)S(1)}, u32[]{:S(2)}) copy-start(bf16[64,2048]{1,0:T(8,128)(2,1)S(1)} %collective-permute-done.2.refs_6_) | copy-start | bytes 786436
  20.1 7.8 %collective-permute-start.7 = (bf16[64,2176]{1,0:T(8,128)(2,1)S(1)}, bf16[64,2176]{1,0:T(8,128)(2,1)}, u32[]{:S(2)}, u32[]{:S(2)}) collective-permute-start(bf16[64,2176]{1,0:T(8,128)(2,1)S(1)} %collective-permute-done.5.refs_9_), channel_id=1, source_target_pairs={{0,1},{1,0},{2,3},{3,2},{4,5},{5,4},{6,7},{7,6},{8,9},{9,8},{10,11... | collective-permute-start | bytes 835592 | tf_op jit(solution)/shard_map/ppermute | solution.py:411
  25.5 7.6 %collective-permute-start.10 = (bf16[64,2048]{1,0:T(8,128)(2,1)}, bf16[64,2048]{1,0:T(8,128)(2,1)}, u32[]{:S(2)}, u32[]{:S(2)}) collective-permute-start(bf16[64,2048]{1,0:T(8,128)(2,1)} %collective-permute-done.8.refs_12_.refs_2_), channel_id=1, source_target_pairs={{0,1},{1,0},{2,3},{3,2},{4,5},{5,4},{6,7},{7,6},{8,9},{9,8},{10,11... | collective-permute-start | bytes 786440 | tf_op jit(solution)/shard_map/ppermute | solution.py:411
  25.5 10.1 %collective-permute-start.11 = (bf16[64,2176]{1,0:T(8,128)(2,1)}, bf16[64,2176]{1,0:T(8,128)(2,1)}, u32[]{:S(2)}, u32[]{:S(2)}) collective-permute-start(bf16[64,2176]{1,0:T(8,128)(2,1)} %collective-permute-done.9.refs_13_.refs_2_), channel_id=1, source_target_pairs={{0,1},{1,0},{2,3},{3,2},{4,5},{5,4},{6,7},{7,6},{8,9},{9,8},{10,11... | collective-permute-start | bytes 835592 | tf_op jit(solution)/shard_map/ppermute | solution.py:411
  27.9 1.0 %copy-start.1 = (bf16[64,2048]{1,0:T(8,128)(2,1)S(1)}, bf16[64,2048]{1,0:T(8,128)(2,1)}, u32[]{:S(2)}) copy-start(bf16[64,2048]{1,0:T(8,128)(2,1)} %copy-done) | copy-start | bytes 786436
  28.9 0.9 %copy-start.3 = (bf16[64,2048]{1,0:T(8,128)(2,1)S(1)}, bf16[64,2048]{1,0:T(8,128)(2,1)}, u32[]{:S(2)}) copy-start(bf16[64,2048]{1,0:T(8,128)(2,1)} %copy-done.2) | copy-start | bytes 786436
  30.1 8.6 %collective-permute-start.12 = (s16[528,128]{1,0:T(8,128)(2,1)S(1)}, s16[528,128]{1,0:T(8,128)(2,1)S(1)}, u32[]{:S(2)}, u32[]{:S(2)}) collective-permute-start(s16[528,128]{1,0:T(8,128)(2,1)S(1)} %shard_map.55), channel_id=1, source_target_pairs={{0,2},{2,0},{1,3},{3,1},{4,6},{6,4},{5,7},{7,5},{8,10},{10,8},{9,1... | collective-permute-start | bytes 405512 | tf_op jit(solution)/shard_map/ppermute | solution.py:445
  35.3 5.2 %collective-permute-start.13 = (s16[272,128]{1,0:T(8,128)(2,1)S(1)}, s16[272,128]{1,0:T(8,128)(2,1)S(1)}, u32[]{:S(2)}, u32[]{:S(2)}) collective-permute-start(s16[272,128]{1,0:T(8,128)(2,1)S(1)} %shard_map.58), channel_id=1, source_target_pairs={{0,2},{2,0},{1,3},{3,1},{4,6},{6,4},{5,7},{7,5},{8,10},{10,8},{9,1... | collective-permute-start | bytes 208904 | tf_op jit(solution)/shard_map/ppermute | solution.py:477
  37.8 4.4 %collective-permute-start.14 = (s16[272,128]{1,0:T(8,128)(2,1)S(1)}, s16[272,128]{1,0:T(8,128)(2,1)S(1)}, u32[]{:S(2)}, u32[]{:S(2)}) collective-permute-start(s16[272,128]{1,0:T(8,128)(2,1)S(1)} %shard_map.59), channel_id=1, source_target_pairs={{0,2},{2,0},{1,3},{3,1},{4,6},{6,4},{5,7},{7,5},{8,10},{10,8},{9,1... | collective-permute-start | bytes 208904 | tf_op jit(solution)/shard_map/ppermute | solution.py:477

commit v7 on v6

--- a/solution.py
+++ b/solution.py
@@ -215,21 +215,17 @@
     out[pl.ds(len(tiles) * qblk, TAIL), :] = tail.astype(jnp.int16)
 
 
-def packed_pieces(part_refs, nb):
+def packed_pieces(part_refs, nb, b):
     chunks, width = len(part_refs), part_refs[0].shape[1]
-    groups = nb // chunks
+    groups, k = nb // chunks, b // chunks
     qblk = (part_refs[0].shape[0] - TAIL) // groups
     tails = [ref[pl.ds(groups * qblk, TAIL), :].astype(jnp.int32).astype(jnp.float32) for ref in part_refs]
     weight = tails[-1][TAIL - 1 :] * (1.0 / WEIGHT_STEPS)
-    found = []
-    for b in range(nb):
-        k = b // chunks
-        tiles = []
-        for ref, tail in zip(part_refs, tails):
-            steps = ref[pl.ds(k * qblk, qblk), :].astype(jnp.int32).astype(jnp.float32)
-            tiles.append(steps * (jnp.exp2(tail[k : k + 1]) * (1.0 / STEPS)))
-        found.append(regroup(tiles, b % chunks, width // chunks) * weight)
-    return found
+    tiles = []
+    for ref, tail in zip(part_refs, tails):
+        steps = ref[pl.ds(k * qblk, qblk), :].astype(jnp.int32).astype(jnp.float32)
+        tiles.append(steps * (jnp.exp2(tail[k : k + 1]) * (1.0 / STEPS)))
+    return regroup(tiles, b % chunks, width // chunks) * weight
 
 
 def far_kernel(sizes, dists, chunks, packed, *refs):
@@ -371,12 +367,11 @@
     block = pick_ranked(owned, z, per - 1)
     stores = []
     chunks = len(came) // (ckpts - 1)
-    parts = [packed_pieces(came[r * chunks : (r + 1) * chunks], nb) for r in range(ckpts - 1)]
     for b in range(nb):
         span = pl.ds(b * qblk, qblk)
         total = last_ref[span, :]
-        for part in parts:
-            total = total + part[b]
+        for r in range(ckpts - 1):
+            total = total + packed_pieces(came[r * chunks : (r + 1) * chunks], nb, b)
         tile[span, :] = total
         stores.append(put_columns(tile, out, owned, block, sems.at[b], span))
         stores[-1].start()

time: 43.3 us -> 43.3 us (level)
  no operation moved by 1% of the time
where the time goes in v7:
time: 43.3 us; the launch traced here: 43 us
  waiting for transfers between devices  20.8 us (48%)
  starting transfers between devices  7.83 us (18%)
  Pallas kernels  7.36 us (17%)
  local copies, waits for them, and re-layouts  6.78 us (16%)
    ppermute x6, waiting for transfers between devices, per_device(): held = [lax.ppermute(part, lines, ring) for part in held]  19.1 us
    pallas_call x2, Pallas kernels, per_device(): pl.pallas_call(functools.partial(piece_kernel, sizes, i, seen + 1, chunks...  4.27 us
    unnamed x12, local copies, waits for them, and re-layouts  3.3 us
    ppermute x1, starting transfers between devices, per_device(): lax.ppermute(terms[r - 1], 'ckpt', shift(ckpts, r))  2.95 us
    ppermute x6, starting transfers between devices, per_device(): held = [lax.ppermute(part, lines, ring) for part in held]  2.63 us
    pallas_call x1, Pallas kernels, per_device(): pl.pallas_call(functools.partial(own_kernel, sizes, dists, chunks), out_s...  1.87 us
    slice x1, local copies, waits for them, and re-layouts, per_device(): asked.append(queries[b * qblk:(b + 1) * qblk])  1.68 us
    ppermute x2, waiting for transfers between devices, per_device(): pieces[r, i] = lax.ppermute(done[r - 1], 'ckpt', shift(ckpts, r))  1.62 us
  transfers between devices with their start and end apart: 15, of which 6 were waited for; matrix products, arithmetic and copies ran while one was open for 4% of the time, Pallas kernels for 15%

profile of v7, /device:TPU:0, one launch (start us, length us, event | category | flops | bytes accessed | tf_op | source)
XLA Modules:
  0.0 43.0 jit_solution(11974877274926261202)
XLA Ops:
  0.0 1.1 %slice_bitcast_fusion.2 = (bf16[64,2048]{1,0:T(8,128)(2,1)S(1)}, bf16[64,2048]{1,0:T(8,128)(2,1)S(1)}) fusion(bf16[1,128,2048]{2,1,0:T(8,128)(2,1)} %param.6), kind=kLoop, calls=%fused_computation.3 | loop fusion | bytes 1048576 | tf_op jit(solution)/shard_map/slice | solution.py:395
  1.1 0.7 %pad.1.clone = bf16[2176]{0:T(1024)(128)(2,1)S(1)} pad(bf16[128]{0:T(256)(128)(2,1)} %bitcast.10, bf16[]{:T(256)} %constant.4), padding=2048_0 | pad | bytes 4610 | tf_op jit(solution)/shard_map/concatenate | solution.py:397
  1.8 0.5 %collective-permute-start.1 = (bf16[64,2176]{1,0:T(8,128)(2,1)S(1)}, bf16[64,2176]{1,0:T(8,128)(2,1)S(1)}, u32[]{:S(2)}, u32[]{:S(2)}) collective-permute-start(bf16[64,2176]{1,0:T(8,128)(2,1)S(1)} %pad_maximum_fusion.refs_3_), channel_id=1, source_target_pairs={{1,5},{5,9},{9,13},{13,12},{12,8},{8,4},{4,0},{0,1},{3,7},{7,11},{... | collective-permute-start | bytes 835592 | tf_op jit(solution)/shard_map/ppermute | solution.py:405
  2.3 2.1 %collective-permute-start = (bf16[64,2048]{1,0:T(8,128)(2,1)S(1)}, bf16[64,2048]{1,0:T(8,128)(2,1)S(1)}, u32[]{:S(2)}, u32[]{:S(2)}) collective-permute-start(bf16[64,2048]{1,0:T(8,128)(2,1)S(1)} %get-tuple-element.16.refs_2_), channel_id=1, source_target_pairs={{1,5},{5,9},{9,13},{13,12},{12,8},{8,4},{4,0},{0,1},{3,7},{7,11},{... | collective-permute-start | bytes 786440 | tf_op jit(solution)/shard_map/ppermute | solution.py:405
  4.4 5.0 %collective-permute-done.1.refs_5_ = bf16[64,2176]{1,0:T(8,128)(2,1)S(1)} collective-permute-done((bf16[64,2176]{1,0:T(8,128)(2,1)S(1)}, bf16[64,2176]{1,0:T(8,128)(2,1)S(1)}, u32[]{:S(2)}, u32[]{:S(2)}) %collective-permute-start.1) | collective-permute-done | bytes 278560 | tf_op jit(solution)/shard_map/ppermute | solution.py:405
  9.4 2.8 %collective-permute-done.refs_4_ = bf16[64,2048]{1,0:T(8,128)(2,1)S(1)} collective-permute-done((bf16[64,2048]{1,0:T(8,128)(2,1)S(1)}, bf16[64,2048]{1,0:T(8,128)(2,1)S(1)}, u32[]{:S(2)}, u32[]{:S(2)}) %collective-permute-start) | collective-permute-done | bytes 262176 | tf_op jit(solution)/shard_map/ppermute | solution.py:405
  12.2 3.7 %collective-permute-done.5.refs_9_ = bf16[64,2176]{1,0:T(8,128)(2,1)S(1)} collective-permute-done((bf16[64,2176]{1,0:T(8,128)(2,1)S(1)}, bf16[64,2176]{1,0:T(8,128)(2,1)S(1)}, u32[]{:S(2)}, u32[]{:S(2)}) %collective-permute-start.5) | collective-permute-done | bytes 278560 | tf_op jit(solution)/shard_map/ppermute | solution.py:405
  15.9 0.7 %copy-done = bf16[64,2048]{1,0:T(8,128)(2,1)} copy-done((bf16[64,2048]{1,0:T(8,128)(2,1)}, bf16[64,2048]{1,0:T(8,128)(2,1)S(1)}, u32[]{:S(2)}) %copy-start) | copy-done | bytes 262168
  16.6 2.2 %collective-permute-done.4.refs_8_ = bf16[64,2048]{1,0:T(8,128)(2,1)} collective-permute-done((bf16[64,2048]{1,0:T(8,128)(2,1)S(1)}, bf16[64,2048]{1,0:T(8,128)(2,1)}, u32[]{:S(2)}, u32[]{:S(2)}) %collective-permute-start.4) | collective-permute-done | bytes 262176 | tf_op jit(solution)/shard_map/ppermute | solution.py:405
  18.9 0.5 %collective-permute-start.6 = (bf16[64,2048]{1,0:T(8,128)(2,1)}, bf16[64,2048]{1,0:T(8,128)(2,1)}, u32[]{:S(2)}, u32[]{:S(2)}) collective-permute-start(bf16[64,2048]{1,0:T(8,128)(2,1)} %collective-permute-done.4.refs_8_), channel_id=1, source_target_pairs={{0,1},{1,0},{2,3},{3,2},{4,5},{5,4},{6,7},{7,6},{8,9},{9,8},{10,11... | collective-permute-start | bytes 786440 | tf_op jit(solution)/shard_map/ppermute | solution.py:406
  19.4 0.7 %copy-done.2 = bf16[64,2048]{1,0:T(8,128)(2,1)} copy-done((bf16[64,2048]{1,0:T(8,128)(2,1)}, bf16[64,2048]{1,0:T(8,128)(2,1)S(1)}, u32[]{:S(2)}) %copy-start.2) | copy-done | bytes 262168
  20.1 5.4 %collective-permute-done.8.refs_12_.refs_2_ = bf16[64,2048]{1,0:T(8,128)(2,1)} collective-permute-done((bf16[64,2048]{1,0:T(8,128)(2,1)}, bf16[64,2048]{1,0:T(8,128)(2,1)}, u32[]{:S(2)}, u32[]{:S(2)}) %collective-permute-start.8) | collective-permute-done | bytes 262176 | tf_op jit(solution)/shard_map/ppermute | solution.py:405
  25.5 0.5 %collective-permute-start.11 = (bf16[64,2176]{1,0:T(8,128)(2,1)}, bf16[64,2176]{1,0:T(8,128)(2,1)}, u32[]{:S(2)}, u32[]{:S(2)}) collective-permute-start(bf16[64,2176]{1,0:T(8,128)(2,1)} %collective-permute-done.9.refs_13_.refs_2_), channel_id=1, source_target_pairs={{0,1},{1,0},{2,3},{3,2},{4,5},{5,4},{6,7},{7,6},{8,9},{9,8},{10,11... | collective-permute-start | bytes 835592 | tf_op jit(solution)/shard_map/ppermute | solution.py:406
  26.1 1.7 %slice_bitcast_fusion = (bf16[256,2048]{1,0:T(8,128)(2,1)S(1)}, bf16[256,2048]{1,0:T(8,128)(2,1)S(1)}) fusion(bf16[1,512,2048]{2,1,0:T(8,128)(2,1)} %param.5), kind=kLoop, calls=%fused_computation | loop fusion | bytes 4194304 | tf_op jit(solution)/shard_map/slice | solution.py:402
  27.9 0.9 %copy-done.1 = bf16[64,2048]{1,0:T(8,128)(2,1)S(1)} copy-done((bf16[64,2048]{1,0:T(8,128)(2,1)S(1)}, bf16[64,2048]{1,0:T(8,128)(2,1)}, u32[]{:S(2)}) %copy-start.1) | copy-done | bytes 262168
  28.9 0.9 %copy-done.3 = bf16[64,2048]{1,0:T(8,128)(2,1)S(1)} copy-done((bf16[64,2048]{1,0:T(8,128)(2,1)S(1)}, bf16[64,2048]{1,0:T(8,128)(2,1)}, u32[]{:S(2)}) %copy-start.3) | copy-done | bytes 262168
  30.1 2.9 %collective-permute-start.12 = (s16[528,128]{1,0:T(8,128)(2,1)S(1)}, s16[528,128]{1,0:T(8,128)(2,1)S(1)}, u32[]{:S(2)}, u32[]{:S(2)}) collective-permute-start(s16[528,128]{1,0:T(8,128)(2,1)S(1)} %shard_map.55), channel_id=1, source_target_pairs={{0,2},{2,0},{1,3},{3,1},{4,6},{6,4},{5,7},{7,5},{8,10},{10,8},{9,1... | collective-permute-start | bytes 405512 | tf_op jit(solution)/shard_map/ppermute | solution.py:440
  33.2 2.1 %shard_map.58 = s16[272,128]{1,0:T(8,128)(2,1)S(1)} custom-call(s32[1,8]{1,0:T(1,128)S(1)} %pad_add_fusion.packed, bf16[256,2048]{1,0:T(8,128)(2,1)S(1)} %get-tuple-element.14.refs_0_, bf16[256,2048]{1,0:T(8,128)(2,1)S(1)} %get-tuple-element.13.refs_1_, bf16[64,2048]{1,0:T(8,128)(2,1)} %collective-permute-done.8.refs_12_.refs_2_, ...), custom_call_target="tpu_custom_call" | custom-call | flops 268435456 | bytes 2097152 | tf_op jit(solution)/shard_map/pallas_call | solution.py:462
  35.3 0.3 collective-permute-start.13
  35.6 2.1 %shard_map.59 = s16[272,128]{1,0:T(8,128)(2,1)S(1)} custom-call(s32[1,8]{1,0:T(1,128)S(1)} %pad_add_fusion.packed, bf16[256,2048]{1,0:T(8,128)(2,1)S(1)} %get-tuple-element.14.refs_0_, bf16[256,2048]{1,0:T(8,128)(2,1)S(1)} %get-tuple-element.13.refs_1_, bf16[64,2176]{1,0:T(8,128)(2,1)} %collective-permute-done.9.refs_13_.refs_2_, ...), custom_call_target="tpu_custom_call" | custom-call | flops 268435456 | bytes 2097152 | tf_op jit(solution)/shard_map/pallas_call | solution.py:462
  37.8 0.9 %collective-permute-start.14 = (s16[272,128]{1,0:T(8,128)(2,1)S(1)}, s16[272,128]{1,0:T(8,128)(2,1)S(1)}, u32[]{:S(2)}, u32[]{:S(2)}) collective-permute-start(s16[272,128]{1,0:T(8,128)(2,1)S(1)} %shard_map.59), channel_id=1, source_target_pairs={{0,2},{2,0},{1,3},{3,1},{4,6},{6,4},{5,7},{7,5},{8,10},{10,8},{9,1... | collective-permute-start | bytes 208904 | tf_op jit(solution)/shard_map/ppermute | solution.py:472
  38.6 1.9 %shard_map.56 = (f32[512,256]{1,0:T(8,128)}, f32[512,128]{1,0:T(8,128)S(1)}) custom-call(s32[1,8]{1,0:T(1,128)S(1)} %pad_add_fusion.packed, bf16[256,2048]{1,0:T(8,128)(2,1)S(1)} %get-tuple-element.14.refs_0_, bf16[256,2048]{1,0:T(8,128)(2,1)S(1)} %get-tuple-element.13.refs_1_, bf16[64,2048]{1,0:T(8,128)(2,1)S(1)} %get-tuple-element.16.refs_2_, ...), custom_call_target="tpu_custom_call" | custom-call | flops 536870912 | bytes 2097152 | tf_op jit(solution)/shard_map/pallas_call | solution.py:477
  40.5 1.6 %collective-permute-done.14.refs_1_ = s16[272,128]{1,0:T(8,128)(2,1)S(1)} collective-permute-done((s16[272,128]{1,0:T(8,128)(2,1)S(1)}, s16[272,128]{1,0:T(8,128)(2,1)S(1)}, u32[]{:S(2)}, u32[]{:S(2)}) %collective-permute-start.14) | collective-permute-done | bytes 69664 | tf_op jit(solution)/shard_map/ppermute | solution.py:472
  42.1 0.8 %shard_map.60 = f32[512,256]{1,0:T(8,128)} custom-call(s32[1,8]{1,0:T(1,128)S(1)} %pad_add_fusion.packed, f32[512,256]{1,0:T(8,128)} %get-tuple-element.9.acc_ref, f32[512,128]{1,0:T(8,128)S(1)} %get-tuple-element.10.last_ref, s16[272,128]{1,0:T(8,128)(2,1)S(1)} %collective-permute-done.13.refs_0_, ...), custom_call_target="tpu_custom_call", output_to_operand_aliasing={{}: (1, {})} | custom-call | tf_op jit(solution)/shard_map/pallas_call | solution.py:491
  (30 shorter events, 0.7 us)
Async XLA Ops:
  1.8 7.6 %collective-permute-start.1 = (bf16[64,2176]{1,0:T(8,128)(2,1)S(1)}, bf16[64,2176]{1,0:T(8,128)(2,1)S(1)}, u32[]{:S(2)}, u32[]{:S(2)}) collective-permute-start(bf16[64,2176]{1,0:T(8,128)(2,1)S(1)} %pad_maximum_fusion.refs_3_), channel_id=1, source_target_pairs={{1,5},{5,9},{9,13},{13,12},{12,8},{8,4},{4,0},{0,1},{3,7},{7,11},{... | collective-permute-start | bytes 835592 | tf_op jit(solution)/shard_map/ppermute | solution.py:405
  2.3 25.4 %copy-start.4 = (s32[2,2]{1,0:T(2,128)S(1)}, s32[2,2]{1,0:T(2,128)}, u32[]{:S(2)}) copy-start(s32[2,2]{1,0:T(2,128)} %param.8) | copy-start | bytes 52
  2.3 25.5 %copy-start.5 = (s32[4]{0:T(128)S(1)}, s32[4]{0:T(128)}, u32[]{:S(2)}) copy-start(s32[4]{0:T(128)} %param.9) | copy-start | bytes 52
  2.3 9.9 %collective-permute-start = (bf16[64,2048]{1,0:T(8,128)(2,1)S(1)}, bf16[64,2048]{1,0:T(8,128)(2,1)S(1)}, u32[]{:S(2)}, u32[]{:S(2)}) collective-permute-start(bf16[64,2048]{1,0:T(8,128)(2,1)S(1)} %get-tuple-element.16.refs_2_), channel_id=1, source_target_pairs={{1,5},{5,9},{9,13},{13,12},{12,8},{8,4},{4,0},{0,1},{3,7},{7,11},{... | collective-permute-start | bytes 786440 | tf_op jit(solution)/shard_map/ppermute | solution.py:405
  9.4 6.5 %collective-permute-start.5 = (bf16[64,2176]{1,0:T(8,128)(2,1)S(1)}, bf16[64,2176]{1,0:T(8,128)(2,1)S(1)}, u32[]{:S(2)}, u32[]{:S(2)}) collective-permute-start(bf16[64,2176]{1,0:T(8,128)(2,1)S(1)} %collective-permute-done.1.refs_5_), channel_id=1, source_target_pairs={{1,5},{5,9},{9,13},{13,12},{12,8},{8,4},{4,0},{0,1},{3,7},{7,11},{... | collective-permute-start | bytes 835592 | tf_op jit(solution)/shard_map/ppermute | solution.py:405
  12.2 6.7 %collective-permute-start.4 = (bf16[64,2048]{1,0:T(8,128)(2,1)S(1)}, bf16[64,2048]{1,0:T(8,128)(2,1)}, u32[]{:S(2)}, u32[]{:S(2)}) collective-permute-start(bf16[64,2048]{1,0:T(8,128)(2,1)S(1)} %collective-permute-done.refs_4_), channel_id=1, source_target_pairs={{1,5},{5,9},{9,13},{13,12},{12,8},{8,4},{4,0},{0,1},{3,7},{7,11},{... | collective-permute-start | bytes 786440 | tf_op jit(solution)/shard_map/ppermute | solution.py:405
  15.9 9.6 %collective-permute-start.9 = (bf16[64,2176]{1,0:T(8,128)(2,1)S(1)}, bf16[64,2176]{1,0:T(8,128)(2,1)}, u32[]{:S(2)}, u32[]{:S(2)}) collective-permute-start(bf16[64,2176]{1,0:T(8,128)(2,1)S(1)} %collective-permute-done.5.refs_9_), channel_id=1, source_target_pairs={{1,5},{5,9},{9,13},{13,12},{12,8},{8,4},{4,0},{0,1},{3,7},{7,11},{... | collective-permute-start | bytes 835592 | tf_op jit(solution)/shard_map/ppermute | solution.py:405
  15.9 3.4 %collective-permute-start.2 = (bf16[64,2048]{1,0:T(8,128)(2,1)S(1)}, bf16[64,2048]{1,0:T(8,128)(2,1)S(1)}, u32[]{:S(2)}, u32[]{:S(2)}) collective-permute-start(bf16[64,2048]{1,0:T(8,128)(2,1)S(1)} %collective-permute-done.refs_4_), channel_id=1, source_target_pairs={{0,1},{1,0},{2,3},{3,2},{4,5},{5,4},{6,7},{7,6},{8,9},{9,8},{10,11... | collective-permute-start | bytes 786440 | tf_op jit(solution)/shard_map/ppermute | solution.py:406
  15.9 0.7 %copy-start = (bf16[64,2048]{1,0:T(8,128)(2,1)}, bf16[64,2048]{1,0:T(8,128)(2,1)S(1)}, u32[]{:S(2)}) copy-start(bf16[64,2048]{1,0:T(8,128)(2,1)S(1)} %collective-permute-done.refs_4_) | copy-start | bytes 786436
  18.8 6.7 %collective-permute-start.8 = (bf16[64,2048]{1,0:T(8,128)(2,1)}, bf16[64,2048]{1,0:T(8,128)(2,1)}, u32[]{:S(2)}, u32[]{:S(2)}) collective-permute-start(bf16[64,2048]{1,0:T(8,128)(2,1)} %collective-permute-done.4.refs_8_), channel_id=1, source_target_pairs={{1,5},{5,9},{9,13},{13,12},{12,8},{8,4},{4,0},{0,1},{3,7},{7,11},{... | collective-permute-start | bytes 786440 | tf_op jit(solution)/shard_map/ppermute | solution.py:405
  18.9 9.1 %collective-permute-start.3 = (bf16[64,2176]{1,0:T(8,128)(2,1)S(1)}, bf16[64,2176]{1,0:T(8,128)(2,1)S(1)}, u32[]{:S(2)}, u32[]{:S(2)}) collective-permute-start(bf16[64,2176]{1,0:T(8,128)(2,1)S(1)} %collective-permute-done.1.refs_5_), channel_id=1, source_target_pairs={{0,1},{1,0},{2,3},{3,2},{4,5},{5,4},{6,7},{7,6},{8,9},{9,8},{10,11... | collective-permute-start | bytes 835592 | tf_op jit(solution)/shard_map/ppermute | solution.py:406
  18.9 9.0 %collective-permute-start.6 = (bf16[64,2048]{1,0:T(8,128)(2,1)}, bf16[64,2048]{1,0:T(8,128)(2,1)}, u32[]{:S(2)}, u32[]{:S(2)}) collective-permute-start(bf16[64,2048]{1,0:T(8,128)(2,1)} %collective-permute-done.4.refs_8_), channel_id=1, source_target_pairs={{0,1},{1,0},{2,3},{3,2},{4,5},{5,4},{6,7},{7,6},{8,9},{9,8},{10,11... | collective-permute-start | bytes 786440 | tf_op jit(solution)/shard_map/ppermute | solution.py:406
  19.4 0.7 %copy-start.2 = (bf16[64,2048]{1,0:T(8,128)(2,1)}, bf16[64,2048]{1,0:T(8,128)(2,1)S(1)}, u32[]{:S(2)}) copy-start(bf16[64,2048]{1,0:T(8,128)(2,1)S(1)} %collective-permute-done.2.refs_6_) | copy-start | bytes 786436
  20.1 7.8 %collective-permute-start.7 = (bf16[64,2176]{1,0:T(8,128)(2,1)S(1)}, bf16[64,2176]{1,0:T(8,128)(2,1)}, u32[]{:S(2)}, u32[]{:S(2)}) collective-permute-start(bf16[64,2176]{1,0:T(8,128)(2,1)S(1)} %collective-permute-done.5.refs_9_), channel_id=1, source_target_pairs={{0,1},{1,0},{2,3},{3,2},{4,5},{5,4},{6,7},{7,6},{8,9},{9,8},{10,11... | collective-permute-start | bytes 835592 | tf_op jit(solution)/shard_map/ppermute | solution.py:406
  25.5 7.6 %collective-permute-start.10 = (bf16[64,2048]{1,0:T(8,128)(2,1)}, bf16[64,2048]{1,0:T(8,128)(2,1)}, u32[]{:S(2)}, u32[]{:S(2)}) collective-permute-start(bf16[64,2048]{1,0:T(8,128)(2,1)} %collective-permute-done.8.refs_12_.refs_2_), channel_id=1, source_target_pairs={{0,1},{1,0},{2,3},{3,2},{4,5},{5,4},{6,7},{7,6},{8,9},{9,8},{10,11... | collective-permute-start | bytes 786440 | tf_op jit(solution)/shard_map/ppermute | solution.py:406
  25.5 10.1 %collective-permute-start.11 = (bf16[64,2176]{1,0:T(8,128)(2,1)}, bf16[64,2176]{1,0:T(8,128)(2,1)}, u32[]{:S(2)}, u32[]{:S(2)}) collective-permute-start(bf16[64,2176]{1,0:T(8,128)(2,1)} %collective-permute-done.9.refs_13_.refs_2_), channel_id=1, source_target_pairs={{0,1},{1,0},{2,3},{3,2},{4,5},{5,4},{6,7},{7,6},{8,9},{9,8},{10,11... | collective-permute-start | bytes 835592 | tf_op jit(solution)/shard_map/ppermute | solution.py:406
  27.9 1.0 %copy-start.1 = (bf16[64,2048]{1,0:T(8,128)(2,1)S(1)}, bf16[64,2048]{1,0:T(8,128)(2,1)}, u32[]{:S(2)}) copy-start(bf16[64,2048]{1,0:T(8,128)(2,1)} %copy-done) | copy-start | bytes 786436
  28.9 0.9 %copy-start.3 = (bf16[64,2048]{1,0:T(8,128)(2,1)S(1)}, bf16[64,2048]{1,0:T(8,128)(2,1)}, u32[]{:S(2)}) copy-start(bf16[64,2048]{1,0:T(8,128)(2,1)} %copy-done.2) | copy-start | bytes 786436
  30.1 8.6 %collective-permute-start.12 = (s16[528,128]{1,0:T(8,128)(2,1)S(1)}, s16[528,128]{1,0:T(8,128)(2,1)S(1)}, u32[]{:S(2)}, u32[]{:S(2)}) collective-permute-start(s16[528,128]{1,0:T(8,128)(2,1)S(1)} %shard_map.55), channel_id=1, source_target_pairs={{0,2},{2,0},{1,3},{3,1},{4,6},{6,4},{5,7},{7,5},{8,10},{10,8},{9,1... | collective-permute-start | bytes 405512 | tf_op jit(solution)/shard_map/ppermute | solution.py:440
  35.3 5.2 %collective-permute-start.13 = (s16[272,128]{1,0:T(8,128)(2,1)S(1)}, s16[272,128]{1,0:T(8,128)(2,1)S(1)}, u32[]{:S(2)}, u32[]{:S(2)}) collective-permute-start(s16[272,128]{1,0:T(8,128)(2,1)S(1)} %shard_map.58), channel_id=1, source_target_pairs={{0,2},{2,0},{1,3},{3,1},{4,6},{6,4},{5,7},{7,5},{8,10},{10,8},{9,1... | collective-permute-start | bytes 208904 | tf_op jit(solution)/shard_map/ppermute | solution.py:472
  37.8 4.4 %collective-permute-start.14 = (s16[272,128]{1,0:T(8,128)(2,1)S(1)}, s16[272,128]{1,0:T(8,128)(2,1)S(1)}, u32[]{:S(2)}, u32[]{:S(2)}) collective-permute-start(s16[272,128]{1,0:T(8,128)(2,1)S(1)} %shard_map.59), channel_id=1, source_target_pairs={{0,2},{2,0},{1,3},{3,1},{4,6},{6,4},{5,7},{7,5},{8,10},{10,8},{9,1... | collective-permute-start | bytes 208904 | tf_op jit(solution)/shard_map/ppermute | solution.py:472
